TPU v7x, 512 devices: a whole 4x4x16 slice. The times are simulated.
512 devices in a mesh: ep: 64 (over z, y), dp: 8 (over x, core).
Axes of the slice: x: 4, y: 4, z: 16, core: 2. Of those that a mesh axis runs over, the one named last changes fastest.
Arguments:
- tokens: bfloat16 [12288, 3584], P(('ep', 'dp')), may hold values from -6 to 6
- grad_out: bfloat16 [12288, 3584], P(('ep', 'dp')), may hold values from -0.29882812 to 0.29882812
- routes: int32 [12288, 2], P(('ep', 'dp')), may hold values from 0 to 7, all different within a row; in each aligned block of 24 rows (0 to 23, 24 to 47, ...) at most 8 rows name the same one
- route_probs: float32 [12288, 2], P(('ep', 'dp')), may hold values from 0.1 to 1
- gate_weight: bfloat16 [64, 3584, 128], P('ep', 'dp'), may hold values from -0.09375 to 0.09375
- up_weight: bfloat16 [64, 3584, 128], P('ep', 'dp'), may hold values from -0.09375 to 0.09375
- down_weight: bfloat16 [64, 3584, 128], P('ep', 'dp'), may hold values from -0.1875 to 0.1875
Outputs:
- grad_tokens: bfloat16 [12288, 3584], P(('ep', 'dp'))
- grad_probs: float32 [12288, 2], P(('ep', 'dp'))
- grad_gate: bfloat16 [64, 3584, 128], P('ep', 'dp')
- grad_up: bfloat16 [64, 3584, 128], P('ep', 'dp')
- grad_down: bfloat16 [64, 3584, 128], P('ep', 'dp')
Inputs may be any that keep to these rules, and one draw needn't show every extreme that they name: `routes`: each row names 2 different experts. Within each aligned block of 24 rows (the tokens of one device) no expert is named by more than 8 rows; in some blocks one expert is named by exactly 8 rows.
All inputs are finite; a program needn't handle non-finite values.
Results may differ from a plain program's by a relative error of at most 0.017.
Values may be sent and summed in bfloat16 or wider, within the bound.
No kernel may reach another device: no remote copies, remote signals or barrier semaphores. Data moves between devices by JAX's collectives and lax.ppermute only.
A program may use at most 64 MiB of HBM per device.

v0:
```python
import jax
import jax.numpy as jnp
from jax import lax
from jax.sharding import PartitionSpec as P

GROUP = 8
TOP = 2


CONTRACT_HIDDEN = (((1,), (1,)), ((), ()))
CONTRACT_ROWS = (((0,), (0,)), ((), ()))


def slot_layout(routes, experts, capacity):
    flat_routes = routes.reshape(-1)
    copies = flat_routes.shape[0]
    onehot = (flat_routes[:, None] == jnp.arange(experts, dtype=jnp.int32)[None, :]).astype(
        jnp.int32
    )
    earlier = jnp.cumsum(onehot, axis=0) - onehot
    slot_rank = jnp.sum(earlier * onehot, axis=1)
    slot_index = flat_routes * capacity + slot_rank
    slot_copy = jnp.full((experts * capacity,), copies, jnp.int32)
    slot_copy = slot_copy.at[slot_index].set(jnp.arange(copies, dtype=jnp.int32))
    return (slot_index, slot_copy)


def per_device(tokens, grad_out, routes, route_probs, gate_weight, up_weight, down_weight):
    tok_count, features = tokens.shape
    ep_size = lax.axis_size("ep")
    experts = ep_size // GROUP
    slots = min(
        tok_count // GROUP,
        max(1, (4 * TOP * tok_count + 3 * experts * GROUP - 1) // (3 * experts * GROUP)),
    )
    capacity = GROUP * slots
    copies = tok_count * TOP
    slot_index, slot_copy = slot_layout(routes, experts, capacity)
    source_row = jnp.where(slot_copy < copies, slot_copy // TOP, tok_count)
    blank = jnp.zeros((1, features), jnp.bfloat16)
    send_tokens = jnp.concatenate([tokens, blank], axis=0)[source_row]
    send_grads = jnp.concatenate([grad_out, blank], axis=0)[source_row]
    flat_probs = jnp.concatenate([route_probs.reshape(-1), jnp.zeros((1,), jnp.float32)])
    send_probs = flat_probs[slot_copy]
    spread_tokens = jnp.broadcast_to(
        send_tokens.reshape(experts, 1, capacity, features), (experts, GROUP, capacity, features)
    ).reshape(ep_size, capacity, features)
    spread_grads = jnp.broadcast_to(
        send_grads.reshape(experts, 1, capacity, features), (experts, GROUP, capacity, features)
    ).reshape(ep_size, capacity, features)
    spread_probs = jnp.broadcast_to(
        send_probs.reshape(experts, 1, capacity), (experts, GROUP, capacity)
    ).reshape(ep_size, capacity)
    rows_tok, rows_grd, rows_prb = (
        lax.all_to_all(spread_tokens, "ep", split_axis=0, concat_axis=0, tiled=True),
        lax.all_to_all(spread_grads, "ep", split_axis=0, concat_axis=0, tiled=True),
        lax.all_to_all(
            spread_probs.astype(jnp.bfloat16), "ep", split_axis=0, concat_axis=0, tiled=True
        ).astype(spread_probs.dtype),
    )
    rows_in = rows_tok.reshape(-1, features)
    rows_grad = rows_grd.reshape(-1, features)
    rows_prob = rows_prb.reshape(-1)
    gate_all, up_all, down_all = (
        lax.all_gather(gate_weight, "dp", axis=1, tiled=True),
        lax.all_gather(up_weight, "dp", axis=1, tiled=True),
        lax.all_gather(down_weight, "dp", axis=1, tiled=True),
    )
    gate_full = gate_all[0]
    up_full = up_all[0]
    down_full = down_all[0]
    gate_pre = jnp.dot(rows_in, gate_full, preferred_element_type=jnp.float32)
    up_pre = jnp.dot(rows_in, up_full, preferred_element_type=jnp.float32)
    sigmoid_gate = jax.nn.sigmoid(gate_pre)
    activated = gate_pre * sigmoid_gate
    hidden = (activated * up_pre).astype(jnp.bfloat16)
    scaled = (rows_prob[:, None] * rows_grad.astype(jnp.float32)).astype(jnp.bfloat16)
    down_grad = jnp.dot(rows_grad, down_full, preferred_element_type=jnp.float32)
    scores = jnp.sum(hidden.astype(jnp.float32) * down_grad, axis=1)
    hidden_grad = rows_prob[:, None] * down_grad
    gate_grad = (
        hidden_grad * up_pre * sigmoid_gate * (1.0 + gate_pre * (1.0 - sigmoid_gate))
    ).astype(jnp.bfloat16)
    up_grad = (hidden_grad * activated).astype(jnp.bfloat16)
    token_part = (
        lax.dot_general(gate_grad, gate_full, CONTRACT_HIDDEN, preferred_element_type=jnp.float32)
        + lax.dot_general(up_grad, up_full, CONTRACT_HIDDEN, preferred_element_type=jnp.float32)
    ).astype(jnp.bfloat16)
    returned, returned_scores = (
        lax.all_to_all(
            token_part.reshape(ep_size, capacity, features),
            "ep",
            split_axis=0,
            concat_axis=0,
            tiled=True,
        ),
        lax.all_to_all(
            scores.reshape(ep_size, capacity).astype(jnp.bfloat16),
            "ep",
            split_axis=0,
            concat_axis=0,
            tiled=True,
        ).astype(jnp.float32),
    )
    slot_rows = jnp.sum(
        returned.reshape(experts, GROUP, capacity, features), axis=1, dtype=jnp.float32
    ).reshape(experts * capacity, features)
    slot_scores = jnp.sum(returned_scores.reshape(experts, GROUP, capacity), axis=1).reshape(-1)
    gate_term = lax.dot_general(
        rows_in, gate_grad, CONTRACT_ROWS, preferred_element_type=jnp.float32
    )
    up_term = lax.dot_general(rows_in, up_grad, CONTRACT_ROWS, preferred_element_type=jnp.float32)
    down_term = lax.dot_general(scaled, hidden, CONTRACT_ROWS, preferred_element_type=jnp.float32)
    gate_sum, up_sum, down_sum = (
        lax.psum_scatter(
            gate_term.astype(jnp.bfloat16), "dp", scatter_dimension=0, tiled=True
        ).astype(jnp.float32),
        lax.psum_scatter(
            up_term.astype(jnp.bfloat16), "dp", scatter_dimension=0, tiled=True
        ).astype(jnp.float32),
        lax.psum_scatter(
            down_term.astype(jnp.bfloat16), "dp", scatter_dimension=0, tiled=True
        ).astype(jnp.float32),
    )
    grad_tokens = jnp.sum(slot_rows[slot_index].reshape(tok_count, TOP, features), axis=1).astype(
        jnp.bfloat16
    )
    grad_probs = slot_scores[slot_index].reshape(tok_count, TOP)
    grad_gate = gate_sum.astype(jnp.bfloat16)[None]
    grad_up = up_sum.astype(jnp.bfloat16)[None]
    grad_down = down_sum.astype(jnp.bfloat16)[None]
    return (grad_tokens, grad_probs, grad_gate, grad_up, grad_down)


def solution(mesh):
    placed = (
        P(("ep", "dp"), None),
        P(("ep", "dp"), None),
        P(("ep", "dp"), None),
        P(("ep", "dp"), None),
        P("ep", "dp", None),
        P("ep", "dp", None),
        P("ep", "dp", None),
    )
    return jax.shard_map(
        per_device,
        mesh=mesh,
        in_specs=placed,
        out_specs=(
            P(("ep", "dp"), None),
            P(("ep", "dp"), None),
            P("ep", "dp", None),
            P("ep", "dp", None),
            P("ep", "dp", None),
        ),
        check_vma=False,
    )
```

profile of v0, /device:TPU:4, one launch (start us, length us, event | category | flops | bytes accessed | tf_op | source)
XLA Modules:
  0.0 604.3 jit_solution(18068888513377550808)
XLA Ops:
  12.8 18.7 %all-to-all-start = ((bf16[64,1,8]{2,1,0:T(2,128)(2,1)}), bf16[64,1,8]{2,1,0:T(2,128)(2,1)S(1)}, u32[]{:S(2)}, u32[]{:S(2)}) async-start(bf16[64,1,8]{2,1,0:T(2,128)(2,1)} %copy.29), calls=%async_computation | async-start | bytes 65536 | tf_op jit(solution)/shard_map/all_to_all | solution.py:57
  33.3 12.8 %all-to-all-done = bf16[64,1,8]{2,1,0:T(2,128)(2,1)S(1)} async-done(((bf16[64,1,8]{2,1,0:T(2,128)(2,1)}), bf16[64,1,8]{2,1,0:T(2,128)(2,1)S(1)}, u32[]{:S(2)}, u32[]{:S(2)}) %all-to-all-start) | async-done | bytes 1056 | tf_op jit(solution)/shard_map/all_to_all | solution.py:57
  46.1 2.1 broadcast_in_dim.51
  48.2 5.7 all-to-all-start.2
  54.8 165.5 %all-to-all-done.2 = bf16[64,8,3584]{2,1,0:T(8,128)(2,1)} async-done(((bf16[64,8,3584]{2,1,0:T(8,128)(2,1)}), bf16[64,8,3584]{2,1,0:T(8,128)(2,1)}, u32[]{:S(2)}, u32[]{:S(2)}) %all-to-all-start.2) | async-done | bytes 3670048 | tf_op jit(solution)/shard_map/all_to_all | solution.py:55
  220.3 2.1 broadcast_in_dim.49
  222.4 6.2 %all-to-all-start.1 = ((bf16[64,8,3584]{2,1,0:T(8,128)(2,1)}), bf16[64,8,3584]{2,1,0:T(8,128)(2,1)}, u32[]{:S(2)}, u32[]{:S(2)}) async-start(bf16[64,8,3584]{2,1,0:T(8,128)(2,1)} %bitcast.64), calls=%async_computation.1 | async-start | bytes 7340032 | tf_op jit(solution)/shard_map/all_to_all | solution.py:56
  228.6 12.3 %all_gather.11 = bf16[1,3584,128]{2,1,0:T(8,128)(2,1)S(1)} all-gather(bf16[1,448,128]{2,1,0:T(8,128)(2,1)S(1)} %copy-done.1), channel_id=1, replica_groups=mesh['ep'=64,'dp'=8] {'dp'}, dimensions={1}, use_global_device_ids=true | all-gather | bytes 1032192 | tf_op jit(solution)/shard_map/all_gather | solution.py:65
  241.0 13.5 %all_gather.10 = bf16[1,3584,128]{2,1,0:T(8,128)(2,1)S(1)} all-gather(bf16[1,448,128]{2,1,0:T(8,128)(2,1)S(1)} %copy-done.2), channel_id=1, replica_groups=mesh['ep'=64,'dp'=8] {'dp'}, dimensions={1}, use_global_device_ids=true | all-gather | bytes 1032192 | tf_op jit(solution)/shard_map/all_gather | solution.py:66
  254.5 13.5 %all_gather.9 = bf16[1,3584,128]{2,1,0:T(8,128)(2,1)S(1)} all-gather(bf16[1,448,128]{2,1,0:T(8,128)(2,1)S(1)} %copy-done.3), channel_id=1, replica_groups=mesh['ep'=64,'dp'=8] {'dp'}, dimensions={1}, use_global_device_ids=true | all-gather | bytes 1032192 | tf_op jit(solution)/shard_map/all_gather | solution.py:67
  268.2 3.4 fusion.3
  271.5 3.4 fusion.5
  274.9 120.6 %all-to-all-done.1 = bf16[64,8,3584]{2,1,0:T(8,128)(2,1)} async-done(((bf16[64,8,3584]{2,1,0:T(8,128)(2,1)}), bf16[64,8,3584]{2,1,0:T(8,128)(2,1)}, u32[]{:S(2)}, u32[]{:S(2)}) %all-to-all-start.1) | async-done | bytes 3670048 | tf_op jit(solution)/shard_map/all_to_all | solution.py:56
  395.5 4.1 multiply_reduce_fusion
  400.3 6.0 all-to-all-start.4
  407.5 3.1 fusion
  410.6 10.2 %all-to-all-done.4 = bf16[64,1,8]{2,1,0:T(2,128)(2,1)S(1)} async-done(((bf16[64,1,8]{2,1,0:T(2,128)(2,1)}), bf16[64,1,8]{2,1,0:T(2,128)(2,1)S(1)}, u32[]{:S(2)}, u32[]{:S(2)}) %all-to-all-start.4) | async-done | bytes 1056 | tf_op jit(solution)/shard_map/all_to_all | solution.py:97
  420.8 5.6 all-to-all-start.3
  426.5 4.4 convolution_convert_fusion
  430.9 4.1 convolution_convert_fusion.1
  435.1 4.1 convolution_convert_fusion.2
  441.0 151.4 %all-to-all-done.3 = bf16[64,8,3584]{2,1,0:T(8,128)(2,1)} async-done(((bf16[64,8,3584]{2,1,0:T(8,128)(2,1)}), bf16[64,8,3584]{2,1,0:T(8,128)(2,1)}, u32[]{:S(2)}, u32[]{:S(2)}) %all-to-all-start.3) | async-done | bytes 3670048 | tf_op jit(solution)/shard_map/all_to_all | solution.py:90
  592.3 2.6 convert_reduce_fusion
  596.2 1.5 reduce_sum.50
  (58 shorter events, 13.3 us)
Async XLA Ops:
  12.8 33.3 %all-to-all-start = ((bf16[64,1,8]{2,1,0:T(2,128)(2,1)}), bf16[64,1,8]{2,1,0:T(2,128)(2,1)S(1)}, u32[]{:S(2)}, u32[]{:S(2)}) async-start(bf16[64,1,8]{2,1,0:T(2,128)(2,1)} %copy.29), calls=%async_computation | async-start | bytes 65536 | tf_op jit(solution)/shard_map/all_to_all | solution.py:57
  48.2 5.8 copy-start
  48.2 172.1 %all-to-all-start.2 = ((bf16[64,8,3584]{2,1,0:T(8,128)(2,1)}), bf16[64,8,3584]{2,1,0:T(8,128)(2,1)}, u32[]{:S(2)}, u32[]{:S(2)}) async-start(bf16[64,8,3584]{2,1,0:T(8,128)(2,1)} %bitcast.65), calls=%async_computation.2 | async-start | bytes 7340032 | tf_op jit(solution)/shard_map/all_to_all | solution.py:55
  222.4 6.2 %copy-start.1 = (bf16[1,448,128]{2,1,0:T(8,128)(2,1)S(1)}, bf16[1,448,128]{2,1,0:T(8,128)(2,1)}, u32[]{:S(2)}) copy-start(bf16[1,448,128]{2,1,0:T(8,128)(2,1)} %param.11) | copy-start | bytes 344068
  222.4 18.5 %copy-start.2 = (bf16[1,448,128]{2,1,0:T(8,128)(2,1)S(1)}, bf16[1,448,128]{2,1,0:T(8,128)(2,1)}, u32[]{:S(2)}) copy-start(bf16[1,448,128]{2,1,0:T(8,128)(2,1)} %param.12) | copy-start | bytes 344068
  222.4 32.0 %copy-start.3 = (bf16[1,448,128]{2,1,0:T(8,128)(2,1)S(1)}, bf16[1,448,128]{2,1,0:T(8,128)(2,1)}, u32[]{:S(2)}) copy-start(bf16[1,448,128]{2,1,0:T(8,128)(2,1)} %param.13) | copy-start | bytes 344068
  222.4 173.1 %all-to-all-start.1 = ((bf16[64,8,3584]{2,1,0:T(8,128)(2,1)}), bf16[64,8,3584]{2,1,0:T(8,128)(2,1)}, u32[]{:S(2)}, u32[]{:S(2)}) async-start(bf16[64,8,3584]{2,1,0:T(8,128)(2,1)} %bitcast.64), calls=%async_computation.1 | async-start | bytes 7340032 | tf_op jit(solution)/shard_map/all_to_all | solution.py:56
  400.3 20.4 %all-to-all-start.4 = ((bf16[64,1,8]{2,1,0:T(2,128)(2,1)}), bf16[64,1,8]{2,1,0:T(2,128)(2,1)S(1)}, u32[]{:S(2)}, u32[]{:S(2)}) async-start(bf16[64,1,8]{2,1,0:T(2,128)(2,1)} %convert_element_type.125), calls=%async_computation.4 | async-start | bytes 65536 | tf_op jit(solution)/shard_map/all_to_all | solution.py:97
  410.6 15.9 %copy-start.4 = (bf16[512,128]{0,1:T(8,128)(2,1)S(1)}, bf16[512,128]{0,1:T(8,128)(2,1)}, u32[]{:S(2)}) copy-start(bf16[512,128]{0,1:T(8,128)(2,1)} %get-tuple-element.26) | copy-start | bytes 393220
  420.8 171.6 %all-to-all-start.3 = ((bf16[64,8,3584]{2,1,0:T(8,128)(2,1)}), bf16[64,8,3584]{2,1,0:T(8,128)(2,1)}, u32[]{:S(2)}, u32[]{:S(2)}) async-start(bf16[64,8,3584]{2,1,0:T(8,128)(2,1)} %fusion), calls=%async_computation.3 | async-start | bytes 7340032 | tf_op jit(solution)/shard_map/all_to_all | solution.py:90
  426.4 171.3 %reduce-scatter.8.cloned.1.call-start = ((), (), s32[]{:S(2)}) async-start(), calls=%async_computation.10 | async-start | bytes 1032192 | tf_op jit(solution)/shard_map/reduce_scatter | solution.py:121
  430.9 166.9 %reduce-scatter.6.cloned.1.call-start = ((), (), s32[]{:S(2)}) async-start(), calls=%async_computation.9 | async-start | bytes 1032192 | tf_op jit(solution)/shard_map/reduce_scatter | solution.py:118
  435.1 162.6 %reduce-scatter.4.cloned.1.call-start = ((), (), s32[]{:S(2)}) async-start(), calls=%async_computation.8 | async-start | bytes 1032192 | tf_op jit(solution)/shard_map/reduce_scatter | solution.py:115
Sparse Core Ops, SparseCore 0:
  431.0 35.7 reduce-scatter.7
  470.2 39.6 reduce-scatter.5
  513.3 39.6 reduce-scatter.3
where the time goes:
time: 605 us; the launch traced here: 604 us
  waiting for transfers between devices  461 us (76%)
  starting transfers between devices  42.4 us (7%)
  blocking collectives  39.3 us (6%)
  matrix products  27.7 us (5%)
  local copies, waits for them, and re-layouts  14.9 us (2%)
  between operations  14 us (2%)
    all_to_all x1, waiting for transfers between devices, per_device(): lax.all_to_all(spread_tokens, 'ep', split_axis=0, concat_axis=0, tiled=True)  166 us
    all_to_all x1, waiting for transfers between devices, per_device(): lax.all_to_all(token_part.reshape(ep_size, capacity, features), 'ep', spl...  151 us
    all_to_all x1, waiting for transfers between devices, per_device(): lax.all_to_all(spread_grads, 'ep', split_axis=0, concat_axis=0, tiled=True)  121 us
    all_to_all x1, starting transfers between devices, per_device(): lax.all_to_all(spread_probs.astype(jnp.bfloat16), 'ep', split_axis=0, con...  18.7 us
    all_gather x1, blocking collectives, per_device(): lax.all_gather(up_weight, 'dp', axis=1, tiled=True)  13.5 us
    all_gather x1, blocking collectives, per_device(): lax.all_gather(down_weight, 'dp', axis=1, tiled=True)  13.5 us
    all_to_all x1, waiting for transfers between devices, per_device(): lax.all_to_all(spread_probs.astype(jnp.bfloat16), 'ep', split_axis=0, con...  12.8 us
    all_gather x1, blocking collectives, per_device(): lax.all_gather(gate_weight, 'dp', axis=1, tiled=True)  12.3 us
  transfers between devices with their start and end apart: 8, of which 5 were waited for; matrix products, arithmetic and copies ran while one was open for 6% of the time, Pallas kernels for 0%

commit v1 on v0

v1 whole, which is shorter than its diff:
```python
import jax
import jax.numpy as jnp
from jax import lax
from jax.sharding import Mesh, PartitionSpec as P

GROUP = 8
CAP = 8
HID = 128
PAD = 128
F32 = jnp.float32
BF16 = jnp.bfloat16
AXES = ("e", "zp", "y", "x", "c")
SWAP = [(0, 1), (1, 0)]


def dot(a, b, dims):
    return lax.dot_general(a, b, (dims, ((), ())), preferred_element_type=F32)


def split(v):
    high = lax.reduce_precision(v, 8, 7)
    return high.astype(BF16), (v - high).astype(BF16)


def columns(v):
    high, low = split(v)
    blank = jnp.zeros((v.shape[0], PAD - 2), BF16)
    return jnp.concatenate([high[:, None], low[:, None], blank], axis=1)


def joined(cols):
    return cols[:, 0].astype(F32) + cols[:, 1].astype(F32)


def swapped(x, axis):
    return lax.all_to_all(x, axis, 0, 0, tiled=True)


def shared(x, axis):
    n = lax.axis_size(axis)
    return swapped(jnp.broadcast_to(x[None], (n,) + x.shape).reshape(n * x.shape[0], -1), axis)


def per_device(tokens, grad_out, routes, route_probs, gate_weight, up_weight, down_weight):
    count, features = tokens.shape
    experts = lax.axis_size("e")
    ny = lax.axis_size("y")
    slots = experts * CAP

    own = jnp.concatenate([gate_weight[0], up_weight[0], down_weight[0]], axis=1)
    other = lax.ppermute(own, "zp", SWAP)
    block = jnp.concatenate(
        [own[:, : 2 * HID], other[:, : 2 * HID], own[:, 2 * HID :], other[:, 2 * HID :]], axis=1
    )
    weights = lax.all_gather(block, ("x", "c"), axis=0, tiled=True)
    w_gu, w_d = weights[:, : 4 * HID], weights[:, 4 * HID :]

    ids = jnp.arange(experts, dtype=jnp.int32)
    first, second = routes[:, 0:1] == ids, routes[:, 1:2] == ids
    named = (first | second).astype(BF16)
    place = jnp.arange(count)
    before = (place[:, None] > place[None, :]).astype(BF16)
    rank = dot(before, named, ((1,), (0,))).T
    taken = (named.T[:, None, :] > 0) & (rank[:, None, :] == jnp.arange(CAP, dtype=F32)[None, :, None])
    prob = jnp.where(first, route_probs[:, 0:1], 0.0) + jnp.where(second, route_probs[:, 1:2], 0.0)
    slot_prob = jnp.sum(jnp.where(taken, prob.T[:, None, :], 0.0), axis=2).reshape(slots)
    select = taken.astype(BF16).reshape(slots, count)
    send_tok = dot(select, tokens, ((1,), (0,))).astype(BF16)
    send_grd = dot(select, grad_out, ((1,), (0,))).astype(BF16)
    send_grd = jnp.concatenate([send_grd, columns(slot_prob)], axis=1)

    rows_tok = shared(swapped(send_tok, "e"), "y")
    rows_ext = shared(swapped(send_grd, "e"), "y")
    rows_grd = rows_ext[:, :features]
    rows_prob = joined(rows_ext[:, features : features + 2])[:, None]

    gu = dot(rows_tok, w_gu, ((1,), (0,)))
    gate_pre = jnp.concatenate([gu[:, :HID], gu[:, 2 * HID : 3 * HID]], axis=1)
    up_pre = jnp.concatenate([gu[:, HID : 2 * HID], gu[:, 3 * HID :]], axis=1)
    sig = jax.nn.sigmoid(gate_pre)
    act = gate_pre * sig
    hidden = (act * up_pre).astype(BF16)
    scaled = (rows_prob * rows_grd.astype(F32)).astype(BF16)
    down_grad = dot(rows_grd, w_d, ((1,), (0,)))
    scores = jnp.sum(hidden.astype(F32) * down_grad, axis=1)
    hidden_grad = rows_prob * down_grad
    gate_grad = (hidden_grad * up_pre * sig * (1.0 + gate_pre * (1.0 - sig))).astype(BF16)
    up_grad = (hidden_grad * act).astype(BF16)
    gu_grad = jnp.concatenate(
        [gate_grad[:, :HID], up_grad[:, :HID], gate_grad[:, HID:], up_grad[:, HID:]], axis=1
    )
    part = dot(gu_grad, w_gu, ((1,), (1,))).astype(BF16)
    part = jnp.concatenate([part, columns(scores)], axis=1)

    term_gu = dot(rows_tok, gu_grad, ((0,), (0,))).astype(BF16)
    term_d = dot(scaled, hidden, ((0,), (0,))).astype(BF16)
    terms = jnp.concatenate([term_gu, term_d], axis=1)
    sums = lax.psum_scatter(terms, ("x", "c"), scatter_dimension=0, tiled=True)
    keep = jnp.concatenate([sums[:, : 2 * HID], sums[:, 4 * HID : 5 * HID]], axis=1)
    give = jnp.concatenate([sums[:, 2 * HID : 4 * HID], sums[:, 5 * HID :]], axis=1)
    grads = (keep.astype(F32) + lax.ppermute(give, "zp", SWAP).astype(F32)).astype(BF16)

    back = jnp.sum(swapped(part, "y").astype(F32).reshape(ny, slots, -1), axis=0)
    back_score = columns(joined(back[:, features : features + 2]))
    back = jnp.concatenate([back[:, :features].astype(BF16), back_score], axis=1)
    back = swapped(back, "e")
    grad_tokens = dot(select, back[:, :features], ((0,), (0,))).astype(BF16)
    score = joined(back[:, features : features + 2]).reshape(experts, CAP, 1)
    score = jnp.sum(jnp.where(taken, score, 0.0), axis=1).T
    grad_probs = jnp.stack(
        [jnp.sum(jnp.where(first, score, 0.0), axis=1), jnp.sum(jnp.where(second, score, 0.0), axis=1)], axis=1
    )
    return (
        grad_tokens,
        grad_probs,
        grads[None, :, :HID],
        grads[None, :, HID : 2 * HID],
        grads[None, :, 2 * HID :],
    )


def solution(mesh):
    fine = Mesh(mesh.devices.reshape(mesh.shape["ep"] // GROUP, 2, GROUP // 2, -1, 2), AXES)
    rows, stored = P(AXES, None), P(AXES[:3], AXES[3:], None)
    return jax.shard_map(
        per_device,
        mesh=fine,
        in_specs=(rows, rows, rows, rows, stored, stored, stored),
        out_specs=(rows, rows, stored, stored, stored),
        check_vma=False,
    )
```

time: 605 us -> 262 us (0.43)
  the two profiles are of different devices: /device:TPU:4 before, /device:TPU:64 now
where the time goes in v1:
time: 262 us; the launch traced here: 261 us
  blocking collectives  121 us (46%)
  waiting for transfers between devices  57.5 us (22%)
  starting transfers between devices  24.1 us (9%)
  local copies, waits for them, and re-layouts  22 us (8%)
  matrix products  15.1 us (6%)
  between operations  14.4 us (5%)
  other arithmetic  6.34 us (2%)
    all_to_all x4, blocking collectives, swapped(): return lax.all_to_all(x, axis, 0, 0, tiled=True)  121 us
    all_to_all x2, waiting for transfers between devices, swapped(): return lax.all_to_all(x, axis, 0, 0, tiled=True)  42.9 us
    all_to_all x2, starting transfers between devices, swapped(): return lax.all_to_all(x, axis, 0, 0, tiled=True)  18.1 us
    dot_general x9, matrix products, dot(): return lax.dot_general(a, b, (dims, ((), ())), preferred_element_type=F32)  15.1 us
    unnamed x24, local copies, waits for them, and re-layouts  14.7 us
    ppermute x1, waiting for transfers between devices, per_device(): lax.ppermute(give, 'zp', SWAP).astype(F32)  8.36 us
    ppermute x1, waiting for transfers between devices, per_device(): other = lax.ppermute(own, 'zp', SWAP)  6.19 us
  transfers between devices with their start and end apart: 6, of which 4 were waited for; matrix products, arithmetic and copies ran while one was open for 6% of the time, Pallas kernels for 0%

profile of v1, /device:TPU:64, one launch (start us, length us, event | category | flops | bytes accessed | tf_op | source)
XLA Modules:
  0.0 260.8 jit_solution(7313951598226510619)
XLA Ops:
  7.2 1.1 pad_maximum_fusion.2
  8.3 4.0 %collective-permute-start = (bf16[448,384]{1,0:T(8,128)(2,1)S(1)}, bf16[448,384]{1,0:T(8,128)(2,1)S(1)}, u32[]{:S(2)}, u32[]{:S(2)}) collective-permute-start(bf16[448,384]{1,0:T(8,128)(2,1)S(1)} %pad_maximum_fusion.2), channel_id=1, source_target_pairs={{0,32},{32,0},{1,33},{33,1},{2,34},{34,2},{3,35},{35,3},{4,36},{36... | collective-permute-start | bytes 1032200 | tf_op jit(solution)/shard_map/ppermute | solution.py:51
  14.1 6.2 %collective-permute-done = bf16[448,384]{1,0:T(8,128)(2,1)S(1)} collective-permute-done((bf16[448,384]{1,0:T(8,128)(2,1)S(1)}, bf16[448,384]{1,0:T(8,128)(2,1)S(1)}, u32[]{:S(2)}, u32[]{:S(2)}) %collective-permute-start) | collective-permute-done | bytes 344096 | tf_op jit(solution)/shard_map/ppermute | solution.py:51
  22.4 1.1 fusion.1
  23.6 14.5 %all-to-all-start.2 = ((bf16[8,8,3584]{2,1,0:T(8,128)(2,1)}), bf16[8,8,3584]{2,1,0:T(8,128)(2,1)S(1)}, u32[]{:S(2)}, u32[]{:S(2)}) async-start(bf16[8,8,3584]{2,1,0:T(8,128)(2,1)} %fusion.1), calls=%async_computation.2 | async-start | bytes 917504 | tf_op jit(solution)/shard_map/all_to_all | solution.py:36
  39.0 26.6 %all-to-all-done.2 = bf16[8,8,3584]{2,1,0:T(8,128)(2,1)S(1)} async-done(((bf16[8,8,3584]{2,1,0:T(8,128)(2,1)}), bf16[8,8,3584]{2,1,0:T(8,128)(2,1)S(1)}, u32[]{:S(2)}, u32[]{:S(2)}) %all-to-all-start.2) | async-done | bytes 458784 | tf_op jit(solution)/shard_map/all_to_all | solution.py:36
  65.6 32.5 %all_to_all.48 = bf16[8,8,3712]{2,1,0:T(8,128)(2,1)S(1)} all-to-all(bf16[8,8,3712]{2,1,0:T(8,128)(2,1)S(1)} %concatenate.52), channel_id=1, replica_groups=mesh['e'=8,'zp'=2,'y'=4,'x'=4,'c'=2] {'e'}, dimensions={0} | all-to-all | bytes 950272 | tf_op jit(solution)/shard_map/all_to_all | solution.py:36
  98.2 23.7 %all_to_all.49 = bf16[4,64,3712]{2,1,0:T(8,128)(2,1)} all-to-all(bf16[4,64,3712]{2,1,0:T(8,128)(2,1)S(1)} %broadcast_in_dim.100), channel_id=1, replica_groups=mesh['e'=8,'zp'=2,'y'=4,'x'=4,'c'=2] {'y'}, dimensions={0} | all-to-all | bytes 3801088 | tf_op jit(solution)/shard_map/all_to_all | solution.py:36
  121.9 1.4 broadcast_in_dim.102
  123.3 3.6 %all-to-all-start.3 = ((bf16[4,64,3584]{2,1,0:T(8,128)(2,1)}), bf16[4,64,3584]{2,1,0:T(8,128)(2,1)S(1)}, u32[]{:S(2)}, u32[]{:S(2)}) async-start(bf16[4,64,3584]{2,1,0:T(8,128)(2,1)} %broadcast_in_dim.102), calls=%async_computation.3 | async-start | bytes 3670016 | tf_op jit(solution)/shard_map/all_to_all | solution.py:36
  127.0 1.1 add_reduce_fusion
  128.1 16.3 %all-to-all-done.3 = bf16[4,64,3584]{2,1,0:T(8,128)(2,1)S(1)} async-done(((bf16[4,64,3584]{2,1,0:T(8,128)(2,1)}), bf16[4,64,3584]{2,1,0:T(8,128)(2,1)S(1)}, u32[]{:S(2)}, u32[]{:S(2)}) %all-to-all-start.3) | async-done | bytes 1835040 | tf_op jit(solution)/shard_map/all_to_all | solution.py:36
  144.4 3.7 %fusion.3 = f32[256,512]{0,1:T(8,128)S(1)} fusion(bf16[256,3584]{1,0:T(8,128)(2,1)S(1)} %bitcast.66, bf16[3584,768]{1,0:T(8,128)(2,1)} %all-gather.2.cloned.1.call-done), kind=kOutput, calls=%fused_computation.12 | convolution fusion | flops 939524096 | bytes 6029312 | tf_op jit(solution)/shard_map/dot_general | solution.py:17
  148.2 2.4 multiply_reduce_fusion
  151.4 1.1 convolution_convert_fusion
  152.5 2.7 %pad_maximum_fusion = bf16[3584,768]{0,1:T(8,128)(2,1)} fusion(bf16[3584,256]{0,1:T(8,128)(2,1)S(1)} %convolution_convert_fusion.1, bf16[3584,512]{0,1:T(8,128)(2,1)S(1)} %convolution_convert_fusion), kind=kLoop, calls=%fused_computation.1 | loop fusion | flops 11010048 | bytes 11010048 | tf_op jit(solution)/shard_map/concatenate | solution.py:97
  155.2 8.3 %copy.76 = bf16[3584,768]{1,0:T(8,128)(2,1)} copy(bf16[3584,768]{0,1:T(8,128)(2,1)} %pad_maximum_fusion) | data formatting | bytes 11010048
  163.9 4.5 %convolution_convert_fusion.2 = bf16[256,3584]{1,0:T(8,128)(2,1)} fusion(bf16[3584,768]{1,0:T(8,128)(2,1)} %all-gather.2.cloned.1.call-done, bf16[256,128]{0,1:T(8,128)(2,1)S(1)} %get-tuple-element.61, bf16[256,128]{0,1:T(8,128)(2,1)S(1)} %get-tuple-element.50, bf16[256,128]{0,1:T(8,128)(2,1)S(1)} %get-tuple-element.62, ...), kind=kOutput, calls=%fused_computation.3 | convolution fusion | flops 941490176 | bytes 5767168 | tf_op jit(solution)/shard_map/dot_general | solution.py:17
  168.4 2.4 concatenate.59
  170.9 19.5 %all_to_all.50 = bf16[4,64,3712]{2,1,0:T(8,128)(2,1)S(1)} all-to-all(bf16[4,64,3712]{2,1,0:T(8,128)(2,1)S(1)} %concatenate.59), channel_id=1, replica_groups=mesh['e'=8,'zp'=2,'y'=4,'x'=4,'c'=2] {'y'}, dimensions={0} | all-to-all | bytes 3801088 | tf_op jit(solution)/shard_map/all_to_all | solution.py:36
  190.8 45.8 %all_to_all.51 = bf16[8,8,3712]{2,1,0:T(8,128)(2,1)S(1)} all-to-all(bf16[8,8,3712]{2,1,0:T(8,128)(2,1)S(1)} %concatenate.63), channel_id=1, replica_groups=mesh['e'=8,'zp'=2,'y'=4,'x'=4,'c'=2] {'e'}, dimensions={0} | all-to-all | bytes 950272 | tf_op jit(solution)/shard_map/all_to_all | solution.py:36
  238.1 1.1 fusion.44
  239.4 1.9 collective-permute-start.1
  243.2 8.4 %collective-permute-done.1 = bf16[448,384]{0,1:T(8,128)(2,1)S(1)} collective-permute-done((bf16[448,384]{0,1:T(8,128)(2,1)S(1)}, bf16[448,384]{0,1:T(8,128)(2,1)S(1)}, u32[]{:S(2)}, u32[]{:S(2)}) %collective-permute-start.1) | collective-permute-done | bytes 344096 | tf_op jit(solution)/shard_map/ppermute | solution.py:101
  (67 shorter events, 12.6 us)
Async XLA Ops:
  7.2 15.3 %copy-start = (bf16[24,3584]{1,0:T(8,128)(2,1)S(1)}, bf16[24,3584]{1,0:T(8,128)(2,1)}, u32[]{:S(2)}) copy-start(bf16[24,3584]{1,0:T(8,128)(2,1)} %param.7) | copy-start | bytes 516100
  7.2 15.1 %copy-start.4 = (s32[24,2]{0,1:T(2,128)S(1)}, s32[24,2]{0,1:T(2,128)}, u32[]{:S(2)}) copy-start(s32[24,2]{0,1:T(2,128)} %param.9) | copy-start | bytes 580
  7.2 137.2 %all-gather.2.cloned.1.call-start = ((), (), s32[]{:S(2)}) async-start(), calls=%async_computation.7 | async-start | bytes 6193152 | tf_op jit(solution)/shard_map/all_gather | solution.py:55
  8.3 29.8 %copy-start.5 = (f32[24,2]{0,1:T(2,128)S(1)}, f32[24,2]{0,1:T(2,128)}, u32[]{:S(2)}) copy-start(f32[24,2]{0,1:T(2,128)} %param.10) | copy-start | bytes 580
  8.3 30.2 %copy-start.3 = (bf16[24,3584]{1,0:T(8,128)(2,1)S(1)}, bf16[24,3584]{1,0:T(8,128)(2,1)}, u32[]{:S(2)}) copy-start(bf16[24,3584]{1,0:T(8,128)(2,1)} %param.8) | copy-start | bytes 516100
  8.3 12.0 %collective-permute-start = (bf16[448,384]{1,0:T(8,128)(2,1)S(1)}, bf16[448,384]{1,0:T(8,128)(2,1)S(1)}, u32[]{:S(2)}, u32[]{:S(2)}) collective-permute-start(bf16[448,384]{1,0:T(8,128)(2,1)S(1)} %pad_maximum_fusion.2), channel_id=1, source_target_pairs={{0,32},{32,0},{1,33},{33,1},{2,34},{34,2},{3,35},{35,3},{4,36},{36... | collective-permute-start | bytes 1032200 | tf_op jit(solution)/shard_map/ppermute | solution.py:51
  21.3 0.8 copy-start.2
  23.6 42.1 %all-to-all-start.2 = ((bf16[8,8,3584]{2,1,0:T(8,128)(2,1)}), bf16[8,8,3584]{2,1,0:T(8,128)(2,1)S(1)}, u32[]{:S(2)}, u32[]{:S(2)}) async-start(bf16[8,8,3584]{2,1,0:T(8,128)(2,1)} %fusion.1), calls=%async_computation.2 | async-start | bytes 917504 | tf_op jit(solution)/shard_map/all_to_all | solution.py:36
  123.3 21.0 %all-to-all-start.3 = ((bf16[4,64,3584]{2,1,0:T(8,128)(2,1)}), bf16[4,64,3584]{2,1,0:T(8,128)(2,1)S(1)}, u32[]{:S(2)}, u32[]{:S(2)}) async-start(bf16[4,64,3584]{2,1,0:T(8,128)(2,1)} %broadcast_in_dim.102), calls=%async_computation.3 | async-start | bytes 3670016 | tf_op jit(solution)/shard_map/all_to_all | solution.py:36
  126.9 110.1 %reduce-scatter.4.cloned.1.call-start = ((), (), s32[]{:S(2)}) async-start(), calls=%async_computation.8 | async-start | bytes 6193152
  144.4 3.8 %copy-start.1 = (bf16[4,64,3712]{2,1,0:T(8,128)(2,1)S(1)}, bf16[4,64,3712]{2,1,0:T(8,128)(2,1)}, u32[]{:S(2)}) copy-start(bf16[4,64,3712]{2,1,0:T(8,128)(2,1)} %all_to_all.49) | copy-start | bytes 5701636
  239.4 12.1 %collective-permute-start.1 = (bf16[448,384]{0,1:T(8,128)(2,1)S(1)}, bf16[448,384]{0,1:T(8,128)(2,1)S(1)}, u32[]{:S(2)}, u32[]{:S(2)}) collective-permute-start(bf16[448,384]{0,1:T(8,128)(2,1)S(1)} %pad_maximum_fusion.1), channel_id=1, source_target_pairs={{0,32},{32,0},{1,33},{33,1},{2,34},{34,2},{3,35},{35,3},{4,36},{36... | collective-permute-start | bytes 1032200 | tf_op jit(solution)/shard_map/ppermute | solution.py:101
Sparse Core Ops, SparseCore 0:
  22.3 48.7 all-gather.1
  163.7 49.6 reduce-scatter.3

commit v2 on v1

v2 whole, which is shorter than its diff:
```python
import functools

import jax
import jax.numpy as jnp
from jax import lax
from jax.experimental import pallas as pl
from jax.experimental.pallas import tpu as pltpu
from jax.sharding import Mesh, PartitionSpec as P


GROUP = 8
CAP = 8
HID = 128
PAD = 128
F32 = jnp.float32
BF16 = jnp.bfloat16
AXES = ("e", "zp", "y", "x", "c")
HOLD = ("zp", "x", "c")
KINDS = 3


def dot(a, b, dims):
    return lax.dot_general(a, b, (dims, ((), ())), preferred_element_type=F32)


def split(v):
    high = lax.reduce_precision(v, 8, 7)
    return high.astype(BF16), (v - high).astype(BF16)


def columns(v):
    high, low = split(v)
    blank = jnp.zeros((v.shape[0], PAD - 2), BF16)
    return jnp.concatenate([high[:, None], low[:, None], blank], axis=1)


def joined(cols):
    return cols[:, 0].astype(F32) + cols[:, 1].astype(F32)


def swapped(x, axis):
    return lax.all_to_all(x, axis, 0, 0, tiled=True)


def shared(x, axis):
    n = lax.axis_size(axis)
    return swapped(jnp.broadcast_to(x[None], (n,) + x.shape).reshape(n * x.shape[0], -1), axis)


def expert_kernel(nz, nx, tok_hbm, ext_hbm, w_hbm, terms_hbm, part_hbm,
                  tok, ext, w, terms, part, gu_acc, d_acc, row_sem, w_sem, terms_sem, part_sem):
    features = tok.shape[1]
    chunk = features // nx
    piece = chunk // 2

    def pieces(x):
        for z in range(nz):
            for c in range(2):
                for m in range(KINDS):
                    yield ((z * nx + x) * 2 + c) * KINDS + m, x * chunk + c * piece, (m * nz + z) * HID

    load_tok = pltpu.make_async_copy(tok_hbm, tok, row_sem.at[0])
    load_ext = pltpu.make_async_copy(ext_hbm, ext, row_sem.at[1])
    load_tok.start()
    loads = []
    for x in range(nx):
        if x == 1:
            load_ext.start()
        loads.append([])
        for i, row, col in pieces(x):
            copy = pltpu.make_async_copy(
                w_hbm.at[pl.ds(i * piece, piece), :],
                w.at[pl.ds(row, piece), pl.ds(col, HID)],
                w_sem.at[i],
            )
            copy.start()
            loads[-1].append(copy)
    wide = nz * HID
    load_tok.wait()
    for x in range(nx):
        for copy in loads[x]:
            copy.wait()
        if x == 0:
            load_ext.wait()
        span = slice(x * chunk, (x + 1) * chunk)
        gu = dot(tok[:, span], w[span, : 2 * wide], ((1,), (0,)))
        dg = dot(ext[:, span], w[span, 2 * wide :], ((1,), (0,)))
        if x == 0:
            gu_acc[...] = gu
            d_acc[...] = dg
        else:
            gu_acc[...] += gu
            d_acc[...] += dg
    extra = ext[:, features:].astype(F32)
    prob = extra[:, 0:1] + extra[:, 1:2]
    gate_pre, up_pre = gu_acc[:, :wide], gu_acc[:, wide:]
    down_grad = d_acc[...]
    sig = jax.nn.sigmoid(gate_pre)
    act = gate_pre * sig
    hidden = (act * up_pre).astype(BF16)
    scores = jnp.sum(hidden.astype(F32) * down_grad, axis=1, keepdims=True)
    hidden_grad = prob * down_grad
    gate_grad = (hidden_grad * up_pre * sig * (1.0 + gate_pre * (1.0 - sig))).astype(BF16)
    up_grad = (hidden_grad * act).astype(BF16)
    gu_grad = jnp.concatenate([gate_grad, up_grad], axis=1)
    stores = []
    for x in range(nx):
        span = slice(x * chunk, (x + 1) * chunk)
        terms[span, : 2 * wide] = dot(tok[:, span], gu_grad, ((0,), (0,))).astype(BF16)
        scaled = (prob * ext[:, span].astype(F32)).astype(BF16)
        terms[span, 2 * wide :] = dot(scaled, hidden, ((0,), (0,))).astype(BF16)
        for i, row, col in pieces(x):
            copy = pltpu.make_async_copy(
                terms.at[pl.ds(row, piece), pl.ds(col, HID)],
                terms_hbm.at[pl.ds(i * piece, piece), :],
                terms_sem.at[i],
            )
            copy.start()
            stores.append(copy)
    lane = lax.broadcasted_iota(jnp.int32, (scores.shape[0], PAD), 1)
    high = scores.astype(BF16).astype(F32)
    low = scores - high
    part[:, features:] = jnp.where(lane == 0, high, jnp.where(lane == 1, low, 0.0)).astype(BF16)
    for x in range(nx):
        span = slice(x * chunk, (x + 1) * chunk)
        part[:, span] = dot(gu_grad, w[span, : 2 * wide], ((1,), (1,))).astype(BF16)
        if x == nx - 1:
            span = slice(x * chunk, features + PAD)
        copy = pltpu.make_async_copy(part.at[:, span], part_hbm.at[:, span], part_sem.at[x])
        copy.start()
        stores.append(copy)
    for copy in stores:
        copy.wait()


def expert_math(tok, ext, w, nz, nx):
    rows, features = tok.shape
    held = w.shape[0]
    wide = nz * HID
    spec = pl.BlockSpec(memory_space=pl.ANY)
    count = nz * nx * 2 * KINDS
    return pl.pallas_call(
        functools.partial(expert_kernel, nz, nx),
        name="expert_math",
        out_shape=(
            jax.ShapeDtypeStruct((held, HID), BF16),
            jax.ShapeDtypeStruct((rows, features + PAD), BF16),
        ),
        in_specs=[spec] * 3,
        out_specs=(spec, spec),
        scratch_shapes=[
            pltpu.VMEM((rows, features), BF16),
            pltpu.VMEM((rows, features + PAD), BF16),
            pltpu.VMEM((features, KINDS * wide), BF16),
            pltpu.VMEM((features, KINDS * wide), BF16),
            pltpu.VMEM((rows, features + PAD), BF16),
            pltpu.VMEM((rows, 2 * wide), F32),
            pltpu.VMEM((rows, wide), F32),
            pltpu.SemaphoreType.DMA((2,)),
            pltpu.SemaphoreType.DMA((count,)),
            pltpu.SemaphoreType.DMA((count,)),
            pltpu.SemaphoreType.DMA((nx,)),
        ],
        cost_estimate=pl.CostEstimate(
            flops=16 * rows * features * wide,
            transcendentals=rows * wide,
            bytes_accessed=2 * (2 * held * HID + 3 * rows * features),
        ),
    )(tok, ext, w)


def layer(tokens, grad_out, routes, route_probs, gate_weight, up_weight, down_weight):
    count, features = tokens.shape
    experts, ny = lax.axis_size("e"), lax.axis_size("y")
    nz, nx = lax.axis_size("zp"), lax.axis_size("x")
    slots = experts * CAP

    stored = jnp.concatenate([gate_weight[0], up_weight[0], down_weight[0]], axis=0)
    weights = lax.all_gather(stored, HOLD, axis=0, tiled=True)

    ids = jnp.arange(experts, dtype=jnp.int32)
    first, second = routes[:, 0:1] == ids, routes[:, 1:2] == ids
    named = (first | second).astype(BF16)
    place = jnp.arange(count)
    before = (place[:, None] > place[None, :]).astype(BF16)
    rank = dot(before, named, ((1,), (0,))).T
    taken = (named.T[:, None, :] > 0) & (rank[:, None, :] == jnp.arange(CAP, dtype=F32)[None, :, None])
    prob = jnp.where(first, route_probs[:, 0:1], 0.0) + jnp.where(second, route_probs[:, 1:2], 0.0)
    slot_prob = jnp.sum(jnp.where(taken, prob.T[:, None, :], 0.0), axis=2).reshape(slots)
    select = taken.astype(BF16).reshape(slots, count)
    send_tok = dot(select, tokens, ((1,), (0,))).astype(BF16)
    send_grd = dot(select, grad_out, ((1,), (0,))).astype(BF16)
    send_grd = jnp.concatenate([send_grd, columns(slot_prob)], axis=1)

    came_tok = swapped(send_tok, "e")
    came_tok, send_grd = lax.optimization_barrier((came_tok, send_grd))
    rows_tok = lax.all_gather(came_tok, "y", axis=0, tiled=True)
    rows_ext = shared(swapped(send_grd, "e"), "y")

    terms, part = expert_math(rows_tok, rows_ext, weights, nz, nx)
    sums = lax.psum_scatter(terms, HOLD, scatter_dimension=0, tiled=True)
    grads = sums.reshape(KINDS, 1, -1, HID)

    back = jnp.sum(swapped(part, "y").astype(F32).reshape(ny, slots, -1), axis=0)
    back_score = columns(joined(back[:, features : features + 2]))
    back = jnp.concatenate([back[:, :features].astype(BF16), back_score], axis=1)
    back = swapped(back, "e")
    grad_tokens = dot(select, back[:, :features], ((0,), (0,))).astype(BF16)
    score = joined(back[:, features : features + 2]).reshape(experts, CAP, 1)
    score = jnp.sum(jnp.where(taken, score, 0.0), axis=1).T
    grad_probs = jnp.stack(
        [jnp.sum(jnp.where(first, score, 0.0), axis=1), jnp.sum(jnp.where(second, score, 0.0), axis=1)], axis=1
    )
    return (grad_tokens, grad_probs, grads[0], grads[1], grads[2])


def solution(mesh):
    fine = Mesh(mesh.devices.reshape(mesh.shape["ep"] // GROUP, 2, GROUP // 2, -1, 2), AXES)
    rows, stored = P(AXES, None), P(AXES[:3], AXES[3:], None)
    return jax.shard_map(
        layer,
        mesh=fine,
        in_specs=(rows, rows, rows, rows, stored, stored, stored),
        out_specs=(rows, rows, stored, stored, stored),
        check_vma=False,
    )
```

time: 262 us -> 247 us (0.943)
  the two profiles are of different devices: /device:TPU:64 before, /device:TPU:71 now
where the time goes in v2:
time: 247 us
  blocking collectives  97.8 us (40%)
  waiting for transfers between devices  92.3 us (37%)
  starting transfers between devices  17.9 us (7%)
  between operations  13.9 us (6%)
  Pallas kernels  11.7 us (5%)
  local copies, waits for them, and re-layouts  7.68 us (3%)
  matrix products  3.48 us (1%)
    all_to_all x3, blocking collectives, swapped(): return lax.all_to_all(x, axis, 0, 0, tiled=True)  97.8 us
    all_to_all x2, waiting for transfers between devices, swapped(): return lax.all_to_all(x, axis, 0, 0, tiled=True)  45.3 us
    all_gather x1, waiting for transfers between devices, layer(): weights = lax.all_gather(stored, HOLD, axis=0, tiled=True)  24 us
    reduce_scatter x1, waiting for transfers between devices, layer(): sums = lax.psum_scatter(terms, HOLD, scatter_dimension=0, tiled=True)  22.9 us
    all_to_all x2, starting transfers between devices, swapped(): return lax.all_to_all(x, axis, 0, 0, tiled=True)  17.8 us
    pallas_call x1, Pallas kernels, expert_math(): pl.pallas_call(functools.partial(expert_kernel, nz, nx), name='expert_mat...  11.7 us
  transfers between devices with their start and end apart: 5, of which 4 were waited for; matrix products, arithmetic and copies ran while one was open for 3% of the time, Pallas kernels for 0%

profile of v2, /device:TPU:71, one launch (start us, length us, event | category | flops | bytes accessed | tf_op | source)
XLA Modules:
  0.0 246.8 jit_solution(1868339645129320065)
XLA Ops:
  7.2 0.8 slice_bitcast_fusion.6
  8.0 0.1 fusion.20
  8.2 1.1 fusion
  9.3 14.2 %all-to-all-start = ((bf16[8,8,3584]{2,1,0:T(8,128)(2,1)}), bf16[8,8,3584]{2,1,0:T(8,128)(2,1)S(1)}, u32[]{:S(2)}, u32[]{:S(2)}) async-start(bf16[8,8,3584]{2,1,0:T(8,128)(2,1)} %fusion), calls=%async_computation | async-start | bytes 917504 | tf_op jit(solution)/shard_map/all_to_all | solution.py:42
  23.5 0.8 slice_bitcast_fusion.4
  24.7 1.2 convolution_convert_fusion
  26.1 26.1 %all-to-all-done = bf16[8,8,3584]{2,1,0:T(8,128)(2,1)S(1)} async-done(((bf16[8,8,3584]{2,1,0:T(8,128)(2,1)}), bf16[8,8,3584]{2,1,0:T(8,128)(2,1)S(1)}, u32[]{:S(2)}, u32[]{:S(2)}) %all-to-all-start) | async-done | bytes 458784 | tf_op jit(solution)/shard_map/all_to_all | solution.py:42
  52.1 0.8 copy-done.3
  53.0 0.8 pad_maximum_fusion
  53.8 29.7 %all_to_all.47 = bf16[8,8,3712]{2,1,0:T(8,128)(2,1)S(1)} all-to-all(bf16[8,8,3712]{2,1,0:T(8,128)(2,1)S(1)} %bitcast.59), channel_id=1, replica_groups=mesh['e'=8,'zp'=2,'y'=4,'x'=4,'c'=2] {'e'}, dimensions={0} | all-to-all | bytes 950272 | tf_op jit(solution)/shard_map/all_to_all | solution.py:42
  83.5 1.4 broadcast_in_dim.77
  84.9 3.6 %all-to-all-start.2 = ((bf16[4,64,3712]{2,1,0:T(8,128)(2,1)}), bf16[4,64,3712]{2,1,0:T(8,128)(2,1)S(1)}, u32[]{:S(2)}, u32[]{:S(2)}) async-start(bf16[4,64,3712]{2,1,0:T(8,128)(2,1)} %broadcast_in_dim.77), calls=%async_computation.2 | async-start | bytes 3801088 | tf_op jit(solution)/shard_map/all_to_all | solution.py:42
  88.6 19.2 %all-to-all-done.2 = bf16[4,64,3712]{2,1,0:T(8,128)(2,1)S(1)} async-done(((bf16[4,64,3712]{2,1,0:T(8,128)(2,1)}), bf16[4,64,3712]{2,1,0:T(8,128)(2,1)S(1)}, u32[]{:S(2)}, u32[]{:S(2)}) %all-to-all-start.2) | async-done | bytes 1900576 | tf_op jit(solution)/shard_map/all_to_all | solution.py:42
  107.8 24.0 %all-gather.5.cloned.1.call-done.w_hbm = bf16[21504,128]{1,0:T(8,128)(2,1)} async-done(((bf16[1344,128]{1,0:T(8,128)(2,1)}), bf16[21504,128]{1,0:T(8,128)(2,1)}) %all-gather.5.cloned.1.call-update) | async-done | bytes 5505040 | tf_op jit(solution)/shard_map/all_gather | solution.py:179
  131.7 11.7 %expert_math.1 = (bf16[21504,128]{1,0:T(8,128)(2,1)}, bf16[256,3712]{1,0:T(8,128)(2,1)}) custom-call(bf16[256,3584]{1,0:T(8,128)(2,1)} %all-gather.3.cloned.1.call-done.tok_hbm, bf16[256,3712]{1,0:T(8,128)(2,1)} %bitcast.57, bf16[21504,128]{1,0:T(8,128)(2,1)} %all-gather.5.cloned.1.call-done.w_hbm), custom_call_target="tpu_custom_call" | custom-call | flops 3758096384 | bytes 16515072 | tf_op jit(solution)/shard_map/expert_math/pallas_call | solution.py:142
  143.5 1.5 copy-done.2
  145.0 27.5 %all_to_all.48 = bf16[4,64,3712]{2,1,0:T(8,128)(2,1)S(1)} all-to-all(bf16[4,64,3712]{2,1,0:T(8,128)(2,1)S(1)} %bitcast.58), channel_id=1, replica_groups=mesh['e'=8,'zp'=2,'y'=4,'x'=4,'c'=2] {'y'}, dimensions={0} | all-to-all | bytes 3801088 | tf_op jit(solution)/shard_map/all_to_all | solution.py:42
  172.5 0.3 convert_reduce_fusion
  173.0 40.6 %all_to_all.49 = bf16[8,8,3712]{2,1,0:T(8,128)(2,1)S(1)} all-to-all(bf16[8,8,3712]{2,1,0:T(8,128)(2,1)S(1)} %concatenate.24), channel_id=1, replica_groups=mesh['e'=8,'zp'=2,'y'=4,'x'=4,'c'=2] {'e'}, dimensions={0} | all-to-all | bytes 950272 | tf_op jit(solution)/shard_map/all_to_all | solution.py:42
  213.6 0.2 add_reduce_fusion
  214.0 0.6 pad_maximum_fusion.1
  214.6 1.0 convolution_convert_fusion.2
  215.6 22.9 %reduce-scatter.2.cloned.1.call-done = bf16[1344,128]{1,0:T(8,128)(2,1)} async-done(((bf16[21504,128]{1,0:T(8,128)(2,1)}), bf16[1344,128]{1,0:T(8,128)(2,1)}) %reduce-scatter.2.cloned.1.call-update) | async-done | bytes 344080 | tf_op jit(solution)/shard_map/reduce_scatter | solution.py:201
  238.5 1.7 slice_bitcast_fusion
  (37 shorter events, 1.2 us)
Async XLA Ops:
  7.2 1.0 copy-start
  7.2 45.8 %copy-start.6 = (bf16[1,448,128]{2,1,0:T(8,128)(2,1)S(1)}, bf16[1,448,128]{2,1,0:T(8,128)(2,1)}, u32[]{:S(2)}) copy-start(bf16[1,448,128]{2,1,0:T(8,128)(2,1)} %param.11) | copy-start | bytes 344068
  7.2 45.8 %copy-start.5 = (bf16[1,448,128]{2,1,0:T(8,128)(2,1)S(1)}, bf16[1,448,128]{2,1,0:T(8,128)(2,1)}, u32[]{:S(2)}) copy-start(bf16[1,448,128]{2,1,0:T(8,128)(2,1)} %param.12) | copy-start | bytes 344068
  7.2 45.8 %copy-start.4 = (bf16[1,448,128]{2,1,0:T(8,128)(2,1)S(1)}, bf16[1,448,128]{2,1,0:T(8,128)(2,1)}, u32[]{:S(2)}) copy-start(bf16[1,448,128]{2,1,0:T(8,128)(2,1)} %param.13) | copy-start | bytes 344068
  9.3 42.8 %all-to-all-start = ((bf16[8,8,3584]{2,1,0:T(8,128)(2,1)}), bf16[8,8,3584]{2,1,0:T(8,128)(2,1)S(1)}, u32[]{:S(2)}, u32[]{:S(2)}) async-start(bf16[8,8,3584]{2,1,0:T(8,128)(2,1)} %fusion), calls=%async_computation | async-start | bytes 917504 | tf_op jit(solution)/shard_map/all_to_all | solution.py:42
  23.5 65.1 %all-gather.3.cloned.1.call-start = ((), (), s32[]{:S(2)}) async-start(), calls=%async_computation.6 | async-start | bytes 2293760 | tf_op jit(solution)/shard_map/all_gather | solution.py:197
  52.1 0.8 copy-start.3
  52.9 78.8 %all-gather.5.cloned.1.call-start = ((), (), s32[]{:S(2)}) async-start(), calls=%async_computation.7 | async-start | bytes 5849088 | tf_op jit(solution)/shard_map/all_gather | solution.py:179
  84.9 22.9 %all-to-all-start.2 = ((bf16[4,64,3712]{2,1,0:T(8,128)(2,1)}), bf16[4,64,3712]{2,1,0:T(8,128)(2,1)S(1)}, u32[]{:S(2)}, u32[]{:S(2)}) async-start(bf16[4,64,3712]{2,1,0:T(8,128)(2,1)} %broadcast_in_dim.77), calls=%async_computation.2 | async-start | bytes 3801088 | tf_op jit(solution)/shard_map/all_to_all | solution.py:42
  88.5 150.0 %reduce-scatter.2.cloned.1.call-start = ((), (), s32[]{:S(2)}) async-start(), calls=%async_computation.8 | async-start | bytes 5849088 | tf_op jit(solution)/shard_map/reduce_scatter | solution.py:201
  107.8 24.0 %copy-start.1 = (bf16[4,64,3712]{2,1,0:T(8,128)(2,1)}, bf16[4,64,3712]{2,1,0:T(8,128)(2,1)S(1)}, u32[]{:S(2)}) copy-start(bf16[4,64,3712]{2,1,0:T(8,128)(2,1)S(1)} %all-to-all-done.2) | copy-start | bytes 5701636
  143.4 1.5 copy-start.2
Sparse Core Ops, SparseCore 0:
  53.0 29.5 all-gather.2
  84.8 46.9 all-gather.4
  143.6 94.8 reduce-scatter.1

commit v3 on v2

--- a/solution.py
+++ b/solution.py
@@ -15,7 +15,8 @@
 F32 = jnp.float32
 BF16 = jnp.bfloat16
 AXES = ("e", "zp", "y", "x", "c")
-HOLD = ("zp", "x", "c")
+HOLD = ("x", "c")
+SWAP = [(0, 1), (1, 0)]
 KINDS = 3
 
 
@@ -47,7 +48,7 @@
     return swapped(jnp.broadcast_to(x[None], (n,) + x.shape).reshape(n * x.shape[0], -1), axis)
 
 
-def expert_kernel(nz, nx, tok_hbm, ext_hbm, w_hbm, terms_hbm, part_hbm,
+def expert_kernel(nz, nx, ny, y_ref, own_hbm, left_hbm, right_hbm, fara_hbm, farb_hbm, ext_hbm, w_hbm, terms_hbm, part_hbm,
                   tok, ext, w, terms, part, gu_acc, d_acc, row_sem, w_sem, terms_sem, part_sem):
     features = tok.shape[1]
     chunk = features // nx
@@ -57,11 +58,18 @@
         for z in range(nz):
             for c in range(2):
                 for m in range(KINDS):
-                    yield ((z * nx + x) * 2 + c) * KINDS + m, x * chunk + c * piece, (m * nz + z) * HID
-
-    load_tok = pltpu.make_async_copy(tok_hbm, tok, row_sem.at[0])
-    load_ext = pltpu.make_async_copy(ext_hbm, ext, row_sem.at[1])
-    load_tok.start()
+                    yield ((x * 2 + c) * nz + z) * KINDS + m, x * chunk + c * piece, (m * nz + z) * HID
+
+    block = own_hbm.shape[0]
+    half = fara_hbm.shape[0]
+    load_tok = []
+    for n, (source, ahead, skip) in enumerate(
+        ((own_hbm, 0, 0), (left_hbm, ny - 1, 0), (right_hbm, 1, 0), (fara_hbm, 2, 0), (farb_hbm, 2, half))
+    ):
+        at = pl.multiple_of(lax.rem(y_ref[0] + ahead, ny) * block + skip, half)
+        load_tok.append(pltpu.make_async_copy(source, tok.at[pl.ds(at, source.shape[0]), :], row_sem.at[n]))
+        load_tok[-1].start()
+    load_ext = pltpu.make_async_copy(ext_hbm, ext, row_sem.at[5])
     loads = []
     for x in range(nx):
         if x == 1:
@@ -76,7 +84,8 @@
             copy.start()
             loads[-1].append(copy)
     wide = nz * HID
-    load_tok.wait()
+    for copy in load_tok:
+        copy.wait()
     for x in range(nx):
         for copy in loads[x]:
             copy.wait()
@@ -133,20 +142,21 @@
         copy.wait()
 
 
-def expert_math(tok, ext, w, nz, nx):
-    rows, features = tok.shape
+def expert_math(y, tok, ext, w, nz, nx):
+    rows, features = ext.shape[0], ext.shape[1] - PAD
+    ny = rows // tok[0].shape[0]
     held = w.shape[0]
     wide = nz * HID
     spec = pl.BlockSpec(memory_space=pl.ANY)
     count = nz * nx * 2 * KINDS
     return pl.pallas_call(
-        functools.partial(expert_kernel, nz, nx),
+        functools.partial(expert_kernel, nz, nx, ny),
         name="expert_math",
         out_shape=(
             jax.ShapeDtypeStruct((held, HID), BF16),
             jax.ShapeDtypeStruct((rows, features + PAD), BF16),
         ),
-        in_specs=[spec] * 3,
+        in_specs=[pl.BlockSpec(memory_space=pltpu.SMEM)] + [spec] * (len(tok) + 2),
         out_specs=(spec, spec),
         scratch_shapes=[
             pltpu.VMEM((rows, features), BF16),
@@ -156,7 +166,7 @@
             pltpu.VMEM((rows, features + PAD), BF16),
             pltpu.VMEM((rows, 2 * wide), F32),
             pltpu.VMEM((rows, wide), F32),
-            pltpu.SemaphoreType.DMA((2,)),
+            pltpu.SemaphoreType.DMA((6,)),
             pltpu.SemaphoreType.DMA((count,)),
             pltpu.SemaphoreType.DMA((count,)),
             pltpu.SemaphoreType.DMA((nx,)),
@@ -166,7 +176,7 @@
             transcendentals=rows * wide,
             bytes_accessed=2 * (2 * held * HID + 3 * rows * features),
         ),
-    )(tok, ext, w)
+    )(y, *tok, ext, w)
 
 
 def layer(tokens, grad_out, routes, route_probs, gate_weight, up_weight, down_weight):
@@ -176,7 +186,8 @@
     slots = experts * CAP
 
     stored = jnp.concatenate([gate_weight[0], up_weight[0], down_weight[0]], axis=0)
-    weights = lax.all_gather(stored, HOLD, axis=0, tiled=True)
+    paired = lax.ppermute(stored, "zp", SWAP)
+    weights = lax.all_gather(jnp.concatenate([stored, paired], axis=0), HOLD, axis=0, tiled=True)
 
     ids = jnp.arange(experts, dtype=jnp.int32)
     first, second = routes[:, 0:1] == ids, routes[:, 1:2] == ids
@@ -192,14 +203,21 @@
     send_grd = dot(select, grad_out, ((1,), (0,))).astype(BF16)
     send_grd = jnp.concatenate([send_grd, columns(slot_prob)], axis=1)
 
-    came_tok = swapped(send_tok, "e")
-    came_tok, send_grd = lax.optimization_barrier((came_tok, send_grd))
-    rows_tok = lax.all_gather(came_tok, "y", axis=0, tiled=True)
-    rows_ext = shared(swapped(send_grd, "e"), "y")
-
-    terms, part = expert_math(rows_tok, rows_ext, weights, nz, nx)
+    own = swapped(send_tok, "e")
+    own, send_grd = lax.optimization_barrier((own, send_grd))
+    up, down = [(i, (i + 1) % ny) for i in range(ny)], [(i, (i - 1) % ny) for i in range(ny)]
+    half = slots // 2
+    left, right = lax.ppermute(own, "y", up), lax.ppermute(own, "y", down)
+    far = lax.ppermute(left[:half], "y", up), lax.ppermute(right[half:], "y", down)
+    came_grd = swapped(send_grd, "e")
+    rows_ext = shared(came_grd, "y")
+
+    y = lax.axis_index("y").astype(jnp.int32).reshape(1)
+    terms, part = expert_math(y, (own, left, right) + far, rows_ext, weights, nz, nx)
     sums = lax.psum_scatter(terms, HOLD, scatter_dimension=0, tiled=True)
-    grads = sums.reshape(KINDS, 1, -1, HID)
+    kept, given = jnp.split(sums, 2, axis=0)
+    given = lax.ppermute(given, "zp", SWAP)
+    grads = (kept.astype(F32) + given.astype(F32)).astype(BF16).reshape(KINDS, 1, -1, HID)
 
     back = jnp.sum(swapped(part, "y").astype(F32).reshape(ny, slots, -1), axis=0)
     back_score = columns(joined(back[:, features : features + 2]))

time: 247 us -> 240 us (0.972)
  the two profiles are of different devices: /device:TPU:71 before, /device:TPU:34 now
where the time goes in v3:
time: 240 us
  blocking collectives  94.6 us (39%)
  waiting for transfers between devices  67.9 us (28%)
  starting transfers between devices  36.6 us (15%)
  between operations  14.3 us (6%)
  Pallas kernels  11.7 us (5%)
  local copies, waits for them, and re-layouts  6.79 us (3%)
  other arithmetic  5.34 us (2%)
  matrix products  2.53 us (1%)
    all_to_all x3, blocking collectives, swapped(): return lax.all_to_all(x, axis, 0, 0, tiled=True)  94.6 us
    all_to_all x2, waiting for transfers between devices, swapped(): return lax.all_to_all(x, axis, 0, 0, tiled=True)  24.6 us
    ppermute x2, waiting for transfers between devices, layer(): left, right = (lax.ppermute(own, 'y', up), lax.ppermute(own, 'y', down))  24.4 us
    all_to_all x2, starting transfers between devices, swapped(): return lax.all_to_all(x, axis, 0, 0, tiled=True)  18.4 us
    pallas_call x1, Pallas kernels, expert_math(): pl.pallas_call(functools.partial(expert_kernel, nz, nx, ny), name='expert...  11.7 us
    ppermute x1, waiting for transfers between devices, layer(): paired = lax.ppermute(stored, 'zp', SWAP)  9.67 us
    ppermute x2, starting transfers between devices, layer(): left, right = (lax.ppermute(own, 'y', up), lax.ppermute(own, 'y', down))  7.05 us
    ppermute x1, waiting for transfers between devices, layer(): given = lax.ppermute(given, 'zp', SWAP)  5.66 us
  transfers between devices with their start and end apart: 10, of which 6 were waited for; matrix products, arithmetic and copies ran while one was open for 3% of the time, Pallas kernels for 0%

profile of v3, /device:TPU:34, one launch (start us, length us, event | category | flops | bytes accessed | tf_op | source)
XLA Modules:
  0.0 239.8 jit_solution(4594110478369434093)
XLA Ops:
  7.2 1.0 pad_maximum_fusion.1
  8.3 2.1 collective-permute-start.4
  10.5 9.7 %collective-permute-done.4 = bf16[1344,128]{1,0:T(8,128)(2,1)S(1)} collective-permute-done((bf16[1344,128]{1,0:T(8,128)(2,1)S(1)}, bf16[1344,128]{1,0:T(8,128)(2,1)S(1)}, u32[]{:S(2)}, u32[]{:S(2)}) %collective-permute-start.4) | collective-permute-done | bytes 344096 | tf_op jit(solution)/shard_map/ppermute | solution.py:189
  20.1 1.9 pad_maximum_fusion
  22.3 1.1 fusion
  23.4 14.2 %all-to-all-start = ((bf16[8,8,3584]{2,1,0:T(8,128)(2,1)}), bf16[8,8,3584]{2,1,0:T(8,128)(2,1)S(1)}, u32[]{:S(2)}, u32[]{:S(2)}) async-start(bf16[8,8,3584]{2,1,0:T(8,128)(2,1)} %fusion), calls=%async_computation | async-start | bytes 917504 | tf_op jit(solution)/shard_map/all_to_all | solution.py:43
  38.5 24.6 %all-to-all-done = bf16[8,8,3584]{2,1,0:T(8,128)(2,1)S(1)} async-done(((bf16[8,8,3584]{2,1,0:T(8,128)(2,1)}), bf16[8,8,3584]{2,1,0:T(8,128)(2,1)S(1)}, u32[]{:S(2)}, u32[]{:S(2)}) %all-to-all-start) | async-done | bytes 458784 | tf_op jit(solution)/shard_map/all_to_all | solution.py:43
  63.1 35.8 %all_to_all.47 = bf16[8,8,3712]{2,1,0:T(8,128)(2,1)S(1)} all-to-all(bf16[8,8,3712]{2,1,0:T(8,128)(2,1)S(1)} %bitcast.60), channel_id=1, replica_groups=mesh['e'=8,'zp'=2,'y'=4,'x'=4,'c'=2] {'e'}, dimensions={0} | all-to-all | bytes 950272 | tf_op jit(solution)/shard_map/all_to_all | solution.py:43
  98.9 1.4 broadcast_in_dim.77
  100.3 4.2 %all-to-all-start.2 = ((bf16[4,64,3712]{2,1,0:T(8,128)(2,1)}), bf16[4,64,3712]{2,1,0:T(8,128)(2,1)S(1)}, u32[]{:S(2)}, u32[]{:S(2)}) async-start(bf16[4,64,3712]{2,1,0:T(8,128)(2,1)} %broadcast_in_dim.77), calls=%async_computation.2 | async-start | bytes 3801088 | tf_op jit(solution)/shard_map/all_to_all | solution.py:43
  104.5 3.9 %collective-permute-start = (bf16[64,3584]{1,0:T(8,128)(2,1)S(1)}, bf16[64,3584]{1,0:T(8,128)(2,1)S(1)}, u32[]{:S(2)}, u32[]{:S(2)}) collective-permute-start(bf16[64,3584]{1,0:T(8,128)(2,1)S(1)} %bitcast.61), channel_id=1, source_target_pairs={{0,8},{8,16},{16,24},{24,0},{1,9},{9,17},{17,25},{25,1},{2,10},{10... | collective-permute-start | bytes 1376264 | tf_op jit(solution)/shard_map/ppermute | solution.py:210
  108.4 3.1 %collective-permute-start.1 = (bf16[64,3584]{1,0:T(8,128)(2,1)S(1)}, bf16[64,3584]{1,0:T(8,128)(2,1)S(1)}, u32[]{:S(2)}, u32[]{:S(2)}) collective-permute-start(bf16[64,3584]{1,0:T(8,128)(2,1)S(1)} %bitcast.62), channel_id=1, source_target_pairs={{0,24},{8,0},{16,8},{24,16},{1,25},{9,1},{17,9},{25,17},{2,26},{10... | collective-permute-start | bytes 1376264 | tf_op jit(solution)/shard_map/ppermute | solution.py:210
  111.6 24.4 %collective-permute-done.left_hbm = bf16[64,3584]{1,0:T(8,128)(2,1)S(1)} collective-permute-done((bf16[64,3584]{1,0:T(8,128)(2,1)S(1)}, bf16[64,3584]{1,0:T(8,128)(2,1)S(1)}, u32[]{:S(2)}, u32[]{:S(2)}) %collective-permute-start) | collective-permute-done | bytes 458784 | tf_op jit(solution)/shard_map/ppermute | solution.py:210
  136.0 1.9 collective-permute-start.2
  137.9 5.1 %collective-permute-start.3 = (bf16[32,3584]{1,0:T(8,128)(2,1)S(1)}, bf16[32,3584]{1,0:T(8,128)(2,1)S(1)}, u32[]{:S(2)}, u32[]{:S(2)}) collective-permute-start(bf16[32,3584]{1,0:T(8,128)(2,1)S(1)} %slice.71), channel_id=1, source_target_pairs={{0,24},{8,0},{16,8},{24,16},{1,25},{9,1},{17,9},{25,17},{2,26},{10... | collective-permute-start | bytes 688136 | tf_op jit(solution)/shard_map/ppermute | solution.py:211
  143.1 2.0 collective-permute-done.2.fara_hbm
  145.1 1.5 collective-permute-done.3.farb_hbm
  148.0 11.7 %expert_math.1 = (bf16[21504,128]{1,0:T(8,128)(2,1)}, bf16[256,3712]{1,0:T(8,128)(2,1)}) custom-call(s32[1]{0:T(128)} %bitcast.4.y_ref, bf16[64,3584]{1,0:T(8,128)(2,1)} %bitcast.63, bf16[64,3584]{1,0:T(8,128)(2,1)} %copy-done.5, bf16[64,3584]{1,0:T(8,128)(2,1)} %copy-done.6, bf16[32,3584]{1,0:T(8,128)(2,1)} %copy-done.9, bf16[32,3584]{1,0:T(8,128)(2,1)} %copy-done.10, ...), custom_call_target="tpu_custom_call" | custom-call | flops 3758096384 | bytes 16515072 | tf_op jit(solution)/shard_map/expert_math/pallas_call | solution.py:152
  159.7 1.5 copy-done.2
  161.2 24.1 %all_to_all.48 = bf16[4,64,3712]{2,1,0:T(8,128)(2,1)S(1)} all-to-all(bf16[4,64,3712]{2,1,0:T(8,128)(2,1)S(1)} %bitcast.59), channel_id=1, replica_groups=mesh['e'=8,'zp'=2,'y'=4,'x'=4,'c'=2] {'y'}, dimensions={0} | all-to-all | bytes 3801088 | tf_op jit(solution)/shard_map/all_to_all | solution.py:43
  185.8 34.8 %all_to_all.49 = bf16[8,8,3712]{2,1,0:T(8,128)(2,1)S(1)} all-to-all(bf16[8,8,3712]{2,1,0:T(8,128)(2,1)S(1)} %concatenate.29), channel_id=1, replica_groups=mesh['e'=8,'zp'=2,'y'=4,'x'=4,'c'=2] {'e'}, dimensions={0} | all-to-all | bytes 950272 | tf_op jit(solution)/shard_map/all_to_all | solution.py:43
  222.0 1.9 collective-permute-start.5
  225.5 5.7 %collective-permute-done.5 = bf16[1344,128]{1,0:T(8,128)(2,1)S(1)} collective-permute-done((bf16[1344,128]{1,0:T(8,128)(2,1)S(1)}, bf16[1344,128]{1,0:T(8,128)(2,1)S(1)}, u32[]{:S(2)}, u32[]{:S(2)}) %collective-permute-start.5) | collective-permute-done | bytes 344096 | tf_op jit(solution)/shard_map/ppermute | solution.py:219
  231.1 1.1 add_convert_fusion
  (59 shorter events, 6.8 us)
Async XLA Ops:
  7.2 15.1 %copy-start = (bf16[24,3584]{1,0:T(8,128)(2,1)S(1)}, bf16[24,3584]{1,0:T(8,128)(2,1)}, u32[]{:S(2)}) copy-start(bf16[24,3584]{1,0:T(8,128)(2,1)} %param.7) | copy-start | bytes 516100
  7.2 15.0 %copy-start.7 = (s32[24,2]{0,1:T(2,128)S(1)}, s32[24,2]{0,1:T(2,128)}, u32[]{:S(2)}) copy-start(s32[24,2]{0,1:T(2,128)} %param.9) | copy-start | bytes 580
  7.2 139.4 %all-gather.2.cloned.1.call-start = ((), (), s32[]{:S(2)}) async-start(), calls=%async_computation.6 | async-start | bytes 6193152 | tf_op jit(solution)/shard_map/all_gather | solution.py:190
  8.3 29.3 %copy-start.8 = (f32[24,2]{0,1:T(2,128)S(1)}, f32[24,2]{0,1:T(2,128)}, u32[]{:S(2)}) copy-start(f32[24,2]{0,1:T(2,128)} %param.10) | copy-start | bytes 580
  8.3 29.8 %copy-start.4 = (bf16[24,3584]{1,0:T(8,128)(2,1)S(1)}, bf16[24,3584]{1,0:T(8,128)(2,1)}, u32[]{:S(2)}) copy-start(bf16[24,3584]{1,0:T(8,128)(2,1)} %param.8) | copy-start | bytes 516100
  8.3 11.8 %collective-permute-start.4 = (bf16[1344,128]{1,0:T(8,128)(2,1)S(1)}, bf16[1344,128]{1,0:T(8,128)(2,1)S(1)}, u32[]{:S(2)}, u32[]{:S(2)}) collective-permute-start(bf16[1344,128]{1,0:T(8,128)(2,1)S(1)} %pad_maximum_fusion.1), channel_id=1, source_target_pairs={{0,32},{32,0},{1,33},{33,1},{2,34},{34,2},{3,35},{35,3},{4,36},{36... | collective-permute-start | bytes 1032200 | tf_op jit(solution)/shard_map/ppermute | solution.py:189
  23.4 39.7 %all-to-all-start = ((bf16[8,8,3584]{2,1,0:T(8,128)(2,1)}), bf16[8,8,3584]{2,1,0:T(8,128)(2,1)S(1)}, u32[]{:S(2)}, u32[]{:S(2)}) async-start(bf16[8,8,3584]{2,1,0:T(8,128)(2,1)} %fusion), calls=%async_computation | async-start | bytes 917504 | tf_op jit(solution)/shard_map/all_to_all | solution.py:43
  63.1 45.3 %copy-start.3 = (bf16[8,8,3584]{2,1,0:T(8,128)(2,1)}, bf16[8,8,3584]{2,1,0:T(8,128)(2,1)S(1)}, u32[]{:S(2)}) copy-start(bf16[8,8,3584]{2,1,0:T(8,128)(2,1)S(1)} %all-to-all-done) | copy-start | bytes 1376260
  100.3 46.3 %all-to-all-start.2 = ((bf16[4,64,3712]{2,1,0:T(8,128)(2,1)}), bf16[4,64,3712]{2,1,0:T(8,128)(2,1)S(1)}, u32[]{:S(2)}, u32[]{:S(2)}) async-start(bf16[4,64,3712]{2,1,0:T(8,128)(2,1)} %broadcast_in_dim.77), calls=%async_computation.2 | async-start | bytes 3801088 | tf_op jit(solution)/shard_map/all_to_all | solution.py:43
  104.5 116.5 %reduce-scatter.2.cloned.1.call-start = ((), (), s32[]{:S(2)}) async-start(), calls=%async_computation.7 | async-start | bytes 6193152 | tf_op jit(solution)/shard_map/reduce_scatter | solution.py:217
  104.5 31.4 %collective-permute-start = (bf16[64,3584]{1,0:T(8,128)(2,1)S(1)}, bf16[64,3584]{1,0:T(8,128)(2,1)S(1)}, u32[]{:S(2)}, u32[]{:S(2)}) collective-permute-start(bf16[64,3584]{1,0:T(8,128)(2,1)S(1)} %bitcast.61), channel_id=1, source_target_pairs={{0,8},{8,16},{16,24},{24,0},{1,9},{9,17},{17,25},{25,1},{2,10},{10... | collective-permute-start | bytes 1376264 | tf_op jit(solution)/shard_map/ppermute | solution.py:210
  108.4 29.5 %collective-permute-start.1 = (bf16[64,3584]{1,0:T(8,128)(2,1)S(1)}, bf16[64,3584]{1,0:T(8,128)(2,1)S(1)}, u32[]{:S(2)}, u32[]{:S(2)}) collective-permute-start(bf16[64,3584]{1,0:T(8,128)(2,1)S(1)} %bitcast.62), channel_id=1, source_target_pairs={{0,24},{8,0},{16,8},{24,16},{1,25},{9,1},{17,9},{25,17},{2,26},{10... | collective-permute-start | bytes 1376264 | tf_op jit(solution)/shard_map/ppermute | solution.py:210
  135.9 10.7 %copy-start.5 = (bf16[64,3584]{1,0:T(8,128)(2,1)}, bf16[64,3584]{1,0:T(8,128)(2,1)S(1)}, u32[]{:S(2)}) copy-start(bf16[64,3584]{1,0:T(8,128)(2,1)S(1)} %collective-permute-done.left_hbm) | copy-start | bytes 1376260
  136.0 9.1 %collective-permute-start.2 = (bf16[32,3584]{1,0:T(8,128)(2,1)S(1)}, bf16[32,3584]{1,0:T(8,128)(2,1)S(1)}, u32[]{:S(2)}, u32[]{:S(2)}) collective-permute-start(bf16[32,3584]{1,0:T(8,128)(2,1)S(1)} %slice.70), channel_id=1, source_target_pairs={{0,8},{8,16},{16,24},{24,0},{1,9},{9,17},{17,25},{25,1},{2,10},{10... | collective-permute-start | bytes 688136 | tf_op jit(solution)/shard_map/ppermute | solution.py:211
  137.9 5.2 %copy-start.6 = (bf16[64,3584]{1,0:T(8,128)(2,1)}, bf16[64,3584]{1,0:T(8,128)(2,1)S(1)}, u32[]{:S(2)}) copy-start(bf16[64,3584]{1,0:T(8,128)(2,1)S(1)} %collective-permute-done.1.right_hbm) | copy-start | bytes 1376260
  137.9 8.7 %collective-permute-start.3 = (bf16[32,3584]{1,0:T(8,128)(2,1)S(1)}, bf16[32,3584]{1,0:T(8,128)(2,1)S(1)}, u32[]{:S(2)}, u32[]{:S(2)}) collective-permute-start(bf16[32,3584]{1,0:T(8,128)(2,1)S(1)} %slice.71), channel_id=1, source_target_pairs={{0,24},{8,0},{16,8},{24,16},{1,25},{9,1},{17,9},{25,17},{2,26},{10... | collective-permute-start | bytes 688136 | tf_op jit(solution)/shard_map/ppermute | solution.py:211
  145.1 1.5 copy-start.9
  146.6 0.7 copy-start.10
  146.6 1.4 copy-start.1
  159.7 1.5 copy-start.2
  222.0 9.1 %collective-permute-start.5 = (bf16[1344,128]{1,0:T(8,128)(2,1)S(1)}, bf16[1344,128]{1,0:T(8,128)(2,1)S(1)}, u32[]{:S(2)}, u32[]{:S(2)}) collective-permute-start(bf16[1344,128]{1,0:T(8,128)(2,1)S(1)} %split.9), channel_id=1, source_target_pairs={{0,32},{32,0},{1,33},{33,1},{2,34},{34,2},{3,35},{35,3},{4,36},{36... | collective-permute-start | bytes 1032200 | tf_op jit(solution)/shard_map/ppermute | solution.py:219
Sparse Core Ops, SparseCore 0:
  22.2 48.3 all-gather.1
  159.8 40.8 reduce-scatter.1

commit v4 on v3

--- a/solution.py
+++ b/solution.py
@@ -48,61 +48,91 @@
     return swapped(jnp.broadcast_to(x[None], (n,) + x.shape).reshape(n * x.shape[0], -1), axis)
 
 
-def expert_kernel(nz, nx, ny, y_ref, own_hbm, left_hbm, right_hbm, fara_hbm, farb_hbm, ext_hbm, w_hbm, terms_hbm, part_hbm,
-                  tok, ext, w, terms, part, gu_acc, d_acc, row_sem, w_sem, terms_sem, part_sem):
+def pieces(nz, nx, x, features):
+    chunk = features // nx
+    piece = chunk // 2
+    for c in range(2):
+        for z in range(nz):
+            for m in range(KINDS):
+                yield m, ((x * 2 + c) * nz + z) * KINDS + m, x * chunk + c * piece, (m * nz + z) * HID
+
+
+def load_weights(nz, nx, features, w_hbm, w, sem, kinds):
+    piece = features // nx // 2
+    loads = []
+    for x in range(nx):
+        loads.append([])
+        for m, i, row, col in pieces(nz, nx, x, features):
+            if m in kinds:
+                copy = pltpu.make_async_copy(
+                    w_hbm.at[pl.ds(i * piece, piece), :],
+                    w.at[pl.ds(row, piece), pl.ds(col, HID)],
+                    sem.at[i],
+                )
+                copy.start()
+                loads[-1].append(copy)
+    return loads
+
+
+def load_rows(ny, y_ref, sources, rows, sem):
+    own = sources[0]
+    block, half = own.shape[0], sources[3].shape[0]
+    loads = []
+    for n, (ahead, skip) in enumerate(((0, 0), (ny - 1, 0), (1, 0), (2, 0), (2, half))):
+        at = pl.multiple_of(lax.rem(y_ref[0] + ahead, ny) * block + skip, half)
+        source = sources[n]
+        loads.append(pltpu.make_async_copy(source, rows.at[pl.ds(at, source.shape[0]), :], sem.at[n]))
+        loads[-1].start()
+    return loads
+
+
+def pre_kernel(nz, nx, ny, y_ref, s0, s1, s2, s3, s4, w_hbm, gu_ref, tok, w, row_sem, w_sem):
+    features = tok.shape[1]
+    chunk = features // nx
+    rows = load_rows(ny, y_ref, (s0, s1, s2, s3, s4), tok, row_sem)
+    loads = load_weights(nz, nx, features, w_hbm, w, w_sem, (0, 1))
+    for copy in rows:
+        copy.wait()
+    for x in range(nx):
+        for copy in loads[x]:
+            copy.wait()
+        span = slice(x * chunk, (x + 1) * chunk)
+        gu = dot(tok[:, span], w[span, :], ((1,), (0,)))
+        if x == 0:
+            gu_ref[...] = gu
+        else:
+            gu_ref[...] += gu
+
+
+def expert_kernel(nz, nx, ny, y_ref, s0, s1, s2, s3, s4, low_hbm, high_hbm, w_hbm, gu_ref, terms_hbm, part_hbm,
+                  tok, ext, w, terms, part, d_acc, row_sem, w_sem, terms_sem, part_sem):
     features = tok.shape[1]
     chunk = features // nx
     piece = chunk // 2
-
-    def pieces(x):
-        for z in range(nz):
-            for c in range(2):
-                for m in range(KINDS):
-                    yield ((x * 2 + c) * nz + z) * KINDS + m, x * chunk + c * piece, (m * nz + z) * HID
-
-    block = own_hbm.shape[0]
-    half = fara_hbm.shape[0]
-    load_tok = []
-    for n, (source, ahead, skip) in enumerate(
-        ((own_hbm, 0, 0), (left_hbm, ny - 1, 0), (right_hbm, 1, 0), (fara_hbm, 2, 0), (farb_hbm, 2, half))
-    ):
-        at = pl.multiple_of(lax.rem(y_ref[0] + ahead, ny) * block + skip, half)
-        load_tok.append(pltpu.make_async_copy(source, tok.at[pl.ds(at, source.shape[0]), :], row_sem.at[n]))
-        load_tok[-1].start()
-    load_ext = pltpu.make_async_copy(ext_hbm, ext, row_sem.at[5])
-    loads = []
-    for x in range(nx):
-        if x == 1:
-            load_ext.start()
-        loads.append([])
-        for i, row, col in pieces(x):
-            copy = pltpu.make_async_copy(
-                w_hbm.at[pl.ds(i * piece, piece), :],
-                w.at[pl.ds(row, piece), pl.ds(col, HID)],
-                w_sem.at[i],
-            )
-            copy.start()
-            loads[-1].append(copy)
+    cut = low_hbm.shape[1]
     wide = nz * HID
-    for copy in load_tok:
-        copy.wait()
-    for x in range(nx):
-        for copy in loads[x]:
+    load_low = pltpu.make_async_copy(low_hbm, ext.at[:, pl.ds(0, cut)], row_sem.at[5])
+    load_high = pltpu.make_async_copy(high_hbm, ext.at[:, pl.ds(cut, high_hbm.shape[1])], row_sem.at[6])
+    load_low.start()
+    loads_d = load_weights(nz, nx, features, w_hbm, w, w_sem, (2,))
+    load_high.start()
+    rows = load_rows(ny, y_ref, (s0, s1, s2, s3, s4), tok, row_sem)
+    loads = load_weights(nz, nx, features, w_hbm, w, w_sem, (0, 1))
+    load_low.wait()
+    for x in range(nx):
+        if x * 2 == nx:
+            load_high.wait()
+        for copy in loads_d[x]:
             copy.wait()
-        if x == 0:
-            load_ext.wait()
         span = slice(x * chunk, (x + 1) * chunk)
-        gu = dot(tok[:, span], w[span, : 2 * wide], ((1,), (0,)))
         dg = dot(ext[:, span], w[span, 2 * wide :], ((1,), (0,)))
         if x == 0:
-            gu_acc[...] = gu
             d_acc[...] = dg
         else:
-            gu_acc[...] += gu
             d_acc[...] += dg
     extra = ext[:, features:].astype(F32)
     prob = extra[:, 0:1] + extra[:, 1:2]
-    gate_pre, up_pre = gu_acc[:, :wide], gu_acc[:, wide:]
+    gate_pre, up_pre = gu_ref[:, :wide], gu_ref[:, wide:]
     down_grad = d_acc[...]
     sig = jax.nn.sigmoid(gate_pre)
     act = gate_pre * sig
@@ -112,13 +142,15 @@
     gate_grad = (hidden_grad * up_pre * sig * (1.0 + gate_pre * (1.0 - sig))).astype(BF16)
     up_grad = (hidden_grad * act).astype(BF16)
     gu_grad = jnp.concatenate([gate_grad, up_grad], axis=1)
+    for copy in rows:
+        copy.wait()
     stores = []
     for x in range(nx):
         span = slice(x * chunk, (x + 1) * chunk)
         terms[span, : 2 * wide] = dot(tok[:, span], gu_grad, ((0,), (0,))).astype(BF16)
         scaled = (prob * ext[:, span].astype(F32)).astype(BF16)
         terms[span, 2 * wide :] = dot(scaled, hidden, ((0,), (0,))).astype(BF16)
-        for i, row, col in pieces(x):
+        for m, i, row, col in pieces(nz, nx, x, features):
             copy = pltpu.make_async_copy(
                 terms.at[pl.ds(row, piece), pl.ds(col, HID)],
                 terms_hbm.at[pl.ds(i * piece, piece), :],
@@ -131,6 +163,8 @@
     low = scores - high
     part[:, features:] = jnp.where(lane == 0, high, jnp.where(lane == 1, low, 0.0)).astype(BF16)
     for x in range(nx):
+        for copy in loads[x]:
+            copy.wait()
         span = slice(x * chunk, (x + 1) * chunk)
         part[:, span] = dot(gu_grad, w[span, : 2 * wide], ((1,), (1,))).astype(BF16)
         if x == nx - 1:
@@ -142,41 +176,67 @@
         copy.wait()
 
 
-def expert_math(y, tok, ext, w, nz, nx):
-    rows, features = ext.shape[0], ext.shape[1] - PAD
-    ny = rows // tok[0].shape[0]
+ANYWHERE = pl.BlockSpec(memory_space=pl.ANY)
+SCALAR = pl.BlockSpec(memory_space=pltpu.SMEM)
+INSIDE = pl.BlockSpec(memory_space=pltpu.VMEM)
+
+
+def pre_math(y, tok, w, rows, nz, nx):
+    features = tok[0].shape[1]
+    wide = nz * HID
+    count = nz * nx * 2 * KINDS
+    return pl.pallas_call(
+        functools.partial(pre_kernel, nz, nx, rows // tok[0].shape[0]),
+        name="pre_math",
+        out_shape=jax.ShapeDtypeStruct((rows, 2 * wide), F32),
+        in_specs=[SCALAR] + [ANYWHERE] * (len(tok) + 1),
+        out_specs=INSIDE,
+        scratch_shapes=[
+            pltpu.VMEM((rows, features), BF16),
+            pltpu.VMEM((features, 2 * wide), BF16),
+            pltpu.SemaphoreType.DMA((5,)),
+            pltpu.SemaphoreType.DMA((count,)),
+        ],
+        cost_estimate=pl.CostEstimate(
+            flops=4 * rows * features * wide,
+            transcendentals=0,
+            bytes_accessed=2 * features * (2 * wide + rows),
+        ),
+    )(y, *tok, w)
+
+
+def expert_math(y, tok, low, high, w, gu, nz, nx):
+    rows, features = low.shape[0], tok[0].shape[1]
     held = w.shape[0]
     wide = nz * HID
-    spec = pl.BlockSpec(memory_space=pl.ANY)
     count = nz * nx * 2 * KINDS
     return pl.pallas_call(
-        functools.partial(expert_kernel, nz, nx, ny),
+        functools.partial(expert_kernel, nz, nx, rows // tok[0].shape[0]),
         name="expert_math",
         out_shape=(
             jax.ShapeDtypeStruct((held, HID), BF16),
             jax.ShapeDtypeStruct((rows, features + PAD), BF16),
         ),
-        in_specs=[pl.BlockSpec(memory_space=pltpu.SMEM)] + [spec] * (len(tok) + 2),
-        out_specs=(spec, spec),
+        in_specs=[SCALAR] + [ANYWHERE] * (len(tok) + 3) + [INSIDE],
+        out_specs=(ANYWHERE, ANYWHERE),
         scratch_shapes=[
             pltpu.VMEM((rows, features), BF16),
             pltpu.VMEM((rows, features + PAD), BF16),
             pltpu.VMEM((features, KINDS * wide), BF16),
             pltpu.VMEM((features, KINDS * wide), BF16),
             pltpu.VMEM((rows, features + PAD), BF16),
-            pltpu.VMEM((rows, 2 * wide), F32),
             pltpu.VMEM((rows, wide), F32),
-            pltpu.SemaphoreType.DMA((6,)),
+            pltpu.SemaphoreType.DMA((7,)),
             pltpu.SemaphoreType.DMA((count,)),
             pltpu.SemaphoreType.DMA((count,)),
             pltpu.SemaphoreType.DMA((nx,)),
         ],
         cost_estimate=pl.CostEstimate(
-            flops=16 * rows * features * wide,
+            flops=12 * rows * features * wide,
             transcendentals=rows * wide,
             bytes_accessed=2 * (2 * held * HID + 3 * rows * features),
         ),
-    )(y, *tok, ext, w)
+    )(y, *tok, low, high, w, gu)
 
 
 def layer(tokens, grad_out, routes, route_probs, gate_weight, up_weight, down_weight):
@@ -208,12 +268,17 @@
     up, down = [(i, (i + 1) % ny) for i in range(ny)], [(i, (i - 1) % ny) for i in range(ny)]
     half = slots // 2
     left, right = lax.ppermute(own, "y", up), lax.ppermute(own, "y", down)
-    far = lax.ppermute(left[:half], "y", up), lax.ppermute(right[half:], "y", down)
+    halves = left[:half], right[half:]
+    far = lax.ppermute(halves[0], "y", up), lax.ppermute(halves[1], "y", down)
     came_grd = swapped(send_grd, "e")
-    rows_ext = shared(came_grd, "y")
+    cut = features * 3 // 7
+    rows_high = lax.all_gather(came_grd[:, cut:], "y", axis=0, tiled=True)
+    rows_low = shared(came_grd[:, :cut], "y")
 
     y = lax.axis_index("y").astype(jnp.int32).reshape(1)
-    terms, part = expert_math(y, (own, left, right) + far, rows_ext, weights, nz, nx)
+    tok = (own, left, right) + far
+    gate_up = pre_math(y, tok, weights, ny * slots, nz, nx)
+    terms, part = expert_math(y, tok, rows_low, rows_high, weights, gate_up, nz, nx)
     sums = lax.psum_scatter(terms, HOLD, scatter_dimension=0, tiled=True)
     kept, given = jnp.split(sums, 2, axis=0)
     given = lax.ppermute(given, "zp", SWAP)

time: 240 us -> 233 us (0.971)
  the two profiles are of different devices: /device:TPU:34 before, /device:TPU:32 now
where the time goes in v4:
time: 233 us; the launch traced here: 232 us
  blocking collectives  93.2 us (40%)
  waiting for transfers between devices  50.6 us (22%)
  starting transfers between devices  43.7 us (19%)
  Pallas kernels  16.3 us (7%)
  between operations  14 us (6%)
  local copies, waits for them, and re-layouts  7.36 us (3%)
  other arithmetic  4.41 us (2%)
  matrix products  2.56 us (1%)
    all_to_all x3, blocking collectives, swapped(): return lax.all_to_all(x, axis, 0, 0, tiled=True)  93.2 us
    all_to_all x2, waiting for transfers between devices, swapped(): return lax.all_to_all(x, axis, 0, 0, tiled=True)  24.3 us
    all_to_all x2, starting transfers between devices, swapped(): return lax.all_to_all(x, axis, 0, 0, tiled=True)  16.8 us
    pallas_call x1, Pallas kernels, expert_math(): pl.pallas_call(functools.partial(expert_kernel, nz, nx, rows // tok[0].sh...  11 us
    ppermute x2, starting transfers between devices, layer(): far = (lax.ppermute(halves[0], 'y', up), lax.ppermute(halves[1], 'y', down))  10.5 us
    ppermute x2, waiting for transfers between devices, layer(): left, right = (lax.ppermute(own, 'y', up), lax.ppermute(own, 'y', down))  10.4 us
    ppermute x1, starting transfers between devices, layer(): paired = lax.ppermute(stored, 'zp', SWAP)  7.36 us
    ppermute x2, starting transfers between devices, layer(): left, right = (lax.ppermute(own, 'y', up), lax.ppermute(own, 'y', down))  7.05 us
  transfers between devices with their start and end apart: 11, of which 7 were waited for; matrix products, arithmetic and copies ran while one was open for 3% of the time, Pallas kernels for 2%

profile of v4, /device:TPU:32, one launch (start us, length us, event | category | flops | bytes accessed | tf_op | source)
XLA Modules:
  0.0 232.2 jit_solution(8174927533382761372)
XLA Ops:
  7.2 1.1 pad_maximum_fusion.1
  8.3 7.4 %collective-permute-start.4 = (bf16[1344,128]{1,0:T(8,128)(2,1)S(1)}, bf16[1344,128]{1,0:T(8,128)(2,1)S(1)}, u32[]{:S(2)}, u32[]{:S(2)}) collective-permute-start(bf16[1344,128]{1,0:T(8,128)(2,1)S(1)} %pad_maximum_fusion.1), channel_id=1, source_target_pairs={{0,32},{32,0},{1,33},{33,1},{2,34},{34,2},{3,35},{35,3},{4,36},{36... | collective-permute-start | bytes 1032200 | tf_op jit(solution)/shard_map/ppermute | solution.py:249
  15.7 5.2 %collective-permute-done.4 = bf16[1344,128]{1,0:T(8,128)(2,1)S(1)} collective-permute-done((bf16[1344,128]{1,0:T(8,128)(2,1)S(1)}, bf16[1344,128]{1,0:T(8,128)(2,1)S(1)}, u32[]{:S(2)}, u32[]{:S(2)}) %collective-permute-start.4) | collective-permute-done | bytes 344096 | tf_op jit(solution)/shard_map/ppermute | solution.py:249
  20.9 1.9 pad_maximum_fusion
  23.1 1.1 fusion
  24.2 13.3 %all-to-all-start = ((bf16[8,8,3584]{2,1,0:T(8,128)(2,1)}), bf16[8,8,3584]{2,1,0:T(8,128)(2,1)S(1)}, u32[]{:S(2)}, u32[]{:S(2)}) async-start(bf16[8,8,3584]{2,1,0:T(8,128)(2,1)} %fusion), calls=%async_computation | async-start | bytes 917504 | tf_op jit(solution)/shard_map/all_to_all | solution.py:43
  38.5 24.3 %all-to-all-done = bf16[8,8,3584]{2,1,0:T(8,128)(2,1)S(1)} async-done(((bf16[8,8,3584]{2,1,0:T(8,128)(2,1)}), bf16[8,8,3584]{2,1,0:T(8,128)(2,1)S(1)}, u32[]{:S(2)}, u32[]{:S(2)}) %all-to-all-start) | async-done | bytes 458784 | tf_op jit(solution)/shard_map/all_to_all | solution.py:43
  62.8 36.3 %all_to_all.50 = bf16[8,8,3712]{2,1,0:T(8,128)(2,1)S(1)} all-to-all(bf16[8,8,3712]{2,1,0:T(8,128)(2,1)S(1)} %bitcast.60), channel_id=1, replica_groups=mesh['e'=8,'zp'=2,'y'=4,'x'=4,'c'=2] {'e'}, dimensions={0} | all-to-all | bytes 950272 | tf_op jit(solution)/shard_map/all_to_all | solution.py:43
  99.8 3.5 %collective-permute-start = (bf16[64,3584]{1,0:T(8,128)(2,1)S(1)}, bf16[64,3584]{1,0:T(8,128)(2,1)S(1)}, u32[]{:S(2)}, u32[]{:S(2)}) collective-permute-start(bf16[64,3584]{1,0:T(8,128)(2,1)S(1)} %bitcast.61), channel_id=1, source_target_pairs={{0,8},{8,16},{16,24},{24,0},{1,9},{9,17},{17,25},{25,1},{2,10},{10... | collective-permute-start | bytes 1376264 | tf_op jit(solution)/shard_map/ppermute | solution.py:270
  103.3 3.5 %collective-permute-start.1 = (bf16[64,3584]{1,0:T(8,128)(2,1)S(1)}, bf16[64,3584]{1,0:T(8,128)(2,1)S(1)}, u32[]{:S(2)}, u32[]{:S(2)}) collective-permute-start(bf16[64,3584]{1,0:T(8,128)(2,1)S(1)} %bitcast.62), channel_id=1, source_target_pairs={{0,24},{8,0},{16,8},{24,16},{1,25},{9,1},{17,9},{25,17},{2,26},{10... | collective-permute-start | bytes 1376264 | tf_op jit(solution)/shard_map/ppermute | solution.py:270
  107.8 3.5 %all-to-all-start.2 = ((bf16[4,64,1536]{2,1,0:T(8,128)(2,1)}), bf16[4,64,1536]{2,1,0:T(8,128)(2,1)S(1)}, u32[]{:S(2)}, u32[]{:S(2)}) async-start(bf16[4,64,1536]{2,1,0:T(8,128)(2,1)} %broadcast_in_dim.74), calls=%async_computation.2 | async-start | bytes 1572864 | tf_op jit(solution)/shard_map/all_to_all | solution.py:43
  111.4 2.7 %collective-permute-done.s1 = bf16[64,3584]{1,0:T(8,128)(2,1)S(1)} collective-permute-done((bf16[64,3584]{1,0:T(8,128)(2,1)S(1)}, bf16[64,3584]{1,0:T(8,128)(2,1)S(1)}, u32[]{:S(2)}, u32[]{:S(2)}) %collective-permute-start) | collective-permute-done | bytes 458784 | tf_op jit(solution)/shard_map/ppermute | solution.py:270
  114.1 4.4 %collective-permute-start.2 = (bf16[32,3584]{1,0:T(8,128)(2,1)S(1)}, bf16[32,3584]{1,0:T(8,128)(2,1)S(1)}, u32[]{:S(2)}, u32[]{:S(2)}) collective-permute-start(bf16[32,3584]{1,0:T(8,128)(2,1)S(1)} %slice.78), channel_id=1, source_target_pairs={{0,8},{8,16},{16,24},{24,0},{1,9},{9,17},{17,25},{25,1},{2,10},{10... | collective-permute-start | bytes 688136 | tf_op jit(solution)/shard_map/ppermute | solution.py:272
  118.5 7.7 %collective-permute-done.1.s2 = bf16[64,3584]{1,0:T(8,128)(2,1)S(1)} collective-permute-done((bf16[64,3584]{1,0:T(8,128)(2,1)S(1)}, bf16[64,3584]{1,0:T(8,128)(2,1)S(1)}, u32[]{:S(2)}, u32[]{:S(2)}) %collective-permute-start.1) | collective-permute-done | bytes 458784 | tf_op jit(solution)/shard_map/ppermute | solution.py:270
  126.2 6.1 %collective-permute-start.3 = (bf16[32,3584]{1,0:T(8,128)(2,1)S(1)}, bf16[32,3584]{1,0:T(8,128)(2,1)S(1)}, u32[]{:S(2)}, u32[]{:S(2)}) collective-permute-start(bf16[32,3584]{1,0:T(8,128)(2,1)S(1)} %slice.79), channel_id=1, source_target_pairs={{0,24},{8,0},{16,8},{24,16},{1,25},{9,1},{17,9},{25,17},{2,26},{10... | collective-permute-start | bytes 688136 | tf_op jit(solution)/shard_map/ppermute | solution.py:272
  132.3 3.1 %collective-permute-done.2.s3 = bf16[32,3584]{1,0:T(8,128)(2,1)S(1)} collective-permute-done((bf16[32,3584]{1,0:T(8,128)(2,1)S(1)}, bf16[32,3584]{1,0:T(8,128)(2,1)S(1)}, u32[]{:S(2)}, u32[]{:S(2)}) %collective-permute-start.2) | collective-permute-done | bytes 229408 | tf_op jit(solution)/shard_map/ppermute | solution.py:272
  135.4 1.8 collective-permute-done.3.s4
  137.9 5.3 %pre_math.1.gu_ref = f32[256,512]{1,0:T(8,128)} custom-call(s32[1]{0:T(128)} %bitcast.4.y_ref, bf16[64,3584]{1,0:T(8,128)(2,1)} %bitcast.63, bf16[64,3584]{1,0:T(8,128)(2,1)} %copy-done.3, bf16[64,3584]{1,0:T(8,128)(2,1)} %copy-done.4, bf16[32,3584]{1,0:T(8,128)(2,1)} %copy-done.7, bf16[32,3584]{1,0:T(8,128)(2,1)} %copy-done.8, ...), custom_call_target="tpu_custom_call" | custom-call | flops 939524096 | bytes 5505024 | tf_op jit(solution)/shard_map/pre_math/pallas_call | solution.py:188
  144.2 11.0 %expert_math.1 = (bf16[21504,128]{1,0:T(8,128)(2,1)}, bf16[256,3712]{1,0:T(8,128)(2,1)}) custom-call(s32[1]{0:T(128)} %bitcast.4.y_ref, bf16[64,3584]{1,0:T(8,128)(2,1)} %bitcast.64, bf16[64,3584]{1,0:T(8,128)(2,1)} %copy-done.3, bf16[64,3584]{1,0:T(8,128)(2,1)} %copy-done.4, bf16[32,3584]{1,0:T(8,128)(2,1)} %copy-done.7, bf16[32,3584]{1,0:T(8,128)(2,1)} %copy-done.8, ...), custom_call_target="tpu_custom_call" | custom-call | flops 2818572288 | bytes 16515072 | tf_op jit(solution)/shard_map/expert_math/pallas_call | solution.py:213
  155.2 1.5 copy-done.1
  156.7 25.1 %all_to_all.51 = bf16[4,64,3712]{2,1,0:T(8,128)(2,1)S(1)} all-to-all(bf16[4,64,3712]{2,1,0:T(8,128)(2,1)S(1)} %bitcast.57), channel_id=1, replica_groups=mesh['e'=8,'zp'=2,'y'=4,'x'=4,'c'=2] {'y'}, dimensions={0} | all-to-all | bytes 3801088 | tf_op jit(solution)/shard_map/all_to_all | solution.py:43
  182.4 31.8 %all_to_all.52 = bf16[8,8,3712]{2,1,0:T(8,128)(2,1)S(1)} all-to-all(bf16[8,8,3712]{2,1,0:T(8,128)(2,1)S(1)} %concatenate.29), channel_id=1, replica_groups=mesh['e'=8,'zp'=2,'y'=4,'x'=4,'c'=2] {'e'}, dimensions={0} | all-to-all | bytes 950272 | tf_op jit(solution)/shard_map/all_to_all | solution.py:43
  215.7 1.9 collective-permute-start.5
  219.2 5.7 %collective-permute-done.5 = bf16[1344,128]{1,0:T(8,128)(2,1)S(1)} collective-permute-done((bf16[1344,128]{1,0:T(8,128)(2,1)S(1)}, bf16[1344,128]{1,0:T(8,128)(2,1)S(1)}, u32[]{:S(2)}, u32[]{:S(2)}) %collective-permute-start.5) | collective-permute-done | bytes 344096 | tf_op jit(solution)/shard_map/ppermute | solution.py:284
  (67 shorter events, 8.9 us)
Async XLA Ops:
  7.2 15.9 %copy-start = (bf16[24,3584]{1,0:T(8,128)(2,1)S(1)}, bf16[24,3584]{1,0:T(8,128)(2,1)}, u32[]{:S(2)}) copy-start(bf16[24,3584]{1,0:T(8,128)(2,1)} %param.7) | copy-start | bytes 516100
  7.2 130.1 %all-gather.5.cloned.1.call-start = ((), (), s32[]{:S(2)}) async-start(), calls=%async_computation.7 | async-start | bytes 6193152 | tf_op jit(solution)/shard_map/all_gather | solution.py:250
  7.2 15.7 %copy-start.10 = (s32[24,2]{0,1:T(2,128)S(1)}, s32[24,2]{0,1:T(2,128)}, u32[]{:S(2)}) copy-start(s32[24,2]{0,1:T(2,128)} %param.9) | copy-start | bytes 580
  8.3 12.6 %collective-permute-start.4 = (bf16[1344,128]{1,0:T(8,128)(2,1)S(1)}, bf16[1344,128]{1,0:T(8,128)(2,1)S(1)}, u32[]{:S(2)}, u32[]{:S(2)}) collective-permute-start(bf16[1344,128]{1,0:T(8,128)(2,1)S(1)} %pad_maximum_fusion.1), channel_id=1, source_target_pairs={{0,32},{32,0},{1,33},{33,1},{2,34},{34,2},{3,35},{35,3},{4,36},{36... | collective-permute-start | bytes 1032200 | tf_op jit(solution)/shard_map/ppermute | solution.py:249
  22.8 14.7 %copy-start.11 = (f32[24,2]{0,1:T(2,128)S(1)}, f32[24,2]{0,1:T(2,128)}, u32[]{:S(2)}) copy-start(f32[24,2]{0,1:T(2,128)} %param.10) | copy-start | bytes 580
  22.8 15.2 %copy-start.9 = (bf16[24,3584]{1,0:T(8,128)(2,1)S(1)}, bf16[24,3584]{1,0:T(8,128)(2,1)}, u32[]{:S(2)}) copy-start(bf16[24,3584]{1,0:T(8,128)(2,1)} %param.8) | copy-start | bytes 516100
  24.2 38.6 %all-to-all-start = ((bf16[8,8,3584]{2,1,0:T(8,128)(2,1)}), bf16[8,8,3584]{2,1,0:T(8,128)(2,1)S(1)}, u32[]{:S(2)}, u32[]{:S(2)}) async-start(bf16[8,8,3584]{2,1,0:T(8,128)(2,1)} %fusion), calls=%async_computation | async-start | bytes 917504 | tf_op jit(solution)/shard_map/all_to_all | solution.py:43
  37.5 105.8 %all-gather.3.cloned.1.call-start = ((), (), s32[]{:S(2)}) async-start(), calls=%async_computation.6 | async-start | bytes 1392640 | tf_op jit(solution)/shard_map/all_gather | solution.py:275
  62.8 45.1 %copy-start.2 = (bf16[8,8,3584]{2,1,0:T(8,128)(2,1)}, bf16[8,8,3584]{2,1,0:T(8,128)(2,1)S(1)}, u32[]{:S(2)}) copy-start(bf16[8,8,3584]{2,1,0:T(8,128)(2,1)S(1)} %all-to-all-done) | copy-start | bytes 1376260
  99.8 14.3 %collective-permute-start = (bf16[64,3584]{1,0:T(8,128)(2,1)S(1)}, bf16[64,3584]{1,0:T(8,128)(2,1)S(1)}, u32[]{:S(2)}, u32[]{:S(2)}) collective-permute-start(bf16[64,3584]{1,0:T(8,128)(2,1)S(1)} %bitcast.61), channel_id=1, source_target_pairs={{0,8},{8,16},{16,24},{24,0},{1,9},{9,17},{17,25},{25,1},{2,10},{10... | collective-permute-start | bytes 1376264 | tf_op jit(solution)/shard_map/ppermute | solution.py:270
  103.3 22.9 %collective-permute-start.1 = (bf16[64,3584]{1,0:T(8,128)(2,1)S(1)}, bf16[64,3584]{1,0:T(8,128)(2,1)S(1)}, u32[]{:S(2)}, u32[]{:S(2)}) collective-permute-start(bf16[64,3584]{1,0:T(8,128)(2,1)S(1)} %bitcast.62), channel_id=1, source_target_pairs={{0,24},{8,0},{16,8},{24,16},{1,25},{9,1},{17,9},{25,17},{2,26},{10... | collective-permute-start | bytes 1376264 | tf_op jit(solution)/shard_map/ppermute | solution.py:270
  107.8 35.4 %all-to-all-start.2 = ((bf16[4,64,1536]{2,1,0:T(8,128)(2,1)}), bf16[4,64,1536]{2,1,0:T(8,128)(2,1)S(1)}, u32[]{:S(2)}, u32[]{:S(2)}) async-start(bf16[4,64,1536]{2,1,0:T(8,128)(2,1)} %broadcast_in_dim.74), calls=%async_computation.2 | async-start | bytes 1572864 | tf_op jit(solution)/shard_map/all_to_all | solution.py:43
  111.3 103.3 %reduce-scatter.2.cloned.1.call-start = ((), (), s32[]{:S(2)}) async-start(), calls=%async_computation.8 | async-start | bytes 6193152 | tf_op jit(solution)/shard_map/reduce_scatter | solution.py:282
  114.1 23.2 %copy-start.3 = (bf16[64,3584]{1,0:T(8,128)(2,1)}, bf16[64,3584]{1,0:T(8,128)(2,1)S(1)}, u32[]{:S(2)}) copy-start(bf16[64,3584]{1,0:T(8,128)(2,1)S(1)} %collective-permute-done.s1) | copy-start | bytes 1376260
  114.1 21.3 %collective-permute-start.2 = (bf16[32,3584]{1,0:T(8,128)(2,1)S(1)}, bf16[32,3584]{1,0:T(8,128)(2,1)S(1)}, u32[]{:S(2)}, u32[]{:S(2)}) collective-permute-start(bf16[32,3584]{1,0:T(8,128)(2,1)S(1)} %slice.78), channel_id=1, source_target_pairs={{0,8},{8,16},{16,24},{24,0},{1,9},{9,17},{17,25},{25,1},{2,10},{10... | collective-permute-start | bytes 688136 | tf_op jit(solution)/shard_map/ppermute | solution.py:272
  126.2 11.1 %copy-start.4 = (bf16[64,3584]{1,0:T(8,128)(2,1)}, bf16[64,3584]{1,0:T(8,128)(2,1)S(1)}, u32[]{:S(2)}) copy-start(bf16[64,3584]{1,0:T(8,128)(2,1)S(1)} %collective-permute-done.1.s2) | copy-start | bytes 1376260
  126.2 11.0 %collective-permute-start.3 = (bf16[32,3584]{1,0:T(8,128)(2,1)S(1)}, bf16[32,3584]{1,0:T(8,128)(2,1)S(1)}, u32[]{:S(2)}, u32[]{:S(2)}) collective-permute-start(bf16[32,3584]{1,0:T(8,128)(2,1)S(1)} %slice.79), channel_id=1, source_target_pairs={{0,24},{8,0},{16,8},{24,16},{1,25},{9,1},{17,9},{25,17},{2,26},{10... | collective-permute-start | bytes 688136 | tf_op jit(solution)/shard_map/ppermute | solution.py:272
  135.4 1.8 copy-start.7
  137.2 0.7 copy-start.8
  143.2 0.9 copy-start.5
  155.2 1.5 copy-start.1
  214.6 10.2 %copy-start.6 = (bf16[2688,128]{1,0:T(8,128)(2,1)S(1)}, bf16[2688,128]{1,0:T(8,128)(2,1)}, u32[]{:S(2)}) copy-start(bf16[2688,128]{1,0:T(8,128)(2,1)} %reduce-scatter.2.cloned.1.call-done) | copy-start | bytes 2064388
  215.7 9.1 %collective-permute-start.5 = (bf16[1344,128]{1,0:T(8,128)(2,1)S(1)}, bf16[1344,128]{1,0:T(8,128)(2,1)S(1)}, u32[]{:S(2)}, u32[]{:S(2)}) collective-permute-start(bf16[1344,128]{1,0:T(8,128)(2,1)S(1)} %split.9), channel_id=1, source_target_pairs={{0,32},{32,0},{1,33},{33,1},{2,34},{34,2},{3,35},{35,3},{4,36},{36... | collective-permute-start | bytes 1032200 | tf_op jit(solution)/shard_map/ppermute | solution.py:284
Sparse Core Ops, SparseCore 0:
  23.0 48.3 all-gather.4
  99.9 35.0 all-gather.2
  155.3 43.3 reduce-scatter.1

commit v5 on v4

--- a/solution.py
+++ b/solution.py
@@ -104,24 +104,37 @@
             gu_ref[...] += gu
 
 
-def expert_kernel(nz, nx, ny, y_ref, s0, s1, s2, s3, s4, low_hbm, high_hbm, w_hbm, gu_ref, terms_hbm, part_hbm,
-                  tok, ext, w, terms, part, d_acc, row_sem, w_sem, terms_sem, part_sem):
-    features = tok.shape[1]
+def load_halves(low_hbm, high_hbm, ext, sem):
+    cut = low_hbm.shape[1]
+    loads = [
+        pltpu.make_async_copy(low_hbm, ext.at[:, pl.ds(0, cut)], sem.at[5]),
+        pltpu.make_async_copy(high_hbm, ext.at[:, pl.ds(cut, high_hbm.shape[1])], sem.at[6]),
+    ]
+    for copy in loads:
+        copy.start()
+    return loads
+
+
+def prob_of(ext, features):
+    extra = ext[:, features:].astype(F32)
+    return extra[:, 0:1] + extra[:, 1:2]
+
+
+def expert_kernel(nz, nx, low_hbm, high_hbm, w_hbm, gu_ref, part_hbm, grad_ref, hidden_ref,
+                  ext, w, part, d_acc, row_sem, w_sem, part_sem):
+    features = w.shape[0]
     chunk = features // nx
-    piece = chunk // 2
     cut = low_hbm.shape[1]
     wide = nz * HID
-    load_low = pltpu.make_async_copy(low_hbm, ext.at[:, pl.ds(0, cut)], row_sem.at[5])
-    load_high = pltpu.make_async_copy(high_hbm, ext.at[:, pl.ds(cut, high_hbm.shape[1])], row_sem.at[6])
-    load_low.start()
+    load_low, load_high = load_halves(low_hbm, high_hbm, ext, row_sem)
     loads_d = load_weights(nz, nx, features, w_hbm, w, w_sem, (2,))
-    load_high.start()
-    rows = load_rows(ny, y_ref, (s0, s1, s2, s3, s4), tok, row_sem)
     loads = load_weights(nz, nx, features, w_hbm, w, w_sem, (0, 1))
     load_low.wait()
-    for x in range(nx):
-        if x * 2 == nx:
+    high_in = False
+    for x in range(nx):
+        if (x + 1) * chunk > cut and not high_in:
             load_high.wait()
+            high_in = True
         for copy in loads_d[x]:
             copy.wait()
         span = slice(x * chunk, (x + 1) * chunk)
@@ -130,20 +143,49 @@
             d_acc[...] = dg
         else:
             d_acc[...] += dg
-    extra = ext[:, features:].astype(F32)
-    prob = extra[:, 0:1] + extra[:, 1:2]
+    prob = prob_of(ext, features)
     gate_pre, up_pre = gu_ref[:, :wide], gu_ref[:, wide:]
     down_grad = d_acc[...]
     sig = jax.nn.sigmoid(gate_pre)
     act = gate_pre * sig
     hidden = (act * up_pre).astype(BF16)
+    hidden_ref[...] = hidden
     scores = jnp.sum(hidden.astype(F32) * down_grad, axis=1, keepdims=True)
     hidden_grad = prob * down_grad
-    gate_grad = (hidden_grad * up_pre * sig * (1.0 + gate_pre * (1.0 - sig))).astype(BF16)
-    up_grad = (hidden_grad * act).astype(BF16)
-    gu_grad = jnp.concatenate([gate_grad, up_grad], axis=1)
+    grad_ref[:, :wide] = (hidden_grad * up_pre * sig * (1.0 + gate_pre * (1.0 - sig))).astype(BF16)
+    grad_ref[:, wide:] = (hidden_grad * act).astype(BF16)
+    gu_grad = grad_ref[...]
+    lane = lax.broadcasted_iota(jnp.int32, (scores.shape[0], PAD), 1)
+    high = scores.astype(BF16).astype(F32)
+    low = scores - high
+    part[:, features:] = jnp.where(lane == 0, high, jnp.where(lane == 1, low, 0.0)).astype(BF16)
+    stores = []
+    for x in range(nx):
+        for copy in loads[x]:
+            copy.wait()
+        span = slice(x * chunk, (x + 1) * chunk)
+        part[:, span] = dot(gu_grad, w[span, : 2 * wide], ((1,), (1,))).astype(BF16)
+        if x == nx - 1:
+            span = slice(x * chunk, features + PAD)
+        copy = pltpu.make_async_copy(part.at[:, span], part_hbm.at[:, span], part_sem.at[x])
+        copy.start()
+        stores.append(copy)
+    for copy in stores:
+        copy.wait()
+
+
+def terms_kernel(nz, nx, ny, y_ref, s0, s1, s2, s3, s4, low_hbm, high_hbm, grad_ref, hidden_ref, terms_hbm,
+                 tok, ext, terms, row_sem, terms_sem):
+    features = tok.shape[1]
+    chunk = features // nx
+    piece = chunk // 2
+    wide = nz * HID
+    rows = load_rows(ny, y_ref, (s0, s1, s2, s3, s4), tok, row_sem)
+    rows += load_halves(low_hbm, high_hbm, ext, row_sem)
     for copy in rows:
         copy.wait()
+    prob = prob_of(ext, features)
+    gu_grad, hidden = grad_ref[...], hidden_ref[...]
     stores = []
     for x in range(nx):
         span = slice(x * chunk, (x + 1) * chunk)
@@ -158,20 +200,6 @@
             )
             copy.start()
             stores.append(copy)
-    lane = lax.broadcasted_iota(jnp.int32, (scores.shape[0], PAD), 1)
-    high = scores.astype(BF16).astype(F32)
-    low = scores - high
-    part[:, features:] = jnp.where(lane == 0, high, jnp.where(lane == 1, low, 0.0)).astype(BF16)
-    for x in range(nx):
-        for copy in loads[x]:
-            copy.wait()
-        span = slice(x * chunk, (x + 1) * chunk)
-        part[:, span] = dot(gu_grad, w[span, : 2 * wide], ((1,), (1,))).astype(BF16)
-        if x == nx - 1:
-            span = slice(x * chunk, features + PAD)
-        copy = pltpu.make_async_copy(part.at[:, span], part_hbm.at[:, span], part_sem.at[x])
-        copy.start()
-        stores.append(copy)
     for copy in stores:
         copy.wait()
 
@@ -205,38 +233,60 @@
     )(y, *tok, w)
 
 
-def expert_math(y, tok, low, high, w, gu, nz, nx):
-    rows, features = low.shape[0], tok[0].shape[1]
-    held = w.shape[0]
+def expert_math(low, high, w, gu, nz, nx):
+    rows, features = gu.shape[0], low.shape[1] + high.shape[1] - PAD
     wide = nz * HID
     count = nz * nx * 2 * KINDS
     return pl.pallas_call(
-        functools.partial(expert_kernel, nz, nx, rows // tok[0].shape[0]),
+        functools.partial(expert_kernel, nz, nx),
         name="expert_math",
         out_shape=(
-            jax.ShapeDtypeStruct((held, HID), BF16),
             jax.ShapeDtypeStruct((rows, features + PAD), BF16),
+            jax.ShapeDtypeStruct((rows, 2 * wide), BF16),
+            jax.ShapeDtypeStruct((rows, wide), BF16),
         ),
-        in_specs=[SCALAR] + [ANYWHERE] * (len(tok) + 3) + [INSIDE],
-        out_specs=(ANYWHERE, ANYWHERE),
+        in_specs=[ANYWHERE] * 3 + [INSIDE],
+        out_specs=(ANYWHERE, INSIDE, INSIDE),
         scratch_shapes=[
-            pltpu.VMEM((rows, features), BF16),
             pltpu.VMEM((rows, features + PAD), BF16),
-            pltpu.VMEM((features, KINDS * wide), BF16),
             pltpu.VMEM((features, KINDS * wide), BF16),
             pltpu.VMEM((rows, features + PAD), BF16),
             pltpu.VMEM((rows, wide), F32),
             pltpu.SemaphoreType.DMA((7,)),
             pltpu.SemaphoreType.DMA((count,)),
-            pltpu.SemaphoreType.DMA((count,)),
             pltpu.SemaphoreType.DMA((nx,)),
         ],
         cost_estimate=pl.CostEstimate(
-            flops=12 * rows * features * wide,
+            flops=6 * rows * features * wide,
             transcendentals=rows * wide,
-            bytes_accessed=2 * (2 * held * HID + 3 * rows * features),
+            bytes_accessed=2 * features * (KINDS * wide + 2 * rows),
         ),
-    )(y, *tok, low, high, w, gu)
+    )(low, high, w, gu)
+
+
+def terms_math(y, tok, low, high, grad, hidden, held, nz, nx):
+    rows, features = low.shape[0], tok[0].shape[1]
+    wide = nz * HID
+    count = nz * nx * 2 * KINDS
+    return pl.pallas_call(
+        functools.partial(terms_kernel, nz, nx, rows // tok[0].shape[0]),
+        name="terms_math",
+        out_shape=jax.ShapeDtypeStruct((held, HID), BF16),
+        in_specs=[SCALAR] + [ANYWHERE] * (len(tok) + 2) + [INSIDE] * 2,
+        out_specs=ANYWHERE,
+        scratch_shapes=[
+            pltpu.VMEM((rows, features), BF16),
+            pltpu.VMEM((rows, features + PAD), BF16),
+            pltpu.VMEM((features, KINDS * wide), BF16),
+            pltpu.SemaphoreType.DMA((7,)),
+            pltpu.SemaphoreType.DMA((count,)),
+        ],
+        cost_estimate=pl.CostEstimate(
+            flops=6 * rows * features * wide,
+            transcendentals=0,
+            bytes_accessed=2 * features * (KINDS * wide + 2 * rows),
+        ),
+    )(y, *tok, low, high, grad, hidden)
 
 
 def layer(tokens, grad_out, routes, route_probs, gate_weight, up_weight, down_weight):
@@ -271,20 +321,22 @@
     halves = left[:half], right[half:]
     far = lax.ppermute(halves[0], "y", up), lax.ppermute(halves[1], "y", down)
     came_grd = swapped(send_grd, "e")
-    cut = features * 3 // 7
+    cut = features // 2
     rows_high = lax.all_gather(came_grd[:, cut:], "y", axis=0, tiled=True)
     rows_low = shared(came_grd[:, :cut], "y")
 
     y = lax.axis_index("y").astype(jnp.int32).reshape(1)
     tok = (own, left, right) + far
     gate_up = pre_math(y, tok, weights, ny * slots, nz, nx)
-    terms, part = expert_math(y, tok, rows_low, rows_high, weights, gate_up, nz, nx)
+    part, grad, hidden = expert_math(rows_low, rows_high, weights, gate_up, nz, nx)
+    back = swapped(part, "y")
+    terms = terms_math(y, tok, rows_low, rows_high, grad, hidden, weights.shape[0], nz, nx)
     sums = lax.psum_scatter(terms, HOLD, scatter_dimension=0, tiled=True)
     kept, given = jnp.split(sums, 2, axis=0)
     given = lax.ppermute(given, "zp", SWAP)
     grads = (kept.astype(F32) + given.astype(F32)).astype(BF16).reshape(KINDS, 1, -1, HID)
 
-    back = jnp.sum(swapped(part, "y").astype(F32).reshape(ny, slots, -1), axis=0)
+    back = jnp.sum(back.astype(F32).reshape(ny, slots, -1), axis=0)
     back_score = columns(joined(back[:, features : features + 2]))
     back = jnp.concatenate([back[:, :features].astype(BF16), back_score], axis=1)
     back = swapped(back, "e")

time: 233 us -> 231 us (level)
  the two profiles are of different devices: /device:TPU:32 before, /device:TPU:34 now
where the time goes in v5:
time: 231 us; the launch traced here: 230 us
  blocking collectives  76.1 us (33%)
  waiting for transfers between devices  61.2 us (26%)
  starting transfers between devices  42.2 us (18%)
  Pallas kernels  21.9 us (9%)
  between operations  14.4 us (6%)
  local copies, waits for them, and re-layouts  7.65 us (3%)
  other arithmetic  4.41 us (2%)
  matrix products  2.53 us (1%)
    all_to_all x2, blocking collectives, swapped(): return lax.all_to_all(x, axis, 0, 0, tiled=True)  56.1 us
    all_to_all x3, waiting for transfers between devices, swapped(): return lax.all_to_all(x, axis, 0, 0, tiled=True)  45.8 us
    all_to_all x3, starting transfers between devices, swapped(): return lax.all_to_all(x, axis, 0, 0, tiled=True)  24.1 us
    all_gather x1, blocking collectives, layer(): rows_high = lax.all_gather(came_grd[:, cut:], 'y', axis=0, tiled=True)  20 us
    pallas_call x1, Pallas kernels, expert_math(): pl.pallas_call(functools.partial(expert_kernel, nz, nx), name='expert_mat...  9.95 us
    ppermute x1, waiting for transfers between devices, layer(): paired = lax.ppermute(stored, 'zp', SWAP)  9.67 us
    ppermute x2, starting transfers between devices, layer(): far = (lax.ppermute(halves[0], 'y', up), lax.ppermute(halves[1], 'y', down))  7.05 us
    ppermute x2, starting transfers between devices, layer(): left, right = (lax.ppermute(own, 'y', up), lax.ppermute(own, 'y', down))  7.04 us
  transfers between devices with their start and end apart: 11, of which 4 were waited for; matrix products, arithmetic and copies ran while one was open for 3% of the time, Pallas kernels for 2%

profile of v5, /device:TPU:34, one launch (start us, length us, event | category | flops | bytes accessed | tf_op | source)
XLA Modules:
  0.0 230.5 jit_solution(16946333058909972305)
XLA Ops:
  7.2 1.1 pad_maximum_fusion.1
  8.3 2.0 collective-permute-start
  10.3 9.7 %collective-permute-done = bf16[1344,128]{1,0:T(8,128)(2,1)S(1)} collective-permute-done((bf16[1344,128]{1,0:T(8,128)(2,1)S(1)}, bf16[1344,128]{1,0:T(8,128)(2,1)S(1)}, u32[]{:S(2)}, u32[]{:S(2)}) %collective-permute-start) | collective-permute-done | bytes 344096 | tf_op jit(solution)/shard_map/ppermute | solution.py:299
  20.0 1.9 pad_maximum_fusion
  22.2 1.1 fusion
  23.3 14.2 %all-to-all-start = ((bf16[8,8,3584]{2,1,0:T(8,128)(2,1)}), bf16[8,8,3584]{2,1,0:T(8,128)(2,1)S(1)}, u32[]{:S(2)}, u32[]{:S(2)}) async-start(bf16[8,8,3584]{2,1,0:T(8,128)(2,1)} %fusion), calls=%async_computation | async-start | bytes 917504 | tf_op jit(solution)/shard_map/all_to_all | solution.py:43
  39.2 23.6 %all-to-all-done = bf16[8,8,3584]{2,1,0:T(8,128)(2,1)S(1)} async-done(((bf16[8,8,3584]{2,1,0:T(8,128)(2,1)}), bf16[8,8,3584]{2,1,0:T(8,128)(2,1)S(1)}, u32[]{:S(2)}, u32[]{:S(2)}) %all-to-all-start) | async-done | bytes 458784 | tf_op jit(solution)/shard_map/all_to_all | solution.py:43
  62.8 6.4 %all-to-all-start.1 = ((bf16[8,8,3712]{2,1,0:T(8,128)(2,1)}), bf16[8,8,3712]{2,1,0:T(8,128)(2,1)S(1)}, u32[]{:S(2)}, u32[]{:S(2)}) async-start(bf16[8,8,3712]{2,1,0:T(8,128)(2,1)} %bitcast.8), calls=%async_computation.1 | async-start | bytes 950272 | tf_op jit(solution)/shard_map/all_to_all | solution.py:43
  69.2 3.5 %collective-permute-start.1 = (bf16[64,3584]{1,0:T(8,128)(2,1)S(1)}, bf16[64,3584]{1,0:T(8,128)(2,1)S(1)}, u32[]{:S(2)}, u32[]{:S(2)}) collective-permute-start(bf16[64,3584]{1,0:T(8,128)(2,1)S(1)} %bitcast.57), channel_id=1, source_target_pairs={{0,8},{8,16},{16,24},{24,0},{1,9},{9,17},{17,25},{25,1},{2,10},{10... | collective-permute-start | bytes 1376264 | tf_op jit(solution)/shard_map/ppermute | solution.py:320
  72.7 3.6 %collective-permute-start.2 = (bf16[64,3584]{1,0:T(8,128)(2,1)S(1)}, bf16[64,3584]{1,0:T(8,128)(2,1)S(1)}, u32[]{:S(2)}, u32[]{:S(2)}) collective-permute-start(bf16[64,3584]{1,0:T(8,128)(2,1)S(1)} %bitcast.58), channel_id=1, source_target_pairs={{0,24},{8,0},{16,8},{24,16},{1,25},{9,1},{17,9},{25,17},{2,26},{10... | collective-permute-start | bytes 1376264 | tf_op jit(solution)/shard_map/ppermute | solution.py:320
  76.3 22.2 %all-to-all-done.1 = bf16[8,8,3712]{2,1,0:T(8,128)(2,1)S(1)} async-done(((bf16[8,8,3712]{2,1,0:T(8,128)(2,1)}), bf16[8,8,3712]{2,1,0:T(8,128)(2,1)S(1)}, u32[]{:S(2)}, u32[]{:S(2)}) %all-to-all-start.1) | async-done | bytes 475168 | tf_op jit(solution)/shard_map/all_to_all | solution.py:43
  99.5 3.5 %all-to-all-start.2 = ((bf16[4,64,1792]{2,1,0:T(8,128)(2,1)}), bf16[4,64,1792]{2,1,0:T(8,128)(2,1)S(1)}, u32[]{:S(2)}, u32[]{:S(2)}) async-start(bf16[4,64,1792]{2,1,0:T(8,128)(2,1)} %broadcast_in_dim.74), calls=%async_computation.2 | async-start | bytes 1835008 | tf_op jit(solution)/shard_map/all_to_all | solution.py:43
  103.1 3.8 %collective-permute-start.3 = (bf16[32,3584]{1,0:T(8,128)(2,1)S(1)}, bf16[32,3584]{1,0:T(8,128)(2,1)S(1)}, u32[]{:S(2)}, u32[]{:S(2)}) collective-permute-start(bf16[32,3584]{1,0:T(8,128)(2,1)S(1)} %slice.80), channel_id=1, source_target_pairs={{0,8},{8,16},{16,24},{24,0},{1,9},{9,17},{17,25},{25,1},{2,10},{10... | collective-permute-start | bytes 688136 | tf_op jit(solution)/shard_map/ppermute | solution.py:322
  107.0 3.2 %collective-permute-start.4 = (bf16[32,3584]{1,0:T(8,128)(2,1)S(1)}, bf16[32,3584]{1,0:T(8,128)(2,1)S(1)}, u32[]{:S(2)}, u32[]{:S(2)}) collective-permute-start(bf16[32,3584]{1,0:T(8,128)(2,1)S(1)} %slice.81), channel_id=1, source_target_pairs={{0,24},{8,0},{16,8},{24,16},{1,25},{9,1},{17,9},{25,17},{2,26},{10... | collective-permute-start | bytes 688136 | tf_op jit(solution)/shard_map/ppermute | solution.py:322
  110.2 20.0 %all_gather.6.high_hbm = bf16[256,1920]{1,0:T(8,128)(2,1)} all-gather(bf16[64,1920]{1,0:T(8,128)(2,1)S(1)} %slice.79), channel_id=1, replica_groups=mesh['e'=8,'zp'=2,'y'=4,'x'=4,'c'=2] {'y'}, dimensions={0}, use_global_device_ids=true | all-gather | bytes 1228800 | tf_op jit(solution)/shard_map/all_gather | solution.py:325
  131.0 5.3 %pre_math.1.gu_ref = f32[256,512]{1,0:T(8,128)} custom-call(s32[1]{0:T(128)} %bitcast.14.y_ref, bf16[64,3584]{1,0:T(8,128)(2,1)} %bitcast.59, bf16[64,3584]{1,0:T(8,128)(2,1)} %copy-done.3, bf16[64,3584]{1,0:T(8,128)(2,1)} %copy-done.4, bf16[32,3584]{1,0:T(8,128)(2,1)} %copy-done.6, bf16[32,3584]{1,0:T(8,128)(2,1)} %copy-done.7, ...), custom_call_target="tpu_custom_call" | custom-call | flops 939524096 | bytes 5505024 | tf_op jit(solution)/shard_map/pre_math/pallas_call | solution.py:216
  137.4 9.9 %expert_math.1 = (bf16[256,3712]{1,0:T(8,128)(2,1)}, bf16[256,512]{1,0:T(8,128)(2,1)}, bf16[256,256]{1,0:T(8,128)(2,1)}) custom-call(bf16[256,1792]{1,0:T(8,128)(2,1)} %bitcast.55, bf16[256,1920]{1,0:T(8,128)(2,1)} %all_gather.6.high_hbm, bf16[21504,128]{1,0:T(8,128)(2,1)} %all-gather.2.cloned.1.call-done.w_hbm, f32[256,512]{1,0:T(8,128)} %pre_math.1.gu_ref), custom_call_target="tpu_custom_call" | custom-call | flops 1409286144 | bytes 9175040 | tf_op jit(solution)/shard_map/expert_math/pallas_call | solution.py:240
  147.3 6.7 %terms_math.1 = bf16[21504,128]{1,0:T(8,128)(2,1)} custom-call(s32[1]{0:T(128)} %bitcast.14.y_ref, bf16[64,3584]{1,0:T(8,128)(2,1)} %bitcast.60, bf16[64,3584]{1,0:T(8,128)(2,1)} %copy-done.3, bf16[64,3584]{1,0:T(8,128)(2,1)} %copy-done.4, bf16[32,3584]{1,0:T(8,128)(2,1)} %copy-done.6, bf16[32,3584]{1,0:T(8,128)(2,1)} %copy-done.7, ...), custom_call_target="tpu_custom_call" | custom-call | flops 1409286144 | bytes 9175040 | tf_op jit(solution)/shard_map/terms_math/pallas_call | solution.py:271
  154.0 1.5 copy-done.5
  155.5 22.4 %all_to_all.50 = bf16[4,64,3712]{2,1,0:T(8,128)(2,1)S(1)} all-to-all(bf16[4,64,3712]{2,1,0:T(8,128)(2,1)S(1)} %bitcast.63), channel_id=1, replica_groups=mesh['e'=8,'zp'=2,'y'=4,'x'=4,'c'=2] {'y'}, dimensions={0} | all-to-all | bytes 3801088 | tf_op jit(solution)/shard_map/all_to_all | solution.py:43
  178.4 33.7 %all_to_all.51 = bf16[8,8,3712]{2,1,0:T(8,128)(2,1)S(1)} all-to-all(bf16[8,8,3712]{2,1,0:T(8,128)(2,1)S(1)} %concatenate.29), channel_id=1, replica_groups=mesh['e'=8,'zp'=2,'y'=4,'x'=4,'c'=2] {'e'}, dimensions={0} | all-to-all | bytes 950272 | tf_op jit(solution)/shard_map/all_to_all | solution.py:43
  212.6 1.1 split.9
  213.7 1.9 collective-permute-start.5
  217.1 5.7 %collective-permute-done.5 = bf16[1344,128]{1,0:T(8,128)(2,1)S(1)} collective-permute-done((bf16[1344,128]{1,0:T(8,128)(2,1)S(1)}, bf16[1344,128]{1,0:T(8,128)(2,1)S(1)}, u32[]{:S(2)}, u32[]{:S(2)}) %collective-permute-start.5) | collective-permute-done | bytes 344096 | tf_op jit(solution)/shard_map/ppermute | solution.py:336
  (67 shorter events, 8.1 us)
Async XLA Ops:
  7.2 15.0 %copy-start = (bf16[24,3584]{1,0:T(8,128)(2,1)S(1)}, bf16[24,3584]{1,0:T(8,128)(2,1)}, u32[]{:S(2)}) copy-start(bf16[24,3584]{1,0:T(8,128)(2,1)} %param.7) | copy-start | bytes 516100
  7.2 123.1 %all-gather.2.cloned.1.call-start = ((), (), s32[]{:S(2)}) async-start(), calls=%async_computation.6 | async-start | bytes 6193152 | tf_op jit(solution)/shard_map/all_gather | solution.py:300
  7.2 14.8 %copy-start.10 = (s32[24,2]{0,1:T(2,128)S(1)}, s32[24,2]{0,1:T(2,128)}, u32[]{:S(2)}) copy-start(s32[24,2]{0,1:T(2,128)} %param.9) | copy-start | bytes 580
  8.3 11.7 %collective-permute-start = (bf16[1344,128]{1,0:T(8,128)(2,1)S(1)}, bf16[1344,128]{1,0:T(8,128)(2,1)S(1)}, u32[]{:S(2)}, u32[]{:S(2)}) collective-permute-start(bf16[1344,128]{1,0:T(8,128)(2,1)S(1)} %pad_maximum_fusion.1), channel_id=1, source_target_pairs={{0,32},{32,0},{1,33},{33,1},{2,34},{34,2},{3,35},{35,3},{4,36},{36... | collective-permute-start | bytes 1032200 | tf_op jit(solution)/shard_map/ppermute | solution.py:299
  21.9 15.6 %copy-start.11 = (f32[24,2]{0,1:T(2,128)S(1)}, f32[24,2]{0,1:T(2,128)}, u32[]{:S(2)}) copy-start(f32[24,2]{0,1:T(2,128)} %param.10) | copy-start | bytes 580
  21.9 16.0 %copy-start.9 = (bf16[24,3584]{1,0:T(8,128)(2,1)S(1)}, bf16[24,3584]{1,0:T(8,128)(2,1)}, u32[]{:S(2)}) copy-start(bf16[24,3584]{1,0:T(8,128)(2,1)} %param.8) | copy-start | bytes 516100
  23.3 39.5 %all-to-all-start = ((bf16[8,8,3584]{2,1,0:T(8,128)(2,1)}), bf16[8,8,3584]{2,1,0:T(8,128)(2,1)S(1)}, u32[]{:S(2)}, u32[]{:S(2)}) async-start(bf16[8,8,3584]{2,1,0:T(8,128)(2,1)} %fusion), calls=%async_computation | async-start | bytes 917504 | tf_op jit(solution)/shard_map/all_to_all | solution.py:43
  62.8 36.7 %copy-start.2 = (bf16[8,8,3584]{2,1,0:T(8,128)(2,1)}, bf16[8,8,3584]{2,1,0:T(8,128)(2,1)S(1)}, u32[]{:S(2)}) copy-start(bf16[8,8,3584]{2,1,0:T(8,128)(2,1)S(1)} %all-to-all-done) | copy-start | bytes 1376260
  62.8 35.7 %all-to-all-start.1 = ((bf16[8,8,3712]{2,1,0:T(8,128)(2,1)}), bf16[8,8,3712]{2,1,0:T(8,128)(2,1)S(1)}, u32[]{:S(2)}, u32[]{:S(2)}) async-start(bf16[8,8,3712]{2,1,0:T(8,128)(2,1)} %bitcast.8), calls=%async_computation.1 | async-start | bytes 950272 | tf_op jit(solution)/shard_map/all_to_all | solution.py:43
  69.2 33.8 %collective-permute-start.1 = (bf16[64,3584]{1,0:T(8,128)(2,1)S(1)}, bf16[64,3584]{1,0:T(8,128)(2,1)S(1)}, u32[]{:S(2)}, u32[]{:S(2)}) collective-permute-start(bf16[64,3584]{1,0:T(8,128)(2,1)S(1)} %bitcast.57), channel_id=1, source_target_pairs={{0,8},{8,16},{16,24},{24,0},{1,9},{9,17},{17,25},{25,1},{2,10},{10... | collective-permute-start | bytes 1376264 | tf_op jit(solution)/shard_map/ppermute | solution.py:320
  72.7 34.2 %collective-permute-start.2 = (bf16[64,3584]{1,0:T(8,128)(2,1)S(1)}, bf16[64,3584]{1,0:T(8,128)(2,1)S(1)}, u32[]{:S(2)}, u32[]{:S(2)}) collective-permute-start(bf16[64,3584]{1,0:T(8,128)(2,1)S(1)} %bitcast.58), channel_id=1, source_target_pairs={{0,24},{8,0},{16,8},{24,16},{1,25},{9,1},{17,9},{25,17},{2,26},{10... | collective-permute-start | bytes 1376264 | tf_op jit(solution)/shard_map/ppermute | solution.py:320
  99.5 36.9 %all-to-all-start.2 = ((bf16[4,64,1792]{2,1,0:T(8,128)(2,1)}), bf16[4,64,1792]{2,1,0:T(8,128)(2,1)S(1)}, u32[]{:S(2)}, u32[]{:S(2)}) async-start(bf16[4,64,1792]{2,1,0:T(8,128)(2,1)} %broadcast_in_dim.74), calls=%async_computation.2 | async-start | bytes 1835008 | tf_op jit(solution)/shard_map/all_to_all | solution.py:43
  103.0 109.6 %reduce-scatter.2.cloned.1.call-start = ((), (), s32[]{:S(2)}) async-start(), calls=%async_computation.7 | async-start | bytes 6193152 | tf_op jit(solution)/shard_map/reduce_scatter | solution.py:334
  103.0 27.2 %copy-start.3 = (bf16[64,3584]{1,0:T(8,128)(2,1)}, bf16[64,3584]{1,0:T(8,128)(2,1)S(1)}, u32[]{:S(2)}) copy-start(bf16[64,3584]{1,0:T(8,128)(2,1)S(1)} %collective-permute-done.1.s1) | copy-start | bytes 1376260
  103.1 27.1 %collective-permute-start.3 = (bf16[32,3584]{1,0:T(8,128)(2,1)S(1)}, bf16[32,3584]{1,0:T(8,128)(2,1)S(1)}, u32[]{:S(2)}, u32[]{:S(2)}) collective-permute-start(bf16[32,3584]{1,0:T(8,128)(2,1)S(1)} %slice.80), channel_id=1, source_target_pairs={{0,8},{8,16},{16,24},{24,0},{1,9},{9,17},{17,25},{25,1},{2,10},{10... | collective-permute-start | bytes 688136 | tf_op jit(solution)/shard_map/ppermute | solution.py:322
  106.9 23.4 %copy-start.4 = (bf16[64,3584]{1,0:T(8,128)(2,1)}, bf16[64,3584]{1,0:T(8,128)(2,1)S(1)}, u32[]{:S(2)}) copy-start(bf16[64,3584]{1,0:T(8,128)(2,1)S(1)} %collective-permute-done.2.s2) | copy-start | bytes 1376260
  107.0 23.3 %collective-permute-start.4 = (bf16[32,3584]{1,0:T(8,128)(2,1)S(1)}, bf16[32,3584]{1,0:T(8,128)(2,1)S(1)}, u32[]{:S(2)}, u32[]{:S(2)}) collective-permute-start(bf16[32,3584]{1,0:T(8,128)(2,1)S(1)} %slice.81), channel_id=1, source_target_pairs={{0,24},{8,0},{16,8},{24,16},{1,25},{9,1},{17,9},{25,17},{2,26},{10... | collective-permute-start | bytes 688136 | tf_op jit(solution)/shard_map/ppermute | solution.py:322
  130.2 0.7 copy-start.6
  130.2 0.8 copy-start.7
  136.3 1.0 copy-start.1
  154.0 1.5 copy-start.5
  212.6 10.2 %copy-start.8 = (bf16[2688,128]{1,0:T(8,128)(2,1)S(1)}, bf16[2688,128]{1,0:T(8,128)(2,1)}, u32[]{:S(2)}) copy-start(bf16[2688,128]{1,0:T(8,128)(2,1)} %reduce-scatter.2.cloned.1.call-done) | copy-start | bytes 2064388
  213.7 9.1 %collective-permute-start.5 = (bf16[1344,128]{1,0:T(8,128)(2,1)S(1)}, bf16[1344,128]{1,0:T(8,128)(2,1)S(1)}, u32[]{:S(2)}, u32[]{:S(2)}) collective-permute-start(bf16[1344,128]{1,0:T(8,128)(2,1)S(1)} %split.9), channel_id=1, source_target_pairs={{0,32},{32,0},{1,33},{33,1},{2,34},{34,2},{3,35},{35,3},{4,36},{36... | collective-permute-start | bytes 1032200 | tf_op jit(solution)/shard_map/ppermute | solution.py:336
Sparse Core Ops, SparseCore 0:
  22.1 48.3 all-gather.1
  154.1 39.8 reduce-scatter.1

commit v6 on v4

v6 whole, which is shorter than its diff:
```python
import functools

import jax
import jax.numpy as jnp
from jax import lax
from jax.experimental import pallas as pl
from jax.experimental.pallas import tpu as pltpu
from jax.sharding import Mesh, PartitionSpec as P


GROUP = 8
CAP = 8
HID = 128
PAD = 128
F32 = jnp.float32
BF16 = jnp.bfloat16
AXES = ("e", "zp", "y", "x", "c")
HOLD = ("x", "c")
SWAP = [(0, 1), (1, 0)]
KINDS = 3
PRE_GRANT = 20 << 20
EXPERT_GRANT = 58 << 20


def dot(a, b, dims):
    return lax.dot_general(a, b, (dims, ((), ())), preferred_element_type=F32)


def split(v):
    high = lax.reduce_precision(v, 8, 7)
    return high.astype(BF16), (v - high).astype(BF16)


def columns(v):
    high, low = split(v)
    blank = jnp.zeros((v.shape[0], PAD - 2), BF16)
    return jnp.concatenate([high[:, None], low[:, None], blank], axis=1)


def joined(cols):
    return cols[:, 0].astype(F32) + cols[:, 1].astype(F32)


def swapped(x, axis):
    return lax.all_to_all(x, axis, 0, 0, tiled=True)


def shared(x, axis):
    n = lax.axis_size(axis)
    return swapped(jnp.broadcast_to(x[None], (n,) + x.shape).reshape(n * x.shape[0], -1), axis)


def pieces(nz, nx, x, features):
    chunk = features // nx
    piece = chunk // 2
    for c in range(2):
        for z in range(nz):
            for m in range(KINDS):
                yield m, ((x * 2 + c) * nz + z) * KINDS + m, x * chunk + c * piece, (m * nz + z) * HID


def load_weights(nz, nx, features, w_hbm, w, sem, kinds):
    piece = features // nx // 2
    loads = []
    for x in range(nx):
        loads.append([])
        for m, i, row, col in pieces(nz, nx, x, features):
            if m in kinds:
                copy = pltpu.make_async_copy(
                    w_hbm.at[pl.ds(i * piece, piece), :],
                    w.at[pl.ds(row, piece), pl.ds(col, HID)],
                    sem.at[i],
                )
                copy.start()
                loads[-1].append(copy)
    return loads


def pre_kernel(nz, nx, ny, y_ref, s0, s1, s2, s3, s4, w_hbm, rows, w, gu_ref, w_sem):
    features = rows.shape[1]
    chunk = features // nx
    wide = nz * HID
    loads = load_weights(nz, nx, features, w_hbm, w, w_sem, range(KINDS))
    block, half = s0.shape[0], s3.shape[0]
    for source, ahead, skip in ((s0, 0, 0), (s1, ny - 1, 0), (s2, 1, 0), (s3, 2, 0), (s4, 2, half)):
        at = pl.multiple_of(lax.rem(y_ref[0] + ahead, ny) * block + skip, half)
        rows[pl.ds(at, source.shape[0]), :] = source[...]
    for x in range(nx):
        for copy in loads[x]:
            copy.wait()
        span = slice(x * chunk, (x + 1) * chunk)
        gu = dot(rows[:, span], w[span, : 2 * wide], ((1,), (0,)))
        if x == 0:
            gu_ref[...] = gu
        else:
            gu_ref[...] += gu


def expert_kernel(nz, nx, rows_hbm, ext, w_hbm, gu_hbm, terms_hbm, part, rows, w, gu_ref, terms, in_sem, terms_sem):
    features = w.shape[0]
    chunk = features // nx
    piece = chunk // 2
    wide = nz * HID
    down = pl.ds(2 * wide, wide)
    load_d = pltpu.make_async_copy(w_hbm.at[:, down], w.at[:, down], in_sem.at[0])
    load_gu = pltpu.make_async_copy(gu_hbm, gu_ref, in_sem.at[1])
    loads = [load_d, load_gu]
    for x in range(nx):
        span = pl.ds(x * chunk, chunk)
        loads.append(pltpu.make_async_copy(rows_hbm.at[:, span], rows.at[:, span], in_sem.at[2 + x]))
    for x in range(nx):
        span, cols = pl.ds(x * chunk, chunk), pl.ds(0, 2 * wide)
        loads.append(pltpu.make_async_copy(w_hbm.at[span, cols], w.at[span, cols], in_sem.at[2 + nx + x]))
    for copy in loads:
        copy.start()
    load_d.wait()
    down_grad = dot(ext[:, :features], w[:, 2 * wide :], ((1,), (0,)))
    extra = ext[:, features:].astype(F32)
    prob = extra[:, 0:1] + extra[:, 1:2]
    load_gu.wait()
    gate_pre, up_pre = gu_ref[:, :wide], gu_ref[:, wide:]
    sig = jax.nn.sigmoid(gate_pre)
    act = gate_pre * sig
    hidden = (act * up_pre).astype(BF16)
    scores = jnp.sum(hidden.astype(F32) * down_grad, axis=1, keepdims=True)
    hidden_grad = prob * down_grad
    gate_grad = (hidden_grad * up_pre * sig * (1.0 + gate_pre * (1.0 - sig))).astype(BF16)
    up_grad = (hidden_grad * act).astype(BF16)
    gu_grad = jnp.concatenate([gate_grad, up_grad], axis=1)
    stores = []
    for x in range(nx):
        loads[2 + x].wait()
        span = slice(x * chunk, (x + 1) * chunk)
        terms[span, : 2 * wide] = dot(rows[:, span], gu_grad, ((0,), (0,))).astype(BF16)
        scaled = (prob * ext[:, span].astype(F32)).astype(BF16)
        terms[span, 2 * wide :] = dot(scaled, hidden, ((0,), (0,))).astype(BF16)
        for m, i, row, col in pieces(nz, nx, x, features):
            copy = pltpu.make_async_copy(
                terms.at[pl.ds(row, piece), pl.ds(col, HID)],
                terms_hbm.at[pl.ds(i * piece, piece), :],
                terms_sem.at[i],
            )
            copy.start()
            stores.append(copy)
    lane = lax.broadcasted_iota(jnp.int32, (scores.shape[0], PAD), 1)
    high = scores.astype(BF16).astype(F32)
    low = scores - high
    part[:, features:] = jnp.where(lane == 0, high, jnp.where(lane == 1, low, 0.0)).astype(BF16)
    for x in range(nx):
        loads[2 + nx + x].wait()
        span = slice(x * chunk, (x + 1) * chunk)
        part[:, span] = dot(gu_grad, w[span, : 2 * wide], ((1,), (1,))).astype(BF16)
    for copy in stores:
        copy.wait()


ANYWHERE = pl.BlockSpec(memory_space=pl.ANY)
SCALAR = pl.BlockSpec(memory_space=pltpu.SMEM)
INSIDE = pl.BlockSpec(memory_space=pltpu.VMEM)


def pre_math(y, tok, w, nrows, nz, nx):
    features = tok[0].shape[1]
    wide = nz * HID
    return pl.pallas_call(
        functools.partial(pre_kernel, nz, nx, nrows // tok[0].shape[0]),
        name="pre_math",
        out_shape=(
            jax.ShapeDtypeStruct((nrows, features), BF16),
            jax.ShapeDtypeStruct((features, KINDS * wide), BF16),
            jax.ShapeDtypeStruct((nrows, 2 * wide), F32),
        ),
        in_specs=[SCALAR] + [INSIDE] * len(tok) + [ANYWHERE],
        out_specs=(INSIDE,) * 3,
        scratch_shapes=[pltpu.SemaphoreType.DMA((nz * nx * 2 * KINDS,))],
        compiler_params=pltpu.CompilerParams(vmem_limit_bytes=PRE_GRANT),
        cost_estimate=pl.CostEstimate(
            flops=4 * nrows * features * wide,
            transcendentals=0,
            bytes_accessed=2 * features * (KINDS * wide + nrows),
        ),
    )(y, *tok, w)


def expert_math(rows, ext, w, gu, held, nz, nx):
    count, features = rows.shape
    wide = nz * HID
    copies = nz * nx * 2 * KINDS
    return pl.pallas_call(
        functools.partial(expert_kernel, nz, nx),
        name="expert_math",
        out_shape=(
            pltpu.HBM((held, HID), BF16),
            jax.ShapeDtypeStruct((count, features + PAD), BF16),
        ),
        in_specs=[ANYWHERE, INSIDE, ANYWHERE, ANYWHERE],
        out_specs=(ANYWHERE, INSIDE),
        scratch_shapes=[
            pltpu.VMEM((count, features), BF16),
            pltpu.VMEM((features, KINDS * wide), BF16),
            pltpu.VMEM((count, 2 * wide), F32),
            pltpu.VMEM((features, KINDS * wide), BF16),
            pltpu.SemaphoreType.DMA((2 + 2 * nx,)),
            pltpu.SemaphoreType.DMA((copies,)),
        ],
        compiler_params=pltpu.CompilerParams(vmem_limit_bytes=EXPERT_GRANT),
        cost_estimate=pl.CostEstimate(
            flops=12 * count * features * wide,
            transcendentals=count * wide,
            bytes_accessed=2 * features * (KINDS * wide + 2 * count),
        ),
    )(rows, ext, w, gu)


def layer(tokens, grad_out, routes, route_probs, gate_weight, up_weight, down_weight):
    count, features = tokens.shape
    experts, ny = lax.axis_size("e"), lax.axis_size("y")
    nz, nx = lax.axis_size("zp"), lax.axis_size("x")
    slots = experts * CAP

    stored = jnp.concatenate([gate_weight[0], up_weight[0], down_weight[0]], axis=0)
    paired = lax.ppermute(stored, "zp", SWAP)
    weights = lax.all_gather(jnp.concatenate([stored, paired], axis=0), HOLD, axis=0, tiled=True)

    ids = jnp.arange(experts, dtype=jnp.int32)
    first, second = routes[:, 0:1] == ids, routes[:, 1:2] == ids
    named = (first | second).astype(BF16)
    place = jnp.arange(count)
    before = (place[:, None] > place[None, :]).astype(BF16)
    rank = dot(before, named, ((1,), (0,))).T
    taken = (named.T[:, None, :] > 0) & (rank[:, None, :] == jnp.arange(CAP, dtype=F32)[None, :, None])
    prob = jnp.where(first, route_probs[:, 0:1], 0.0) + jnp.where(second, route_probs[:, 1:2], 0.0)
    slot_prob = jnp.sum(jnp.where(taken, prob.T[:, None, :], 0.0), axis=2).reshape(slots)
    select = taken.astype(BF16).reshape(slots, count)
    send_tok = dot(select, tokens, ((1,), (0,))).astype(BF16)
    send_grd = dot(select, grad_out, ((1,), (0,))).astype(BF16)
    send_grd = jnp.concatenate([send_grd, columns(slot_prob)], axis=1)

    own = swapped(send_tok, "e")
    own, send_grd = lax.optimization_barrier((own, send_grd))
    up, down = [(i, (i + 1) % ny) for i in range(ny)], [(i, (i - 1) % ny) for i in range(ny)]
    half = slots // 2
    left, right = lax.ppermute(own, "y", up), lax.ppermute(own, "y", down)
    halves = left[:half], right[half:]
    far = lax.ppermute(halves[0], "y", up), lax.ppermute(halves[1], "y", down)
    came_grd = swapped(send_grd, "e")
    rows_ext = shared(came_grd, "y")

    y = lax.axis_index("y").astype(jnp.int32).reshape(1)
    rows, blocks, gate_up = pre_math(y, (own, left, right) + far, weights, ny * slots, nz, nx)
    terms, part = expert_math(rows, rows_ext, blocks, gate_up, weights.shape[0], nz, nx)
    back = swapped(part, "y")
    sums = lax.psum_scatter(terms, HOLD, scatter_dimension=0, tiled=True)
    kept, given = jnp.split(sums, 2, axis=0)
    given = lax.ppermute(given, "zp", SWAP)
    grads = (kept.astype(F32) + given.astype(F32)).astype(BF16).reshape(KINDS, 1, -1, HID)

    back = jnp.sum(back.astype(F32).reshape(ny, slots, -1), axis=0)
    back_score = columns(joined(back[:, features : features + 2]))
    back = jnp.concatenate([back[:, :features].astype(BF16), back_score], axis=1)
    back = swapped(back, "e")
    grad_tokens = dot(select, back[:, :features], ((0,), (0,))).astype(BF16)
    score = joined(back[:, features : features + 2]).reshape(experts, CAP, 1)
    score = jnp.sum(jnp.where(taken, score, 0.0), axis=1).T
    grad_probs = jnp.stack(
        [jnp.sum(jnp.where(first, score, 0.0), axis=1), jnp.sum(jnp.where(second, score, 0.0), axis=1)], axis=1
    )
    return (grad_tokens, grad_probs, grads[0], grads[1], grads[2])


def solution(mesh):
    fine = Mesh(mesh.devices.reshape(mesh.shape["ep"] // GROUP, 2, GROUP // 2, -1, 2), AXES)
    rows, stored = P(AXES, None), P(AXES[:3], AXES[3:], None)
    return jax.shard_map(
        layer,
        mesh=fine,
        in_specs=(rows, rows, rows, rows, stored, stored, stored),
        out_specs=(rows, rows, stored, stored, stored),
        check_vma=False,
    )
```

time: 233 us -> 251 us (1.077)
  the two profiles are of different devices: /device:TPU:32 before, /device:TPU:4 now
where the time goes in v6:
time: 251 us; the launch traced here: 250 us
  blocking collectives  94.6 us (38%)
  waiting for transfers between devices  63.7 us (25%)
  starting transfers between devices  43.1 us (17%)
  between operations  14.3 us (6%)
  Pallas kernels  14 us (6%)
  local copies, waits for them, and re-layouts  12.4 us (5%)
  other arithmetic  5.35 us (2%)
  matrix products  2.54 us (1%)
    all_to_all x3, blocking collectives, swapped(): return lax.all_to_all(x, axis, 0, 0, tiled=True)  94.6 us
    all_to_all x2, waiting for transfers between devices, swapped(): return lax.all_to_all(x, axis, 0, 0, tiled=True)  23.7 us
    ppermute x2, waiting for transfers between devices, layer(): left, right = (lax.ppermute(own, 'y', up), lax.ppermute(own, 'y', down))  23.6 us
    all_to_all x2, starting transfers between devices, swapped(): return lax.all_to_all(x, axis, 0, 0, tiled=True)  19.4 us
    pallas_call x1, Pallas kernels, expert_math(): pl.pallas_call(functools.partial(expert_kernel, nz, nx), name='expert_mat...  11 us
    unnamed x18, local copies, waits for them, and re-layouts  8.51 us
    ppermute x1, waiting for transfers between devices, layer(): paired = lax.ppermute(stored, 'zp', SWAP)  8.05 us
    ppermute x2, starting transfers between devices, layer(): far = (lax.ppermute(halves[0], 'y', up), lax.ppermute(halves[1], 'y', down))  7.05 us
  transfers between devices with their start and end apart: 10, of which 6 were waited for; matrix products, arithmetic and copies ran while one was open for 2% of the time, Pallas kernels for 1%

profile of v6, /device:TPU:4, one launch (start us, length us, event | category | flops | bytes accessed | tf_op | source)
XLA Modules:
  0.0 250.1 jit_solution(8620923589250106200)
XLA Ops:
  8.3 4.0 %collective-permute-start.4 = (bf16[1344,128]{1,0:T(8,128)(2,1)S(1)}, bf16[1344,128]{1,0:T(8,128)(2,1)S(1)}, u32[]{:S(2)}, u32[]{:S(2)}) collective-permute-start(bf16[1344,128]{1,0:T(8,128)(2,1)S(1)} %pad_maximum_fusion.1), channel_id=1, source_target_pairs={{0,32},{32,0},{1,33},{33,1},{2,34},{34,2},{3,35},{35,3},{4,36},{36... | collective-permute-start | bytes 1032200 | tf_op jit(solution)/shard_map/ppermute | solution.py:222
  12.3 8.0 %collective-permute-done.4 = bf16[1344,128]{1,0:T(8,128)(2,1)S(1)} collective-permute-done((bf16[1344,128]{1,0:T(8,128)(2,1)S(1)}, bf16[1344,128]{1,0:T(8,128)(2,1)S(1)}, u32[]{:S(2)}, u32[]{:S(2)}) %collective-permute-start.4) | collective-permute-done | bytes 344096 | tf_op jit(solution)/shard_map/ppermute | solution.py:222
  20.3 1.9 pad_maximum_fusion
  23.6 14.9 %all-to-all-start = ((bf16[8,8,3584]{2,1,0:T(8,128)(2,1)}), bf16[8,8,3584]{2,1,0:T(8,128)(2,1)S(1)}, u32[]{:S(2)}, u32[]{:S(2)}) async-start(bf16[8,8,3584]{2,1,0:T(8,128)(2,1)} %fusion), calls=%async_computation | async-start | bytes 917504 | tf_op jit(solution)/shard_map/all_to_all | solution.py:45
  39.4 23.7 %all-to-all-done = bf16[8,8,3584]{2,1,0:T(8,128)(2,1)S(1)} async-done(((bf16[8,8,3584]{2,1,0:T(8,128)(2,1)}), bf16[8,8,3584]{2,1,0:T(8,128)(2,1)S(1)}, u32[]{:S(2)}, u32[]{:S(2)}) %all-to-all-start) | async-done | bytes 458784 | tf_op jit(solution)/shard_map/all_to_all | solution.py:45
  63.1 32.3 %all_to_all.47 = bf16[8,8,3712]{2,1,0:T(8,128)(2,1)S(1)} all-to-all(bf16[8,8,3712]{2,1,0:T(8,128)(2,1)S(1)} %bitcast.62), channel_id=1, replica_groups=mesh['e'=8,'zp'=2,'y'=4,'x'=4,'c'=2] {'e'}, dimensions={0} | all-to-all | bytes 950272 | tf_op jit(solution)/shard_map/all_to_all | solution.py:45
  95.5 1.4 broadcast_in_dim.77
  96.9 4.5 %all-to-all-start.2 = ((bf16[4,64,3712]{2,1,0:T(8,128)(2,1)}), bf16[4,64,3712]{2,1,0:T(8,128)(2,1)}, u32[]{:S(2)}, u32[]{:S(2)}) async-start(bf16[4,64,3712]{2,1,0:T(8,128)(2,1)} %broadcast_in_dim.77), calls=%async_computation.2 | async-start | bytes 3801088 | tf_op jit(solution)/shard_map/all_to_all | solution.py:45
  101.4 3.9 %collective-permute-start = (bf16[64,3584]{1,0:T(8,128)(2,1)S(1)}, bf16[64,3584]{1,0:T(8,128)(2,1)S(1)}, u32[]{:S(2)}, u32[]{:S(2)}) collective-permute-start(bf16[64,3584]{1,0:T(8,128)(2,1)S(1)} %bitcast.55), channel_id=1, source_target_pairs={{0,8},{8,16},{16,24},{24,0},{1,9},{9,17},{17,25},{25,1},{2,10},{10... | collective-permute-start | bytes 1376264 | tf_op jit(solution)/shard_map/ppermute | solution.py:243
  105.3 3.1 %collective-permute-start.1 = (bf16[64,3584]{1,0:T(8,128)(2,1)S(1)}, bf16[64,3584]{1,0:T(8,128)(2,1)S(1)}, u32[]{:S(2)}, u32[]{:S(2)}) collective-permute-start(bf16[64,3584]{1,0:T(8,128)(2,1)S(1)} %bitcast.56), channel_id=1, source_target_pairs={{0,24},{8,0},{16,8},{24,16},{1,25},{9,1},{17,9},{25,17},{2,26},{10... | collective-permute-start | bytes 1376264 | tf_op jit(solution)/shard_map/ppermute | solution.py:243
  108.4 23.6 %collective-permute-done.s1 = bf16[64,3584]{1,0:T(8,128)(2,1)S(1)} collective-permute-done((bf16[64,3584]{1,0:T(8,128)(2,1)S(1)}, bf16[64,3584]{1,0:T(8,128)(2,1)S(1)}, u32[]{:S(2)}, u32[]{:S(2)}) %collective-permute-start) | collective-permute-done | bytes 458784 | tf_op jit(solution)/shard_map/ppermute | solution.py:243
  132.0 1.9 collective-permute-start.2
  134.0 5.1 %collective-permute-start.3 = (bf16[32,3584]{1,0:T(8,128)(2,1)S(1)}, bf16[32,3584]{1,0:T(8,128)(2,1)S(1)}, u32[]{:S(2)}, u32[]{:S(2)}) collective-permute-start(bf16[32,3584]{1,0:T(8,128)(2,1)S(1)} %slice.71), channel_id=1, source_target_pairs={{0,24},{8,0},{16,8},{24,16},{1,25},{9,1},{17,9},{25,17},{2,26},{10... | collective-permute-start | bytes 688136 | tf_op jit(solution)/shard_map/ppermute | solution.py:245
  139.1 2.0 collective-permute-done.2.s3
  141.2 1.5 collective-permute-done.3.s4
  142.7 2.6 %copy-done.1 = bf16[21504,128]{1,0:T(8,128)(2,1)S(1)} copy-done((bf16[21504,128]{1,0:T(8,128)(2,1)S(1)}, bf16[21504,128]{1,0:T(8,128)(2,1)}, u32[]{:S(2)}) %copy-start.1) | copy-done | bytes 5505048
  145.2 3.0 %pre_math.1 = (bf16[256,3584]{1,0:T(8,128)(2,1)S(1)}, bf16[3584,768]{1,0:T(8,128)(2,1)S(1)}, f32[256,512]{1,0:T(8,128)S(1)}) custom-call(s32[1]{0:T(128)} %bitcast.4.y_ref, bf16[64,3584]{1,0:T(8,128)(2,1)S(1)} %bitcast.57, bf16[64,3584]{1,0:T(8,128)(2,1)S(1)} %collective-permute-done.s1, bf16[64,3584]{1,0:T(8,128)(2,1)S(1)} %collective-permute-done.1.s2, ...), custom_call_target="tpu_custom_call" | custom-call | flops 939524096 | bytes 7340032 | tf_op jit(solution)/shard_map/pre_math/pallas_call | solution.py:165
  148.2 2.4 copy-done.2
  152.7 11.0 %expert_math.1 = (bf16[21504,128]{1,0:T(8,128)(2,1)}, bf16[256,3712]{1,0:T(8,128)(2,1)}) custom-call(bf16[256,3584]{1,0:T(8,128)(2,1)} %copy-done.3, bf16[256,3712]{1,0:T(8,128)(2,1)} %bitcast.14.ext, bf16[3584,768]{1,0:T(8,128)(2,1)} %copy-done.2, f32[256,512]{1,0:T(8,128)} %copy-done.4), custom_call_target="tpu_custom_call" | custom-call | flops 2818572288 | bytes 9175040 | tf_op jit(solution)/shard_map/expert_math/pallas_call | solution.py:189
  163.8 1.5 copy-done.5
  165.2 23.3 %all_to_all.48 = bf16[4,64,3712]{2,1,0:T(8,128)(2,1)S(1)} all-to-all(bf16[4,64,3712]{2,1,0:T(8,128)(2,1)S(1)} %bitcast.61), channel_id=1, replica_groups=mesh['e'=8,'zp'=2,'y'=4,'x'=4,'c'=2] {'y'}, dimensions={0} | all-to-all | bytes 3801088 | tf_op jit(solution)/shard_map/all_to_all | solution.py:45
  189.1 39.0 %all_to_all.49 = bf16[8,8,3712]{2,1,0:T(8,128)(2,1)S(1)} all-to-all(bf16[8,8,3712]{2,1,0:T(8,128)(2,1)S(1)} %concatenate.29), channel_id=1, replica_groups=mesh['e'=8,'zp'=2,'y'=4,'x'=4,'c'=2] {'e'}, dimensions={0} | all-to-all | bytes 950272 | tf_op jit(solution)/shard_map/all_to_all | solution.py:45
  229.5 5.6 %collective-permute-start.5 = (bf16[1344,128]{1,0:T(8,128)(2,1)S(1)}, bf16[1344,128]{1,0:T(8,128)(2,1)S(1)}, u32[]{:S(2)}, u32[]{:S(2)}) collective-permute-start(bf16[1344,128]{1,0:T(8,128)(2,1)S(1)} %split.9), channel_id=1, source_target_pairs={{0,32},{32,0},{1,33},{33,1},{2,34},{34,2},{3,35},{35,3},{4,36},{36... | collective-permute-start | bytes 1032200 | tf_op jit(solution)/shard_map/ppermute | solution.py:255
  236.7 4.8 %collective-permute-done.5 = bf16[1344,128]{1,0:T(8,128)(2,1)S(1)} collective-permute-done((bf16[1344,128]{1,0:T(8,128)(2,1)S(1)}, bf16[1344,128]{1,0:T(8,128)(2,1)S(1)}, u32[]{:S(2)}, u32[]{:S(2)}) %collective-permute-start.5) | collective-permute-done | bytes 344096 | tf_op jit(solution)/shard_map/ppermute | solution.py:255
  (56 shorter events, 10.7 us)
Async XLA Ops:
  7.2 15.3 %copy-start = (bf16[24,3584]{1,0:T(8,128)(2,1)S(1)}, bf16[24,3584]{1,0:T(8,128)(2,1)}, u32[]{:S(2)}) copy-start(bf16[24,3584]{1,0:T(8,128)(2,1)} %param.7) | copy-start | bytes 516100
  7.2 15.2 %copy-start.7 = (s32[24,2]{0,1:T(2,128)S(1)}, s32[24,2]{0,1:T(2,128)}, u32[]{:S(2)}) copy-start(s32[24,2]{0,1:T(2,128)} %param.9) | copy-start | bytes 580
  7.2 135.5 %all-gather.2.cloned.1.call-start = ((), (), s32[]{:S(2)}) async-start(), calls=%async_computation.6 | async-start | bytes 6193152 | tf_op jit(solution)/shard_map/all_gather | solution.py:223
  8.3 30.2 %copy-start.8 = (f32[24,2]{0,1:T(2,128)S(1)}, f32[24,2]{0,1:T(2,128)}, u32[]{:S(2)}) copy-start(f32[24,2]{0,1:T(2,128)} %param.10) | copy-start | bytes 580
  8.3 30.7 %copy-start.6 = (bf16[24,3584]{1,0:T(8,128)(2,1)S(1)}, bf16[24,3584]{1,0:T(8,128)(2,1)}, u32[]{:S(2)}) copy-start(bf16[24,3584]{1,0:T(8,128)(2,1)} %param.8) | copy-start | bytes 516100
  8.3 12.0 %collective-permute-start.4 = (bf16[1344,128]{1,0:T(8,128)(2,1)S(1)}, bf16[1344,128]{1,0:T(8,128)(2,1)S(1)}, u32[]{:S(2)}, u32[]{:S(2)}) collective-permute-start(bf16[1344,128]{1,0:T(8,128)(2,1)S(1)} %pad_maximum_fusion.1), channel_id=1, source_target_pairs={{0,32},{32,0},{1,33},{33,1},{2,34},{34,2},{3,35},{35,3},{4,36},{36... | collective-permute-start | bytes 1032200 | tf_op jit(solution)/shard_map/ppermute | solution.py:222
  23.6 39.5 %all-to-all-start = ((bf16[8,8,3584]{2,1,0:T(8,128)(2,1)}), bf16[8,8,3584]{2,1,0:T(8,128)(2,1)S(1)}, u32[]{:S(2)}, u32[]{:S(2)}) async-start(bf16[8,8,3584]{2,1,0:T(8,128)(2,1)} %fusion), calls=%async_computation | async-start | bytes 917504 | tf_op jit(solution)/shard_map/all_to_all | solution.py:45
  96.9 55.8 %all-to-all-start.2 = ((bf16[4,64,3712]{2,1,0:T(8,128)(2,1)}), bf16[4,64,3712]{2,1,0:T(8,128)(2,1)}, u32[]{:S(2)}, u32[]{:S(2)}) async-start(bf16[4,64,3712]{2,1,0:T(8,128)(2,1)} %broadcast_in_dim.77), calls=%async_computation.2 | async-start | bytes 3801088 | tf_op jit(solution)/shard_map/all_to_all | solution.py:45
  101.4 127.1 %reduce-scatter.2.cloned.1.call-start = ((), (), s32[]{:S(2)}) async-start(), calls=%async_computation.7 | async-start | bytes 6193152 | tf_op jit(solution)/shard_map/reduce_scatter | solution.py:253
  101.4 30.7 %collective-permute-start = (bf16[64,3584]{1,0:T(8,128)(2,1)S(1)}, bf16[64,3584]{1,0:T(8,128)(2,1)S(1)}, u32[]{:S(2)}, u32[]{:S(2)}) collective-permute-start(bf16[64,3584]{1,0:T(8,128)(2,1)S(1)} %bitcast.55), channel_id=1, source_target_pairs={{0,8},{8,16},{16,24},{24,0},{1,9},{9,17},{17,25},{25,1},{2,10},{10... | collective-permute-start | bytes 1376264 | tf_op jit(solution)/shard_map/ppermute | solution.py:243
  105.3 28.7 %collective-permute-start.1 = (bf16[64,3584]{1,0:T(8,128)(2,1)S(1)}, bf16[64,3584]{1,0:T(8,128)(2,1)S(1)}, u32[]{:S(2)}, u32[]{:S(2)}) collective-permute-start(bf16[64,3584]{1,0:T(8,128)(2,1)S(1)} %bitcast.56), channel_id=1, source_target_pairs={{0,24},{8,0},{16,8},{24,16},{1,25},{9,1},{17,9},{25,17},{2,26},{10... | collective-permute-start | bytes 1376264 | tf_op jit(solution)/shard_map/ppermute | solution.py:243
  132.0 9.1 %collective-permute-start.2 = (bf16[32,3584]{1,0:T(8,128)(2,1)S(1)}, bf16[32,3584]{1,0:T(8,128)(2,1)S(1)}, u32[]{:S(2)}, u32[]{:S(2)}) collective-permute-start(bf16[32,3584]{1,0:T(8,128)(2,1)S(1)} %slice.70), channel_id=1, source_target_pairs={{0,8},{8,16},{16,24},{24,0},{1,9},{9,17},{17,25},{25,1},{2,10},{10... | collective-permute-start | bytes 688136 | tf_op jit(solution)/shard_map/ppermute | solution.py:245
  134.0 8.7 %collective-permute-start.3 = (bf16[32,3584]{1,0:T(8,128)(2,1)S(1)}, bf16[32,3584]{1,0:T(8,128)(2,1)S(1)}, u32[]{:S(2)}, u32[]{:S(2)}) collective-permute-start(bf16[32,3584]{1,0:T(8,128)(2,1)S(1)} %slice.71), channel_id=1, source_target_pairs={{0,24},{8,0},{16,8},{24,16},{1,25},{9,1},{17,9},{25,17},{2,26},{10... | collective-permute-start | bytes 688136 | tf_op jit(solution)/shard_map/ppermute | solution.py:245
  142.7 2.6 %copy-start.1 = (bf16[21504,128]{1,0:T(8,128)(2,1)S(1)}, bf16[21504,128]{1,0:T(8,128)(2,1)}, u32[]{:S(2)}) copy-start(bf16[21504,128]{1,0:T(8,128)(2,1)} %all-gather.2.cloned.1.call-done.w_hbm) | copy-start | bytes 16515076
  148.2 2.4 copy-start.2
  150.6 1.2 copy-start.3
  151.9 0.8 copy-start.4
  163.7 1.5 copy-start.5
  229.5 11.9 %collective-permute-start.5 = (bf16[1344,128]{1,0:T(8,128)(2,1)S(1)}, bf16[1344,128]{1,0:T(8,128)(2,1)S(1)}, u32[]{:S(2)}, u32[]{:S(2)}) collective-permute-start(bf16[1344,128]{1,0:T(8,128)(2,1)S(1)} %split.9), channel_id=1, source_target_pairs={{0,32},{32,0},{1,33},{33,1},{2,34},{34,2},{3,35},{35,3},{4,36},{36... | collective-permute-start | bytes 1032200 | tf_op jit(solution)/shard_map/ppermute | solution.py:255
Sparse Core Ops, SparseCore 0:
  22.4 48.2 all-gather.1
  163.9 45.7 reduce-scatter.1

commit v7 on v6

--- a/solution.py
+++ b/solution.py
@@ -96,25 +96,37 @@
             gu_ref[...] += gu
 
 
-def expert_kernel(nz, nx, rows_hbm, ext, w_hbm, gu_hbm, terms_hbm, part, rows, w, gu_ref, terms, in_sem, terms_sem):
+def expert_kernel(nz, nx, rows_hbm, ext_hbm, w_hbm, gu_hbm, terms_hbm, part_hbm,
+                  rows, ext, w, gu_ref, terms, part, in_sem, terms_sem, part_sem):
     features = w.shape[0]
     chunk = features // nx
     piece = chunk // 2
     wide = nz * HID
-    down = pl.ds(2 * wide, wide)
-    load_d = pltpu.make_async_copy(w_hbm.at[:, down], w.at[:, down], in_sem.at[0])
-    load_gu = pltpu.make_async_copy(gu_hbm, gu_ref, in_sem.at[1])
-    loads = [load_d, load_gu]
-    for x in range(nx):
-        span = pl.ds(x * chunk, chunk)
-        loads.append(pltpu.make_async_copy(rows_hbm.at[:, span], rows.at[:, span], in_sem.at[2 + x]))
-    for x in range(nx):
-        span, cols = pl.ds(x * chunk, chunk), pl.ds(0, 2 * wide)
-        loads.append(pltpu.make_async_copy(w_hbm.at[span, cols], w.at[span, cols], in_sem.at[2 + nx + x]))
-    for copy in loads:
+    down, cols = pl.ds(2 * wide, wide), pl.ds(0, 2 * wide)
+    spans = [pl.ds(x * chunk, chunk) for x in range(nx)]
+    tail = pl.ds(features, PAD)
+    moves = [(w_hbm.at[span, down], w.at[span, down]) for span in spans]
+    moves += [(ext_hbm.at[:, span], ext.at[:, span]) for span in spans]
+    moves += [(rows_hbm.at[:, span], rows.at[:, span]) for span in spans]
+    moves += [(w_hbm.at[span, cols], w.at[span, cols]) for span in spans]
+    moves += [(ext_hbm.at[:, tail], ext.at[:, tail]), (gu_hbm, gu_ref)]
+    loads = [pltpu.make_async_copy(source, target, in_sem.at[n]) for n, (source, target) in enumerate(moves)]
+    load_extra, load_gu = loads[4 * nx :]
+    for x in range(nx):
+        loads[x].start()
+        loads[nx + x].start()
+    load_extra.start()
+    load_gu.start()
+    for copy in loads[2 * nx : 4 * nx]:
         copy.start()
-    load_d.wait()
-    down_grad = dot(ext[:, :features], w[:, 2 * wide :], ((1,), (0,)))
+    down_grad = None
+    for x in range(nx):
+        loads[x].wait()
+        loads[nx + x].wait()
+        span = slice(x * chunk, (x + 1) * chunk)
+        term = dot(ext[:, span], w[span, 2 * wide :], ((1,), (0,)))
+        down_grad = term if x == 0 else down_grad + term
+    load_extra.wait()
     extra = ext[:, features:].astype(F32)
     prob = extra[:, 0:1] + extra[:, 1:2]
     load_gu.wait()
@@ -129,7 +141,7 @@
     gu_grad = jnp.concatenate([gate_grad, up_grad], axis=1)
     stores = []
     for x in range(nx):
-        loads[2 + x].wait()
+        loads[2 * nx + x].wait()
         span = slice(x * chunk, (x + 1) * chunk)
         terms[span, : 2 * wide] = dot(rows[:, span], gu_grad, ((0,), (0,))).astype(BF16)
         scaled = (prob * ext[:, span].astype(F32)).astype(BF16)
@@ -147,9 +159,14 @@
     low = scores - high
     part[:, features:] = jnp.where(lane == 0, high, jnp.where(lane == 1, low, 0.0)).astype(BF16)
     for x in range(nx):
-        loads[2 + nx + x].wait()
+        loads[3 * nx + x].wait()
         span = slice(x * chunk, (x + 1) * chunk)
         part[:, span] = dot(gu_grad, w[span, : 2 * wide], ((1,), (1,))).astype(BF16)
+        if x == nx - 1:
+            span = slice(x * chunk, features + PAD)
+        copy = pltpu.make_async_copy(part.at[:, span], part_hbm.at[:, span], part_sem.at[x])
+        copy.start()
+        stores.append(copy)
     for copy in stores:
         copy.wait()
 
@@ -193,15 +210,18 @@
             pltpu.HBM((held, HID), BF16),
             jax.ShapeDtypeStruct((count, features + PAD), BF16),
         ),
-        in_specs=[ANYWHERE, INSIDE, ANYWHERE, ANYWHERE],
-        out_specs=(ANYWHERE, INSIDE),
+        in_specs=[ANYWHERE] * 4,
+        out_specs=(ANYWHERE, ANYWHERE),
         scratch_shapes=[
             pltpu.VMEM((count, features), BF16),
+            pltpu.VMEM((count, features + PAD), BF16),
             pltpu.VMEM((features, KINDS * wide), BF16),
             pltpu.VMEM((count, 2 * wide), F32),
             pltpu.VMEM((features, KINDS * wide), BF16),
-            pltpu.SemaphoreType.DMA((2 + 2 * nx,)),
+            pltpu.VMEM((count, features + PAD), BF16),
+            pltpu.SemaphoreType.DMA((2 + 4 * nx,)),
             pltpu.SemaphoreType.DMA((copies,)),
+            pltpu.SemaphoreType.DMA((nx,)),
         ],
         compiler_params=pltpu.CompilerParams(vmem_limit_bytes=EXPERT_GRANT),
         cost_estimate=pl.CostEstimate(
@@ -253,7 +273,8 @@
     sums = lax.psum_scatter(terms, HOLD, scatter_dimension=0, tiled=True)
     kept, given = jnp.split(sums, 2, axis=0)
     given = lax.ppermute(given, "zp", SWAP)
-    grads = (kept.astype(F32) + given.astype(F32)).astype(BF16).reshape(KINDS, 1, -1, HID)
+    kept, given = kept.reshape(KINDS, 1, -1, HID), given.reshape(KINDS, 1, -1, HID)
+    grads = [(kept[m].astype(F32) + given[m].astype(F32)).astype(BF16) for m in range(KINDS)]
 
     back = jnp.sum(back.astype(F32).reshape(ny, slots, -1), axis=0)
     back_score = columns(joined(back[:, features : features + 2]))

time: 251 us -> 248 us (0.988)
  no operation moved by 1% of the time
where the time goes in v7:
time: 248 us
  blocking collectives  94.6 us (38%)
  waiting for transfers between devices  63.2 us (25%)
  starting transfers between devices  43.1 us (17%)
  between operations  14.3 us (6%)
  Pallas kernels  12.3 us (5%)
  local copies, waits for them, and re-layouts  11.7 us (5%)
  other arithmetic  6.06 us (2%)
  matrix products  2.54 us (1%)
    all_to_all x3, blocking collectives, swapped(): return lax.all_to_all(x, axis, 0, 0, tiled=True)  94.6 us
    all_to_all x2, waiting for transfers between devices, swapped(): return lax.all_to_all(x, axis, 0, 0, tiled=True)  23.7 us
    ppermute x2, waiting for transfers between devices, layer(): left, right = (lax.ppermute(own, 'y', up), lax.ppermute(own, 'y', down))  23.6 us
    all_to_all x2, starting transfers between devices, swapped(): return lax.all_to_all(x, axis, 0, 0, tiled=True)  19.4 us
    pallas_call x1, Pallas kernels, expert_math(): pl.pallas_call(functools.partial(expert_kernel, nz, nx), name='expert_mat...  9.28 us
    unnamed x18, local copies, waits for them, and re-layouts  8.51 us
    ppermute x1, waiting for transfers between devices, layer(): paired = lax.ppermute(stored, 'zp', SWAP)  8.05 us
    ppermute x2, starting transfers between devices, layer(): far = (lax.ppermute(halves[0], 'y', up), lax.ppermute(halves[1], 'y', down))  7.05 us
  transfers between devices with their start and end apart: 10, of which 6 were waited for; matrix products, arithmetic and copies ran while one was open for 2% of the time, Pallas kernels for 1%

profile of v7, /device:TPU:4, one launch (start us, length us, event | category | flops | bytes accessed | tf_op | source)
XLA Modules:
  0.0 247.8 jit_solution(16817770050923766749)
XLA Ops:
  8.3 4.0 %collective-permute-start.4 = (bf16[1344,128]{1,0:T(8,128)(2,1)S(1)}, bf16[1344,128]{1,0:T(8,128)(2,1)S(1)}, u32[]{:S(2)}, u32[]{:S(2)}) collective-permute-start(bf16[1344,128]{1,0:T(8,128)(2,1)S(1)} %pad_maximum_fusion.1), channel_id=1, source_target_pairs={{0,32},{32,0},{1,33},{33,1},{2,34},{34,2},{3,35},{35,3},{4,36},{36... | collective-permute-start | bytes 1032200 | tf_op jit(solution)/shard_map/ppermute | solution.py:242
  12.3 8.0 %collective-permute-done.4 = bf16[1344,128]{1,0:T(8,128)(2,1)S(1)} collective-permute-done((bf16[1344,128]{1,0:T(8,128)(2,1)S(1)}, bf16[1344,128]{1,0:T(8,128)(2,1)S(1)}, u32[]{:S(2)}, u32[]{:S(2)}) %collective-permute-start.4) | collective-permute-done | bytes 344096 | tf_op jit(solution)/shard_map/ppermute | solution.py:242
  20.3 1.9 pad_maximum_fusion
  23.6 14.9 %all-to-all-start = ((bf16[8,8,3584]{2,1,0:T(8,128)(2,1)}), bf16[8,8,3584]{2,1,0:T(8,128)(2,1)S(1)}, u32[]{:S(2)}, u32[]{:S(2)}) async-start(bf16[8,8,3584]{2,1,0:T(8,128)(2,1)} %fusion), calls=%async_computation | async-start | bytes 917504 | tf_op jit(solution)/shard_map/all_to_all | solution.py:45
  39.4 23.7 %all-to-all-done = bf16[8,8,3584]{2,1,0:T(8,128)(2,1)S(1)} async-done(((bf16[8,8,3584]{2,1,0:T(8,128)(2,1)}), bf16[8,8,3584]{2,1,0:T(8,128)(2,1)S(1)}, u32[]{:S(2)}, u32[]{:S(2)}) %all-to-all-start) | async-done | bytes 458784 | tf_op jit(solution)/shard_map/all_to_all | solution.py:45
  63.1 32.3 %all_to_all.47 = bf16[8,8,3712]{2,1,0:T(8,128)(2,1)S(1)} all-to-all(bf16[8,8,3712]{2,1,0:T(8,128)(2,1)S(1)} %bitcast.62), channel_id=1, replica_groups=mesh['e'=8,'zp'=2,'y'=4,'x'=4,'c'=2] {'e'}, dimensions={0} | all-to-all | bytes 950272 | tf_op jit(solution)/shard_map/all_to_all | solution.py:45
  96.9 4.5 %all-to-all-start.2 = ((bf16[4,64,3712]{2,1,0:T(8,128)(2,1)}), bf16[4,64,3712]{2,1,0:T(8,128)(2,1)}, u32[]{:S(2)}, u32[]{:S(2)}) async-start(bf16[4,64,3712]{2,1,0:T(8,128)(2,1)} %broadcast_in_dim.77), calls=%async_computation.2 | async-start | bytes 3801088 | tf_op jit(solution)/shard_map/all_to_all | solution.py:45
  101.4 3.9 %collective-permute-start = (bf16[64,3584]{1,0:T(8,128)(2,1)S(1)}, bf16[64,3584]{1,0:T(8,128)(2,1)S(1)}, u32[]{:S(2)}, u32[]{:S(2)}) collective-permute-start(bf16[64,3584]{1,0:T(8,128)(2,1)S(1)} %bitcast.55), channel_id=1, source_target_pairs={{0,8},{8,16},{16,24},{24,0},{1,9},{9,17},{17,25},{25,1},{2,10},{10... | collective-permute-start | bytes 1376264 | tf_op jit(solution)/shard_map/ppermute | solution.py:263
  105.3 3.1 %collective-permute-start.1 = (bf16[64,3584]{1,0:T(8,128)(2,1)S(1)}, bf16[64,3584]{1,0:T(8,128)(2,1)S(1)}, u32[]{:S(2)}, u32[]{:S(2)}) collective-permute-start(bf16[64,3584]{1,0:T(8,128)(2,1)S(1)} %bitcast.56), channel_id=1, source_target_pairs={{0,24},{8,0},{16,8},{24,16},{1,25},{9,1},{17,9},{25,17},{2,26},{10... | collective-permute-start | bytes 1376264 | tf_op jit(solution)/shard_map/ppermute | solution.py:263
  108.4 23.6 %collective-permute-done.s1 = bf16[64,3584]{1,0:T(8,128)(2,1)S(1)} collective-permute-done((bf16[64,3584]{1,0:T(8,128)(2,1)S(1)}, bf16[64,3584]{1,0:T(8,128)(2,1)S(1)}, u32[]{:S(2)}, u32[]{:S(2)}) %collective-permute-start) | collective-permute-done | bytes 458784 | tf_op jit(solution)/shard_map/ppermute | solution.py:263
  132.0 1.9 collective-permute-start.2
  134.0 5.1 %collective-permute-start.3 = (bf16[32,3584]{1,0:T(8,128)(2,1)S(1)}, bf16[32,3584]{1,0:T(8,128)(2,1)S(1)}, u32[]{:S(2)}, u32[]{:S(2)}) collective-permute-start(bf16[32,3584]{1,0:T(8,128)(2,1)S(1)} %slice.89), channel_id=1, source_target_pairs={{0,24},{8,0},{16,8},{24,16},{1,25},{9,1},{17,9},{25,17},{2,26},{10... | collective-permute-start | bytes 688136 | tf_op jit(solution)/shard_map/ppermute | solution.py:265
  139.1 2.0 collective-permute-done.2.s3
  141.2 1.5 collective-permute-done.3.s4
  142.7 2.6 %copy-done.1 = bf16[21504,128]{1,0:T(8,128)(2,1)S(1)} copy-done((bf16[21504,128]{1,0:T(8,128)(2,1)S(1)}, bf16[21504,128]{1,0:T(8,128)(2,1)}, u32[]{:S(2)}) %copy-start.1) | copy-done | bytes 5505048
  145.2 3.0 %pre_math.1 = (bf16[256,3584]{1,0:T(8,128)(2,1)S(1)}, bf16[3584,768]{1,0:T(8,128)(2,1)S(1)}, f32[256,512]{1,0:T(8,128)S(1)}) custom-call(s32[1]{0:T(128)} %bitcast.4.y_ref, bf16[64,3584]{1,0:T(8,128)(2,1)S(1)} %bitcast.57, bf16[64,3584]{1,0:T(8,128)(2,1)S(1)} %collective-permute-done.s1, bf16[64,3584]{1,0:T(8,128)(2,1)S(1)} %collective-permute-done.1.s2, ...), custom_call_target="tpu_custom_call" | custom-call | flops 939524096 | bytes 7340032 | tf_op jit(solution)/shard_map/pre_math/pallas_call | solution.py:182
  148.2 2.4 copy-done.2
  152.7 9.3 %expert_math.1 = (bf16[21504,128]{1,0:T(8,128)(2,1)}, bf16[256,3712]{1,0:T(8,128)(2,1)}) custom-call(bf16[256,3584]{1,0:T(8,128)(2,1)} %copy-done.3, bf16[256,3712]{1,0:T(8,128)(2,1)} %bitcast.14.ext_hbm, bf16[3584,768]{1,0:T(8,128)(2,1)} %copy-done.2, f32[256,512]{1,0:T(8,128)} %copy-done.4), custom_call_target="tpu_custom_call" | custom-call | flops 2818572288 | bytes 9175040 | tf_op jit(solution)/shard_map/expert_math/pallas_call | solution.py:206
  162.0 1.5 copy-done.5
  163.5 23.3 %all_to_all.48 = bf16[4,64,3712]{2,1,0:T(8,128)(2,1)S(1)} all-to-all(bf16[4,64,3712]{2,1,0:T(8,128)(2,1)S(1)} %bitcast.61), channel_id=1, replica_groups=mesh['e'=8,'zp'=2,'y'=4,'x'=4,'c'=2] {'y'}, dimensions={0} | all-to-all | bytes 3801088 | tf_op jit(solution)/shard_map/all_to_all | solution.py:45
  187.3 39.0 %all_to_all.49 = bf16[8,8,3712]{2,1,0:T(8,128)(2,1)S(1)} all-to-all(bf16[8,8,3712]{2,1,0:T(8,128)(2,1)S(1)} %concatenate.29), channel_id=1, replica_groups=mesh['e'=8,'zp'=2,'y'=4,'x'=4,'c'=2] {'e'}, dimensions={0} | all-to-all | bytes 950272 | tf_op jit(solution)/shard_map/all_to_all | solution.py:45
  227.7 5.6 %collective-permute-start.5 = (bf16[1344,128]{1,0:T(8,128)(2,1)S(1)}, bf16[1344,128]{1,0:T(8,128)(2,1)S(1)}, u32[]{:S(2)}, u32[]{:S(2)}) collective-permute-start(bf16[1344,128]{1,0:T(8,128)(2,1)S(1)} %split.5), channel_id=1, source_target_pairs={{0,32},{32,0},{1,33},{33,1},{2,34},{34,2},{3,35},{35,3},{4,36},{36... | collective-permute-start | bytes 1032200 | tf_op jit(solution)/shard_map/ppermute | solution.py:275
  234.9 4.3 %collective-permute-done.5 = bf16[1344,128]{1,0:T(8,128)(2,1)S(1)} collective-permute-done((bf16[1344,128]{1,0:T(8,128)(2,1)S(1)}, bf16[1344,128]{1,0:T(8,128)(2,1)S(1)}, u32[]{:S(2)}, u32[]{:S(2)}) %collective-permute-start.5) | collective-permute-done | bytes 344096 | tf_op jit(solution)/shard_map/ppermute | solution.py:275
  239.1 1.8 fusion.5
  (55 shorter events, 10.2 us)
Async XLA Ops:
  7.2 15.3 %copy-start = (bf16[24,3584]{1,0:T(8,128)(2,1)S(1)}, bf16[24,3584]{1,0:T(8,128)(2,1)}, u32[]{:S(2)}) copy-start(bf16[24,3584]{1,0:T(8,128)(2,1)} %param.7) | copy-start | bytes 516100
  7.2 15.2 %copy-start.7 = (s32[24,2]{0,1:T(2,128)S(1)}, s32[24,2]{0,1:T(2,128)}, u32[]{:S(2)}) copy-start(s32[24,2]{0,1:T(2,128)} %param.9) | copy-start | bytes 580
  7.2 135.5 %all-gather.2.cloned.1.call-start = ((), (), s32[]{:S(2)}) async-start(), calls=%async_computation.6 | async-start | bytes 6193152 | tf_op jit(solution)/shard_map/all_gather | solution.py:243
  8.3 30.2 %copy-start.8 = (f32[24,2]{0,1:T(2,128)S(1)}, f32[24,2]{0,1:T(2,128)}, u32[]{:S(2)}) copy-start(f32[24,2]{0,1:T(2,128)} %param.10) | copy-start | bytes 580
  8.3 30.7 %copy-start.6 = (bf16[24,3584]{1,0:T(8,128)(2,1)S(1)}, bf16[24,3584]{1,0:T(8,128)(2,1)}, u32[]{:S(2)}) copy-start(bf16[24,3584]{1,0:T(8,128)(2,1)} %param.8) | copy-start | bytes 516100
  8.3 12.0 %collective-permute-start.4 = (bf16[1344,128]{1,0:T(8,128)(2,1)S(1)}, bf16[1344,128]{1,0:T(8,128)(2,1)S(1)}, u32[]{:S(2)}, u32[]{:S(2)}) collective-permute-start(bf16[1344,128]{1,0:T(8,128)(2,1)S(1)} %pad_maximum_fusion.1), channel_id=1, source_target_pairs={{0,32},{32,0},{1,33},{33,1},{2,34},{34,2},{3,35},{35,3},{4,36},{36... | collective-permute-start | bytes 1032200 | tf_op jit(solution)/shard_map/ppermute | solution.py:242
  23.6 39.5 %all-to-all-start = ((bf16[8,8,3584]{2,1,0:T(8,128)(2,1)}), bf16[8,8,3584]{2,1,0:T(8,128)(2,1)S(1)}, u32[]{:S(2)}, u32[]{:S(2)}) async-start(bf16[8,8,3584]{2,1,0:T(8,128)(2,1)} %fusion), calls=%async_computation | async-start | bytes 917504 | tf_op jit(solution)/shard_map/all_to_all | solution.py:45
  96.9 55.8 %all-to-all-start.2 = ((bf16[4,64,3712]{2,1,0:T(8,128)(2,1)}), bf16[4,64,3712]{2,1,0:T(8,128)(2,1)}, u32[]{:S(2)}, u32[]{:S(2)}) async-start(bf16[4,64,3712]{2,1,0:T(8,128)(2,1)} %broadcast_in_dim.77), calls=%async_computation.2 | async-start | bytes 3801088 | tf_op jit(solution)/shard_map/all_to_all | solution.py:45
  101.4 125.3 %reduce-scatter.2.cloned.1.call-start = ((), (), s32[]{:S(2)}) async-start(), calls=%async_computation.7 | async-start | bytes 6193152 | tf_op jit(solution)/shard_map/reduce_scatter | solution.py:273
  101.4 30.7 %collective-permute-start = (bf16[64,3584]{1,0:T(8,128)(2,1)S(1)}, bf16[64,3584]{1,0:T(8,128)(2,1)S(1)}, u32[]{:S(2)}, u32[]{:S(2)}) collective-permute-start(bf16[64,3584]{1,0:T(8,128)(2,1)S(1)} %bitcast.55), channel_id=1, source_target_pairs={{0,8},{8,16},{16,24},{24,0},{1,9},{9,17},{17,25},{25,1},{2,10},{10... | collective-permute-start | bytes 1376264 | tf_op jit(solution)/shard_map/ppermute | solution.py:263
  105.3 28.7 %collective-permute-start.1 = (bf16[64,3584]{1,0:T(8,128)(2,1)S(1)}, bf16[64,3584]{1,0:T(8,128)(2,1)S(1)}, u32[]{:S(2)}, u32[]{:S(2)}) collective-permute-start(bf16[64,3584]{1,0:T(8,128)(2,1)S(1)} %bitcast.56), channel_id=1, source_target_pairs={{0,24},{8,0},{16,8},{24,16},{1,25},{9,1},{17,9},{25,17},{2,26},{10... | collective-permute-start | bytes 1376264 | tf_op jit(solution)/shard_map/ppermute | solution.py:263
  132.0 9.1 %collective-permute-start.2 = (bf16[32,3584]{1,0:T(8,128)(2,1)S(1)}, bf16[32,3584]{1,0:T(8,128)(2,1)S(1)}, u32[]{:S(2)}, u32[]{:S(2)}) collective-permute-start(bf16[32,3584]{1,0:T(8,128)(2,1)S(1)} %slice.88), channel_id=1, source_target_pairs={{0,8},{8,16},{16,24},{24,0},{1,9},{9,17},{17,25},{25,1},{2,10},{10... | collective-permute-start | bytes 688136 | tf_op jit(solution)/shard_map/ppermute | solution.py:265
  134.0 8.7 %collective-permute-start.3 = (bf16[32,3584]{1,0:T(8,128)(2,1)S(1)}, bf16[32,3584]{1,0:T(8,128)(2,1)S(1)}, u32[]{:S(2)}, u32[]{:S(2)}) collective-permute-start(bf16[32,3584]{1,0:T(8,128)(2,1)S(1)} %slice.89), channel_id=1, source_target_pairs={{0,24},{8,0},{16,8},{24,16},{1,25},{9,1},{17,9},{25,17},{2,26},{10... | collective-permute-start | bytes 688136 | tf_op jit(solution)/shard_map/ppermute | solution.py:265
  142.7 2.6 %copy-start.1 = (bf16[21504,128]{1,0:T(8,128)(2,1)S(1)}, bf16[21504,128]{1,0:T(8,128)(2,1)}, u32[]{:S(2)}) copy-start(bf16[21504,128]{1,0:T(8,128)(2,1)} %all-gather.2.cloned.1.call-done.w_hbm) | copy-start | bytes 16515076
  148.2 2.4 copy-start.2
  150.6 1.2 copy-start.3
  151.9 0.8 copy-start.4
  162.0 1.5 copy-start.5
  227.7 11.4 %collective-permute-start.5 = (bf16[1344,128]{1,0:T(8,128)(2,1)S(1)}, bf16[1344,128]{1,0:T(8,128)(2,1)S(1)}, u32[]{:S(2)}, u32[]{:S(2)}) collective-permute-start(bf16[1344,128]{1,0:T(8,128)(2,1)S(1)} %split.5), channel_id=1, source_target_pairs={{0,32},{32,0},{1,33},{33,1},{2,34},{34,2},{3,35},{35,3},{4,36},{36... | collective-permute-start | bytes 1032200 | tf_op jit(solution)/shard_map/ppermute | solution.py:275
Sparse Core Ops, SparseCore 0:
  22.4 48.2 all-gather.1
  162.1 45.7 reduce-scatter.1

commit v8 on v7

--- a/solution.py
+++ b/solution.py
@@ -277,8 +277,10 @@
     grads = [(kept[m].astype(F32) + given[m].astype(F32)).astype(BF16) for m in range(KINDS)]
 
     back = jnp.sum(back.astype(F32).reshape(ny, slots, -1), axis=0)
-    back_score = columns(joined(back[:, features : features + 2]))
-    back = jnp.concatenate([back[:, :features].astype(BF16), back_score], axis=1)
+    score = back[:, features : features + 1] + back[:, features + 1 : features + 2]
+    high = lax.reduce_precision(score, 8, 7)
+    lane = lax.broadcasted_iota(jnp.int32, back.shape, 1)
+    back = jnp.where(lane == features, high, jnp.where(lane == features + 1, score - high, back)).astype(BF16)
     back = swapped(back, "e")
     grad_tokens = dot(select, back[:, :features], ((0,), (0,))).astype(BF16)
     score = joined(back[:, features : features + 2]).reshape(experts, CAP, 1)

time: 248 us -> 248 us (level)
  the two profiles are of different devices: /device:TPU:4 before, /device:TPU:2 now
where the time goes in v8:
time: 248 us; the launch traced here: 247 us
  waiting for transfers between devices  81.9 us (33%)
  blocking collectives  71.2 us (29%)
  starting transfers between devices  48 us (19%)
  between operations  14.3 us (6%)
  Pallas kernels  12.3 us (5%)
  local copies, waits for them, and re-layouts  10.3 us (4%)
  other arithmetic  6.34 us (3%)
  matrix products  2.53 us (1%)
    all_to_all x2, blocking collectives, swapped(): return lax.all_to_all(x, axis, 0, 0, tiled=True)  71.2 us
    all_to_all x3, waiting for transfers between devices, swapped(): return lax.all_to_all(x, axis, 0, 0, tiled=True)  42.3 us
    all_to_all x3, starting transfers between devices, swapped(): return lax.all_to_all(x, axis, 0, 0, tiled=True)  24.4 us
    ppermute x2, waiting for transfers between devices, layer(): left, right = (lax.ppermute(own, 'y', up), lax.ppermute(own, 'y', down))  23.6 us
    pallas_call x1, Pallas kernels, expert_math(): pl.pallas_call(functools.partial(expert_kernel, nz, nx), name='expert_mat...  9.26 us
    ppermute x1, waiting for transfers between devices, layer(): paired = lax.ppermute(stored, 'zp', SWAP)  8.05 us
    ppermute x2, starting transfers between devices, layer(): far = (lax.ppermute(halves[0], 'y', up), lax.ppermute(halves[1], 'y', down))  7.05 us
    ppermute x2, starting transfers between devices, layer(): left, right = (lax.ppermute(own, 'y', up), lax.ppermute(own, 'y', down))  7.05 us
  transfers between devices with their start and end apart: 11, of which 7 were waited for; matrix products, arithmetic and copies ran while one was open for 3% of the time, Pallas kernels for 1%

profile of v8, /device:TPU:2, one launch (start us, length us, event | category | flops | bytes accessed | tf_op | source)
XLA Modules:
  0.0 246.8 jit_solution(5104802553927024887)
XLA Ops:
  8.3 4.0 %collective-permute-start.4 = (bf16[1344,128]{1,0:T(8,128)(2,1)S(1)}, bf16[1344,128]{1,0:T(8,128)(2,1)S(1)}, u32[]{:S(2)}, u32[]{:S(2)}) collective-permute-start(bf16[1344,128]{1,0:T(8,128)(2,1)S(1)} %pad_maximum_fusion.1), channel_id=1, source_target_pairs={{0,32},{32,0},{1,33},{33,1},{2,34},{34,2},{3,35},{35,3},{4,36},{36... | collective-permute-start | bytes 1032200 | tf_op jit(solution)/shard_map/ppermute | solution.py:242
  12.3 8.0 %collective-permute-done.4 = bf16[1344,128]{1,0:T(8,128)(2,1)S(1)} collective-permute-done((bf16[1344,128]{1,0:T(8,128)(2,1)S(1)}, bf16[1344,128]{1,0:T(8,128)(2,1)S(1)}, u32[]{:S(2)}, u32[]{:S(2)}) %collective-permute-start.4) | collective-permute-done | bytes 344096 | tf_op jit(solution)/shard_map/ppermute | solution.py:242
  20.3 1.9 pad_maximum_fusion
  23.6 14.9 %all-to-all-start = ((bf16[8,8,3584]{2,1,0:T(8,128)(2,1)}), bf16[8,8,3584]{2,1,0:T(8,128)(2,1)S(1)}, u32[]{:S(2)}, u32[]{:S(2)}) async-start(bf16[8,8,3584]{2,1,0:T(8,128)(2,1)} %fusion), calls=%async_computation | async-start | bytes 917504 | tf_op jit(solution)/shard_map/all_to_all | solution.py:45
  39.4 23.8 %all-to-all-done = bf16[8,8,3584]{2,1,0:T(8,128)(2,1)S(1)} async-done(((bf16[8,8,3584]{2,1,0:T(8,128)(2,1)}), bf16[8,8,3584]{2,1,0:T(8,128)(2,1)S(1)}, u32[]{:S(2)}, u32[]{:S(2)}) %all-to-all-start) | async-done | bytes 458784 | tf_op jit(solution)/shard_map/all_to_all | solution.py:45
  63.2 32.3 %all_to_all.47 = bf16[8,8,3712]{2,1,0:T(8,128)(2,1)S(1)} all-to-all(bf16[8,8,3712]{2,1,0:T(8,128)(2,1)S(1)} %bitcast.62), channel_id=1, replica_groups=mesh['e'=8,'zp'=2,'y'=4,'x'=4,'c'=2] {'e'}, dimensions={0} | all-to-all | bytes 950272 | tf_op jit(solution)/shard_map/all_to_all | solution.py:45
  96.9 4.5 %all-to-all-start.2 = ((bf16[4,64,3712]{2,1,0:T(8,128)(2,1)}), bf16[4,64,3712]{2,1,0:T(8,128)(2,1)}, u32[]{:S(2)}, u32[]{:S(2)}) async-start(bf16[4,64,3712]{2,1,0:T(8,128)(2,1)} %broadcast_in_dim.96), calls=%async_computation.2 | async-start | bytes 3801088 | tf_op jit(solution)/shard_map/all_to_all | solution.py:45
  101.4 3.9 %collective-permute-start = (bf16[64,3584]{1,0:T(8,128)(2,1)S(1)}, bf16[64,3584]{1,0:T(8,128)(2,1)S(1)}, u32[]{:S(2)}, u32[]{:S(2)}) collective-permute-start(bf16[64,3584]{1,0:T(8,128)(2,1)S(1)} %bitcast.55), channel_id=1, source_target_pairs={{0,8},{8,16},{16,24},{24,0},{1,9},{9,17},{17,25},{25,1},{2,10},{10... | collective-permute-start | bytes 1376264 | tf_op jit(solution)/shard_map/ppermute | solution.py:263
  105.3 3.1 %collective-permute-start.1 = (bf16[64,3584]{1,0:T(8,128)(2,1)S(1)}, bf16[64,3584]{1,0:T(8,128)(2,1)S(1)}, u32[]{:S(2)}, u32[]{:S(2)}) collective-permute-start(bf16[64,3584]{1,0:T(8,128)(2,1)S(1)} %bitcast.56), channel_id=1, source_target_pairs={{0,24},{8,0},{16,8},{24,16},{1,25},{9,1},{17,9},{25,17},{2,26},{10... | collective-permute-start | bytes 1376264 | tf_op jit(solution)/shard_map/ppermute | solution.py:263
  108.4 23.6 %collective-permute-done.s1 = bf16[64,3584]{1,0:T(8,128)(2,1)S(1)} collective-permute-done((bf16[64,3584]{1,0:T(8,128)(2,1)S(1)}, bf16[64,3584]{1,0:T(8,128)(2,1)S(1)}, u32[]{:S(2)}, u32[]{:S(2)}) %collective-permute-start) | collective-permute-done | bytes 458784 | tf_op jit(solution)/shard_map/ppermute | solution.py:263
  132.0 1.9 collective-permute-start.2
  134.0 5.1 %collective-permute-start.3 = (bf16[32,3584]{1,0:T(8,128)(2,1)S(1)}, bf16[32,3584]{1,0:T(8,128)(2,1)S(1)}, u32[]{:S(2)}, u32[]{:S(2)}) collective-permute-start(bf16[32,3584]{1,0:T(8,128)(2,1)S(1)} %slice.81), channel_id=1, source_target_pairs={{0,24},{8,0},{16,8},{24,16},{1,25},{9,1},{17,9},{25,17},{2,26},{10... | collective-permute-start | bytes 688136 | tf_op jit(solution)/shard_map/ppermute | solution.py:265
  139.1 2.0 collective-permute-done.2.s3
  141.2 1.5 collective-permute-done.3.s4
  142.7 2.6 %copy-done.1 = bf16[21504,128]{1,0:T(8,128)(2,1)S(1)} copy-done((bf16[21504,128]{1,0:T(8,128)(2,1)S(1)}, bf16[21504,128]{1,0:T(8,128)(2,1)}, u32[]{:S(2)}) %copy-start.1) | copy-done | bytes 5505048
  145.2 3.0 %pre_math.1 = (bf16[256,3584]{1,0:T(8,128)(2,1)S(1)}, bf16[3584,768]{1,0:T(8,128)(2,1)S(1)}, f32[256,512]{1,0:T(8,128)S(1)}) custom-call(s32[1]{0:T(128)} %bitcast.4.y_ref, bf16[64,3584]{1,0:T(8,128)(2,1)S(1)} %bitcast.57, bf16[64,3584]{1,0:T(8,128)(2,1)S(1)} %collective-permute-done.s1, bf16[64,3584]{1,0:T(8,128)(2,1)S(1)} %collective-permute-done.1.s2, ...), custom_call_target="tpu_custom_call" | custom-call | flops 939524096 | bytes 7340032 | tf_op jit(solution)/shard_map/pre_math/pallas_call | solution.py:182
  148.2 2.4 copy-done.2
  152.7 9.3 %expert_math.1 = (bf16[21504,128]{1,0:T(8,128)(2,1)}, bf16[256,3712]{1,0:T(8,128)(2,1)}) custom-call(bf16[256,3584]{1,0:T(8,128)(2,1)} %copy-done.3, bf16[256,3712]{1,0:T(8,128)(2,1)} %bitcast.14.ext_hbm, bf16[3584,768]{1,0:T(8,128)(2,1)} %copy-done.2, f32[256,512]{1,0:T(8,128)} %copy-done.4), custom_call_target="tpu_custom_call" | custom-call | flops 2818572288 | bytes 9175040 | tf_op jit(solution)/shard_map/expert_math/pallas_call | solution.py:206
  162.0 5.0 %all-to-all-start.3 = ((bf16[4,64,3712]{2,1,0:T(8,128)(2,1)}), bf16[4,64,3712]{2,1,0:T(8,128)(2,1)S(1)}, u32[]{:S(2)}, u32[]{:S(2)}) async-start(bf16[4,64,3712]{2,1,0:T(8,128)(2,1)} %bitcast.61), calls=%async_computation.3 | async-start | bytes 3801088 | tf_op jit(solution)/shard_map/all_to_all | solution.py:45
  167.0 18.5 %all-to-all-done.3 = bf16[4,64,3712]{2,1,0:T(8,128)(2,1)S(1)} async-done(((bf16[4,64,3712]{2,1,0:T(8,128)(2,1)}), bf16[4,64,3712]{2,1,0:T(8,128)(2,1)S(1)}, u32[]{:S(2)}, u32[]{:S(2)}) %all-to-all-start.3) | async-done | bytes 1900576 | tf_op jit(solution)/shard_map/all_to_all | solution.py:45
  186.3 38.9 %all_to_all.48 = bf16[8,8,3712]{2,1,0:T(8,128)(2,1)S(1)} all-to-all(bf16[8,8,3712]{2,1,0:T(8,128)(2,1)S(1)} %fusion.2), channel_id=1, replica_groups=mesh['e'=8,'zp'=2,'y'=4,'x'=4,'c'=2] {'e'}, dimensions={0} | all-to-all | bytes 950272 | tf_op jit(solution)/shard_map/all_to_all | solution.py:45
  226.7 5.6 %collective-permute-start.5 = (bf16[1344,128]{1,0:T(8,128)(2,1)S(1)}, bf16[1344,128]{1,0:T(8,128)(2,1)S(1)}, u32[]{:S(2)}, u32[]{:S(2)}) collective-permute-start(bf16[1344,128]{1,0:T(8,128)(2,1)S(1)} %split.5), channel_id=1, source_target_pairs={{0,32},{32,0},{1,33},{33,1},{2,34},{34,2},{3,35},{35,3},{4,36},{36... | collective-permute-start | bytes 1032200 | tf_op jit(solution)/shard_map/ppermute | solution.py:275
  233.8 4.4 %collective-permute-done.5 = bf16[1344,128]{1,0:T(8,128)(2,1)S(1)} collective-permute-done((bf16[1344,128]{1,0:T(8,128)(2,1)S(1)}, bf16[1344,128]{1,0:T(8,128)(2,1)S(1)}, u32[]{:S(2)}, u32[]{:S(2)}) %collective-permute-start.5) | collective-permute-done | bytes 344096 | tf_op jit(solution)/shard_map/ppermute | solution.py:275
  238.2 1.8 fusion.6
  (55 shorter events, 10.5 us)
Async XLA Ops:
  7.2 15.3 %copy-start = (bf16[24,3584]{1,0:T(8,128)(2,1)S(1)}, bf16[24,3584]{1,0:T(8,128)(2,1)}, u32[]{:S(2)}) copy-start(bf16[24,3584]{1,0:T(8,128)(2,1)} %param.7) | copy-start | bytes 516100
  7.2 15.2 %copy-start.6 = (s32[24,2]{0,1:T(2,128)S(1)}, s32[24,2]{0,1:T(2,128)}, u32[]{:S(2)}) copy-start(s32[24,2]{0,1:T(2,128)} %param.9) | copy-start | bytes 580
  7.2 135.5 %all-gather.2.cloned.1.call-start = ((), (), s32[]{:S(2)}) async-start(), calls=%async_computation.6 | async-start | bytes 6193152 | tf_op jit(solution)/shard_map/all_gather | solution.py:243
  8.3 30.2 %copy-start.7 = (f32[24,2]{0,1:T(2,128)S(1)}, f32[24,2]{0,1:T(2,128)}, u32[]{:S(2)}) copy-start(f32[24,2]{0,1:T(2,128)} %param.10) | copy-start | bytes 580
  8.3 30.7 %copy-start.5 = (bf16[24,3584]{1,0:T(8,128)(2,1)S(1)}, bf16[24,3584]{1,0:T(8,128)(2,1)}, u32[]{:S(2)}) copy-start(bf16[24,3584]{1,0:T(8,128)(2,1)} %param.8) | copy-start | bytes 516100
  8.3 12.0 %collective-permute-start.4 = (bf16[1344,128]{1,0:T(8,128)(2,1)S(1)}, bf16[1344,128]{1,0:T(8,128)(2,1)S(1)}, u32[]{:S(2)}, u32[]{:S(2)}) collective-permute-start(bf16[1344,128]{1,0:T(8,128)(2,1)S(1)} %pad_maximum_fusion.1), channel_id=1, source_target_pairs={{0,32},{32,0},{1,33},{33,1},{2,34},{34,2},{3,35},{35,3},{4,36},{36... | collective-permute-start | bytes 1032200 | tf_op jit(solution)/shard_map/ppermute | solution.py:242
  23.6 39.6 %all-to-all-start = ((bf16[8,8,3584]{2,1,0:T(8,128)(2,1)}), bf16[8,8,3584]{2,1,0:T(8,128)(2,1)S(1)}, u32[]{:S(2)}, u32[]{:S(2)}) async-start(bf16[8,8,3584]{2,1,0:T(8,128)(2,1)} %fusion), calls=%async_computation | async-start | bytes 917504 | tf_op jit(solution)/shard_map/all_to_all | solution.py:45
  96.9 55.8 %all-to-all-start.2 = ((bf16[4,64,3712]{2,1,0:T(8,128)(2,1)}), bf16[4,64,3712]{2,1,0:T(8,128)(2,1)}, u32[]{:S(2)}, u32[]{:S(2)}) async-start(bf16[4,64,3712]{2,1,0:T(8,128)(2,1)} %broadcast_in_dim.96), calls=%async_computation.2 | async-start | bytes 3801088 | tf_op jit(solution)/shard_map/all_to_all | solution.py:45
  101.4 124.3 %reduce-scatter.2.cloned.1.call-start = ((), (), s32[]{:S(2)}) async-start(), calls=%async_computation.7 | async-start | bytes 6193152 | tf_op jit(solution)/shard_map/reduce_scatter | solution.py:273
  101.4 30.6 %collective-permute-start = (bf16[64,3584]{1,0:T(8,128)(2,1)S(1)}, bf16[64,3584]{1,0:T(8,128)(2,1)S(1)}, u32[]{:S(2)}, u32[]{:S(2)}) collective-permute-start(bf16[64,3584]{1,0:T(8,128)(2,1)S(1)} %bitcast.55), channel_id=1, source_target_pairs={{0,8},{8,16},{16,24},{24,0},{1,9},{9,17},{17,25},{25,1},{2,10},{10... | collective-permute-start | bytes 1376264 | tf_op jit(solution)/shard_map/ppermute | solution.py:263
  105.3 28.7 %collective-permute-start.1 = (bf16[64,3584]{1,0:T(8,128)(2,1)S(1)}, bf16[64,3584]{1,0:T(8,128)(2,1)S(1)}, u32[]{:S(2)}, u32[]{:S(2)}) collective-permute-start(bf16[64,3584]{1,0:T(8,128)(2,1)S(1)} %bitcast.56), channel_id=1, source_target_pairs={{0,24},{8,0},{16,8},{24,16},{1,25},{9,1},{17,9},{25,17},{2,26},{10... | collective-permute-start | bytes 1376264 | tf_op jit(solution)/shard_map/ppermute | solution.py:263
  132.0 9.1 %collective-permute-start.2 = (bf16[32,3584]{1,0:T(8,128)(2,1)S(1)}, bf16[32,3584]{1,0:T(8,128)(2,1)S(1)}, u32[]{:S(2)}, u32[]{:S(2)}) collective-permute-start(bf16[32,3584]{1,0:T(8,128)(2,1)S(1)} %slice.80), channel_id=1, source_target_pairs={{0,8},{8,16},{16,24},{24,0},{1,9},{9,17},{17,25},{25,1},{2,10},{10... | collective-permute-start | bytes 688136 | tf_op jit(solution)/shard_map/ppermute | solution.py:265
  134.0 8.7 %collective-permute-start.3 = (bf16[32,3584]{1,0:T(8,128)(2,1)S(1)}, bf16[32,3584]{1,0:T(8,128)(2,1)S(1)}, u32[]{:S(2)}, u32[]{:S(2)}) collective-permute-start(bf16[32,3584]{1,0:T(8,128)(2,1)S(1)} %slice.81), channel_id=1, source_target_pairs={{0,24},{8,0},{16,8},{24,16},{1,25},{9,1},{17,9},{25,17},{2,26},{10... | collective-permute-start | bytes 688136 | tf_op jit(solution)/shard_map/ppermute | solution.py:265
  142.7 2.6 %copy-start.1 = (bf16[21504,128]{1,0:T(8,128)(2,1)S(1)}, bf16[21504,128]{1,0:T(8,128)(2,1)}, u32[]{:S(2)}) copy-start(bf16[21504,128]{1,0:T(8,128)(2,1)} %all-gather.2.cloned.1.call-done.w_hbm) | copy-start | bytes 16515076
  148.2 2.4 copy-start.2
  150.6 1.2 copy-start.3
  151.9 0.8 copy-start.4
  162.0 23.5 %all-to-all-start.3 = ((bf16[4,64,3712]{2,1,0:T(8,128)(2,1)}), bf16[4,64,3712]{2,1,0:T(8,128)(2,1)S(1)}, u32[]{:S(2)}, u32[]{:S(2)}) async-start(bf16[4,64,3712]{2,1,0:T(8,128)(2,1)} %bitcast.61), calls=%async_computation.3 | async-start | bytes 3801088 | tf_op jit(solution)/shard_map/all_to_all | solution.py:45
  226.7 11.5 %collective-permute-start.5 = (bf16[1344,128]{1,0:T(8,128)(2,1)S(1)}, bf16[1344,128]{1,0:T(8,128)(2,1)S(1)}, u32[]{:S(2)}, u32[]{:S(2)}) collective-permute-start(bf16[1344,128]{1,0:T(8,128)(2,1)S(1)} %split.5), channel_id=1, source_target_pairs={{0,32},{32,0},{1,33},{33,1},{2,34},{34,2},{3,35},{35,3},{4,36},{36... | collective-permute-start | bytes 1032200 | tf_op jit(solution)/shard_map/ppermute | solution.py:275
Sparse Core Ops, SparseCore 0:
  22.4 48.5 all-gather.1
  162.1 45.6 reduce-scatter.1
